TPU v7x, 1024 devices: a whole 4x8x16 slice. The times are simulated.
1024 devices in a mesh: sub: 128 (over z_hi, y, x), slab: 8 (over z_lo, core).
Axes of the slice: x: 4, y: 8, z: 16 (z_hi: 4, z_lo: 4; z = z_hi * 4 + z_lo), core: 2. Of those that a mesh axis runs over, the one named last changes fastest.
Arguments:
- coarse_basis: bfloat16 [512, 64, 4000], P('sub', 'slab'), may hold values from -6 to 6
- jacobians: bfloat16 [4, 750, 750], replicated, may hold values from -0.21875 to 0.21875
- element_faces: int32 [20480, 6], P(('sub', 'slab')), may hold values from 1 to 58, as said below
- element_type: int32 [20480], P(('sub', 'slab')), may hold values from 0 to 3
- element_count: int32 [1024], P(('sub', 'slab')), may hold values from 1 to 20, 15360 in all
- vertex_ids: int32 [1024, 32], P(('sub', 'slab')), may hold values from 0 to 511, as said below
Outputs:
- second_image: bfloat16 [512, 64, 4000], P('sub', 'slab')
- coarse_matrix: float32 [512, 512], P('sub')
Inputs may be any that keep to these rules, and one draw needn't show every extreme that they name: `element_faces`: each row names six different cells of the subdomain's extended face grid of (6) x (10) cells, numbered row-major, the own face blocks at rows 1 to 4 and columns 1 to 8; never one of the four corner cells. Each subdomain's live slots are its first element_count slots. `vertex_ids`: the 32 ids of one subdomain are different.
All inputs are finite; a program needn't handle non-finite values. No bound on the sum of `element_count` on one device may be relied on, other than what follows from the above.
Results may differ from a plain program's by a relative error of at most 0.0049.
Values may be sent and summed in bfloat16 or wider, within the bound.
No kernel may reach another device: no remote copies, remote signals or barrier semaphores. Data moves between devices by JAX's collectives and lax.ppermute only.
A program may use at most 64 MiB of HBM per device.

v0:
```python
import math

import jax
import jax.numpy as jnp
from jax import lax
from jax.sharding import PartitionSpec as P

CV = 4


def extended_2(x, sides, width):
    for axis, dim in sides:
        peers, length = (lax.axis_size(axis), x.shape[dim])
        up = [(i, (i + 1) % peers) for i in range(peers - 1)]
        down = [(j, i) for i, j in up]
        last = lax.slice_in_dim(x, length - width, length, axis=dim)
        initial = lax.slice_in_dim(x, 0, width, axis=dim)
        before = lax.ppermute(last, axis, up)
        after = lax.ppermute(initial, axis, down)
        x = jnp.concatenate([before, x, after], axis=dim)
    return x


def apply_operator(field, element_faces, element_type, element_count, jacobians):
    row_count = field.shape[0]
    col_count = field.shape[1]
    face_dofs = jacobians.shape[1] // 6
    columns = field.shape[2] // face_dofs
    extended = extended_2(field, (("sub", 0), ("slab", 1)), 1)
    flat_faces = extended.reshape(-1, face_dofs, columns)
    slot_count = element_faces.shape[0]

    def visit(slot_index, totals):
        picked = lax.dynamic_index_in_dim(element_faces, slot_index, 0, keepdims=False)
        element_kind = lax.dynamic_index_in_dim(element_type, slot_index, 0, keepdims=False)
        face_block = jnp.take(flat_faces, picked, axis=0).reshape(6 * face_dofs, columns)
        matrix = lax.dynamic_index_in_dim(jacobians, element_kind, 0, keepdims=False)
        product = jnp.dot(matrix, face_block, preferred_element_type=jnp.float32).reshape(
            6, face_dofs, columns
        )
        weight = (slot_index < element_count[0]).astype(jnp.float32)
        return totals.at[picked].add(product * weight)

    start_totals = jnp.zeros((flat_faces.shape[0], face_dofs, columns), jnp.float32)
    totals = lax.fori_loop(0, slot_count, visit, start_totals)
    gathered = totals.reshape(row_count + 2, col_count + 2, face_dofs * columns)
    returned = extended_2(gathered, (("sub", 0), ("slab", 1)), 1)
    owned = gathered[1:-1, 1:-1]
    owned = owned.at[0].add(returned[0, 2 : col_count + 2])
    owned = owned.at[row_count - 1].add(returned[row_count + 3, 2 : col_count + 2])
    owned = owned.at[:, 0].add(returned[2 : row_count + 2, 0])
    owned = owned.at[:, col_count - 1].add(returned[2 : row_count + 2, col_count + 3])
    return owned


def body(coarse_basis, jacobians, element_faces, element_type, element_count, vertex_ids):
    first_image = apply_operator(
        coarse_basis, element_faces, element_type, element_count, jacobians
    ).astype(jnp.bfloat16)
    second_image = apply_operator(
        first_image, element_faces, element_type, element_count, jacobians
    ).astype(jnp.bfloat16)
    face_dofs = jacobians.shape[1] // 6
    columns = coarse_basis.shape[2] // face_dofs
    left_basis = coarse_basis.reshape(-1, columns)
    right_image = first_image.reshape(-1, columns)
    local_coarse = lax.dot_general(
        left_basis, right_image, (((0,), (0,)), ((), ())), preferred_element_type=jnp.float32
    )
    local_coarse = local_coarse * (1.0 / math.sqrt(left_basis.shape[0]))
    vertex_total = CV * lax.axis_size("sub")
    one_hot = (vertex_ids[0][:, None] == jnp.arange(vertex_total, dtype=jnp.int32)[None, :]).astype(
        jnp.float32
    )
    placed = jnp.dot(
        local_coarse, one_hot, precision=lax.Precision.HIGHEST, preferred_element_type=jnp.float32
    )
    dense_terms = jnp.dot(
        one_hot.T, placed, precision=lax.Precision.HIGHEST, preferred_element_type=jnp.float32
    )
    row_part = lax.psum_scatter(dense_terms, "sub", scatter_dimension=0, tiled=True)
    coarse_matrix = lax.psum(row_part, "slab")
    return (second_image, coarse_matrix)


def solution(mesh):
    return jax.shard_map(
        body,
        mesh=mesh,
        in_specs=(
            P("sub", "slab", None),
            P(),
            P(("sub", "slab"), None),
            P(("sub", "slab")),
            P(("sub", "slab")),
            P(("sub", "slab"), None),
        ),
        out_specs=(P("sub", "slab", None), P("sub", None)),
        check_vma=False,
    )
```

profile of v0, /device:TPU:1, one launch (start us, length us, event | category | flops | bytes accessed | tf_op | source)
XLA Modules:
  0.0 2235.3 jit_solution(7409836133859848624)
XLA Ops:
  8.1 3.9 collective-permute-start
  14.3 2.7 collective-permute-done.1
  17.2 6.0 collective-permute-start.2
  23.2 9.9 collective-permute-start.3
  33.1 5.0 copy.39
  38.6 2.7 reshape.341
  41.4 178.0 %while.34 = (s32[]{:T(128)}, f32[60,125,32]{1,2,0:T(8,128)S(1)}, s32[20,6]{1,0:T(8,128)S(1)}, s32[20]{0:T(128)S(1)}, bf16[4,750,750]{2,1,0:T(8,128)(2,1)}, /*ind...) while((s32[]{:T(128)}, f32[60,125,32]{1,2,0:T(8,128)S(1)}, ...), condition=%wide.region_2.4_spmd, body=%wide.region_0.3_spmd.sunk | while | flops 36073084 | bytes 6445453 | solution.py:45
  225.0 2.7 copy.35
  227.7 3.2 reshape.342
  235.7 8.8 collective-permute-done.5
  249.7 3.4 collective-permute-done.7
  258.8 3.3 collective-permute-done.9
  262.3 3.1 collective-permute-start.10
  267.7 3.6 collective-permute-done.11
  271.7 2.7 reshape.343
  274.5 204.7 %while.35 = (s32[]{:T(128)}, f32[60,125,32]{1,2,0:T(8,128)S(1)}, s32[20,6]{1,0:T(8,128)}, s32[20]{0:T(128)S(1)}, bf16[4,750,750]{2,1,0:T(8,128)(2,1)}, /*index=5...) while((s32[]{:T(128)}, f32[60,125,32]{1,2,0:T(8,128)S(1)}, ...), condition=%wide.region_5.7_spmd, body=%wide.region_3.6_spmd.sunk | while | flops 36073084 | bytes 6445453 | solution.py:45
  479.8 3.1 collective-permute-start.12
  484.6 2.6 copy.40
  487.2 3.2 reshape.344
  492.6 6.4 collective-permute-done.13
  499.2 3.4 collective-permute-start.14
  505.1 3.8 collective-permute-done.15
  510.1 1617.5 %all-reduce.3.cloned.1.call-done = f32[512,512]{1,0:T(8,128)} async-done(((f32[512,512]{1,0:T(8,128)}), f32[512,512]{1,0:T(8,128)}) %all-reduce.3.cloned.1.call-update) | async-done | bytes 1048592
  2128.3 100.2 %psum.7 = f32[4,512]{1,0:T(4,128)} all-reduce(f32[4,512]{1,0:T(4,128)S(1)} %constant_dynamic-slice_fusion.4), channel_id=1, replica_groups=mesh['sub'=128,'slab'=8] {'slab'}, use_global_device_ids=true, to_apply=%region_7.9 | all-reduce | flops 2048 | bytes 16384 | tf_op jit(solution)/shard_map/psum | solution.py:82
  (564 shorter events, 312.4 us)
Async XLA Ops:
  7.2 2120.4 %all-reduce.3.cloned.1.call-start = ((), (), s32[]{:S(2)}) async-start(), calls=%async_computation | async-start | bytes 2097152
  8.1 5.3 collective-permute-start
  12.1 5.0 collective-permute-start.1
  17.2 21.0 collective-permute-start.2
  23.2 14.9 copy-start.2
  23.2 15.0 collective-permute-start.3
  38.6 2.8 copy-start.4
  219.4 0.6 copy-start.1
  219.4 2.9 copy-start
  221.0 14.6 collective-permute-start.4
  234.3 10.3 collective-permute-start.5
  244.8 4.5 collective-permute-start.6
  246.7 6.4 collective-permute-start.7
  255.3 12.1 copy-start.3
  255.3 3.5 collective-permute-start.8
  257.1 5.0 collective-permute-start.9
  262.3 5.5 collective-permute-start.10
  265.4 5.9 collective-permute-start.11
  479.8 12.6 collective-permute-start.12
  491.0 7.9 collective-permute-start.13
  499.2 5.4 collective-permute-start.14
  502.6 6.3 collective-permute-start.15
Sparse Core Ops, SparseCore 0:
  484.7 1642.7 all-reduce.2
where the time goes:
time: 2240 us
  waiting for transfers between devices  1650 us (74%)
  local copies, waits for them, and re-layouts  231 us (10%)
  loops' own time  107 us (5%)
  blocking collectives  100 us (4%)
  other arithmetic  66.2 us (3%)
  starting transfers between devices  45.9 us (2%)
    unnamed x2, waiting for transfers between devices  1620 us
    another operation x2, loops' own time, apply_operator(): totals = lax.fori_loop(0, slot_count, visit, start_totals)  107 us
    psum x1, blocking collectives, body(): coarse_matrix = lax.psum(row_part, 'slab')  100 us
    gather x40, local copies, waits for them, and re-layouts, visit(): jnp.take(flat_faces, picked, axis=0).reshape(6 * face_dofs, columns)  85.2 us
    dynamic_slice x40, local copies, waits for them, and re-layouts, visit(): lax.dynamic_index_in_dim(jacobians, element_kind, 0, keepdims=False)  53.6 us
  transfers between devices with their start and end apart: 17, of which 8 were waited for; matrix products, arithmetic and copies ran while one was open for 1% of the time, Pallas kernels for 0%

commit v1 on v0

v1 whole, which is shorter than its diff:
```python
import functools
import math

import jax
import jax.numpy as jnp
from jax import lax
from jax.experimental import pallas as pl
from jax.experimental.pallas import tpu as pltpu
from jax.sharding import PartitionSpec as P

FR = 32
LANES = 128
PACK = 4
VMEM_LIMIT = 50 * 1024 * 1024


def swap_slots(values):
    slot = lax.broadcasted_iota(jnp.int32, values[0].shape, 1) // 32
    upper = slot >= 2
    odd = slot % 2 == 1
    a, b, c, d = values
    a, c = jnp.where(upper, pltpu.roll(c, 64, 1), a), jnp.where(upper, c, pltpu.roll(a, 64, 1))
    b, d = jnp.where(upper, pltpu.roll(d, 64, 1), b), jnp.where(upper, d, pltpu.roll(b, 64, 1))
    a, b = jnp.where(odd, pltpu.roll(b, 32, 1), a), jnp.where(odd, b, pltpu.roll(a, 96, 1))
    c, d = jnp.where(odd, pltpu.roll(d, 32, 1), c), jnp.where(odd, d, pltpu.roll(c, 96, 1))
    return [a, b, c, d]


def plan_kernel(slots, faces_ref, type_ref, count_ref, cells_ref, kind_ref, total_ref):
    groups = kind_ref.shape[0]
    for i in range(groups * PACK * 6):
        cells_ref[i] = 0
    for i in range(groups):
        kind_ref[i] = 0
    count = count_ref[0]
    kinds = 4

    def tally(slot, sizes):
        live = slot < count
        return tuple(
            size + (live & (type_ref[slot] == kind)).astype(jnp.int32)
            for kind, size in enumerate(sizes)
        )

    sizes = lax.fori_loop(0, slots, tally, (jnp.int32(0),) * kinds)
    firsts, place = [], jnp.int32(0)
    for size in sizes:
        firsts.append(place)
        place = place + (size + PACK - 1) // PACK * PACK
    total_ref[0] = place // PACK

    def put(slot, nexts):
        kind = type_ref[slot]
        position = nexts[kinds - 1]
        for other in range(kinds - 1):
            position = jnp.where(kind == other, nexts[other], position)
        kind_ref[position // PACK] = kind
        for f in range(6):
            cells_ref[position * 6 + f] = faces_ref[slot, f]
        return tuple(at + (kind == other).astype(jnp.int32) for other, at in enumerate(nexts))

    lax.fori_loop(0, count, put, tuple(firsts))


def apply_kernel(
    flat, dims, cells_ref, kind_ref, total_ref, own_ref, up_ref, down_ref, left_ref, right_ref,
    jac_hbm, *rest
):
    rows, cols, dofs = dims
    edge = 6 * dofs
    width = cols + 2
    if flat:
        (t_ref, v_ref, to_up, to_down, to_left, to_right, field, totals, x_ref, y_ref, jac, sem) = rest
    else:
        (t_ref, to_up, to_down, to_left, to_right, field, totals, x_ref, y_ref, jac, sem) = rest

    fetch = pltpu.make_async_copy(jac_hbm, jac, sem)
    fetch.start()

    def cell_rows(cell):
        return pl.ds(pl.multiple_of(cell * FR, FR), FR)

    zero = jnp.zeros((FR, LANES), jnp.float32)
    field[0:FR, :] = zero
    if flat:
        sources = [(own_ref.at[r], (r + 1) * width + 1, 1, cols) for r in range(rows)]
        sources += [(up_ref, 1, 1, cols), (down_ref, (rows + 1) * width + 1, 1, cols)]
        sources += [(left_ref, width, width, rows), (right_ref, 2 * width - 1, width, rows)]
        for ref, first, step, many in sources:
            length = ref.shape[1]
            for a in range(FR):
                high = min(LANES * (a + 1), length)
                tile = ref[:, LANES * a : high].astype(jnp.float32)
                if high < LANES * (a + 1):
                    gap = jnp.zeros((many, LANES * (a + 1) - high), jnp.float32)
                    tile = jnp.concatenate([tile, gap], axis=1)
                field[pl.ds(first * FR + a, many, stride=step * FR), :] = tile
        for r in range(rows):
            for c in range(cols):
                cell = (r + 1) * width + c + 1
                v_ref[r * cols + c] = field[cell * FR : (cell + 1) * FR, :].astype(jnp.bfloat16)
    else:
        for r in range(rows):
            for c in range(cols):
                cell = (r + 1) * width + c + 1
                field[cell * FR : (cell + 1) * FR, :] = own_ref[r * cols + c].astype(jnp.float32)
        for c in range(cols):
            for ref, r in ((up_ref, 0), (down_ref, rows + 1)):
                cell = r * width + c + 1
                field[cell * FR : (cell + 1) * FR, :] = ref[c].astype(jnp.float32)
        for r in range(rows):
            for ref, c in ((left_ref, 0), (right_ref, cols + 1)):
                cell = (r + 1) * width + c
                field[cell * FR : (cell + 1) * FR, :] = ref[r].astype(jnp.float32)
    for cell in range((rows + 2) * width):
        totals[cell * FR : (cell + 1) * FR, :] = zero
    y_ref[edge // 8 * 8 :, :] = jnp.zeros((y_ref.shape[0] - edge // 8 * 8, LANES), jnp.float32)

    fetch.wait()

    def group(g, carry):
        kind = kind_ref[g]
        cells = [[cells_ref[(g * PACK + s) * 6 + f] for s in range(PACK)] for f in range(6)]
        for f in range(6):
            spread = swap_slots([field[cell_rows(cells[f][s]), :] for s in range(PACK)])
            for b in range(4):
                x_ref[pl.ds(f * dofs + b, FR, stride=4), :] = spread[b]
        y_ref[0:edge, :] = jnp.dot(
            jac[kind], x_ref[0:edge, :].astype(jnp.bfloat16), preferred_element_type=jnp.float32
        )
        for f in range(6):
            back = swap_slots([y_ref[pl.ds(f * dofs + b, FR, stride=4), :] for b in range(4)])
            for s in range(PACK):
                at = cell_rows(cells[f][s])
                totals[at, :] = totals[at, :] + back[s]
        return carry

    lax.fori_loop(0, total_ref[0], group, jnp.int32(0))

    for r in range(rows):
        for c in range(cols):
            cell = (r + 1) * width + c + 1
            t_ref[r * cols + c] = totals[cell * FR : (cell + 1) * FR, :]
    for c in range(cols):
        for ref, r in ((to_up, 0), (to_down, rows + 1)):
            cell = r * width + c + 1
            ref[c] = totals[cell * FR : (cell + 1) * FR, :].astype(jnp.bfloat16)
    for r in range(rows):
        for ref, c in ((to_left, 0), (to_right, cols + 1)):
            cell = (r + 1) * width + c
            ref[r] = totals[cell * FR : (cell + 1) * FR, :].astype(jnp.bfloat16)


def combined(dims, r, c, t_ref, up_ref, down_ref, left_ref, right_ref):
    rows, cols, dofs = dims
    value = t_ref[r * cols + c]
    if r == 0:
        value = value + up_ref[c].astype(jnp.float32)
    if r == rows - 1:
        value = value + down_ref[c].astype(jnp.float32)
    if c == 0:
        value = value + left_ref[r].astype(jnp.float32)
    if c == cols - 1:
        value = value + right_ref[r].astype(jnp.float32)
    return value


def middle_kernel(
    dims, t_ref, up_ref, down_ref, left_ref, right_ref, v_ref, ids_ref,
    w_ref, to_up, to_down, to_left, to_right, mail_ref
):
    rows, cols, dofs = dims
    row = lax.broadcasted_iota(jnp.int32, (FR, LANES), 0)
    slot = lax.broadcasted_iota(jnp.int32, (FR, LANES), 1) // 32
    real = row * 4 + slot < dofs
    for r in range(rows):
        for c in range(cols):
            value = combined(dims, r, c, t_ref, up_ref, down_ref, left_ref, right_ref)
            value = jnp.where(real, value, 0.0).astype(jnp.bfloat16)
            w_ref[r * cols + c] = value
            if r == 0:
                to_up[c] = value
            if r == rows - 1:
                to_down[c] = value
            if c == 0:
                to_left[r] = value
            if c == cols - 1:
                to_right[r] = value
    v = v_ref[...].reshape(rows * cols * FR, LANES)
    w = w_ref[...].reshape(rows * cols * FR, LANES)
    square = lax.dot_general(v, w, (((0,), (0,)), ((), ())), preferred_element_type=jnp.float32)
    side = lax.broadcasted_iota(jnp.int32, (LANES, LANES), 1) // 32
    diagonal = lax.broadcasted_iota(jnp.int32, (LANES, LANES), 0) // 32 == side
    square = jnp.where(diagonal, square, 0.0)
    local = square[0:32] + square[32:64] + square[64:96] + square[96:128]
    local = local + pltpu.roll(local, 64, 1)
    local = (local + pltpu.roll(local, 32, 1)) * (1.0 / math.sqrt(rows * cols * dofs))
    local = jnp.where(diagonal, jnp.concatenate([local] * 4, axis=0), 0.0)
    owners = mail_ref.shape[0]
    ids = ids_ref[...]
    owner = lax.broadcasted_iota(jnp.int32, (owners, LANES), 0)
    vertex = 4 * owner + lax.broadcasted_iota(jnp.int32, (owners, LANES), 1) // 32
    place = (vertex == ids).astype(jnp.bfloat16)
    high = local.astype(jnp.bfloat16)
    low = (local - high.astype(jnp.float32)).astype(jnp.bfloat16)
    mail_ref[:, 0, :] = jnp.dot(place, high, preferred_element_type=jnp.float32) + jnp.dot(
        place, low, preferred_element_type=jnp.float32
    )
    mail_ref[:, 1, :] = jnp.broadcast_to(ids.astype(jnp.float32), (owners, LANES))


def expand_kernel(mail_ref, out_ref, turned_ref, flat_ref, hot_ref):
    senders = mail_ref.shape[0]
    vertices = out_ref.shape[2]
    ids = mail_ref[:, 1, :]
    vertex = lax.broadcasted_iota(jnp.int32, (senders, vertices), 1).astype(jnp.float32)
    turned_ref[...] = mail_ref[:, 0, :].T
    for s in range(32):
        part = slice(s * senders, (s + 1) * senders)
        flat_ref[:, part] = turned_ref[pl.ds(s, 4, stride=32), :]
        hot_ref[part, :] = (ids[:, s : s + 1] == vertex).astype(jnp.bfloat16)
    values = flat_ref[...]
    high = values.astype(jnp.bfloat16).astype(jnp.float32)
    both = jnp.concatenate([high, values - high], axis=0).astype(jnp.bfloat16)
    wide = jnp.dot(both, hot_ref[...], preferred_element_type=jnp.float32)
    total = wide[0:4] + wide[4:8]
    for j in range(out_ref.shape[0]):
        out_ref[j] = total


def last_kernel(dims, t_ref, up_ref, down_ref, left_ref, right_ref, out_ref, hold):
    rows, cols, dofs = dims
    length = out_ref.shape[2]
    for r in range(rows):
        for c in range(cols):
            value = combined(dims, r, c, t_ref, up_ref, down_ref, left_ref, right_ref)
            hold[pl.ds(r * FR * cols + c, FR, stride=cols), :] = value
    for r in range(rows):
        for a in range(FR):
            high = min(LANES * (a + 1), length)
            start = (r * FR + a) * cols
            tile = hold[start : start + cols, 0 : high - LANES * a]
            out_ref[r, :, LANES * a : high] = tile.astype(jnp.bfloat16)


VM = pl.BlockSpec(memory_space=pltpu.VMEM)
SM = pl.BlockSpec(memory_space=pltpu.SMEM)
HBM = pl.BlockSpec(memory_space=pltpu.HBM)


def struct(shape, dtype=jnp.bfloat16):
    return jax.ShapeDtypeStruct(shape, dtype)


def plan(element_faces, element_type, element_count):
    slots = element_faces.shape[0]
    groups = (slots + 3 * 4) // PACK + 1
    return pl.pallas_call(
        functools.partial(plan_kernel, slots),
        out_shape=(
            struct((groups * PACK * 6,), jnp.int32),
            struct((groups,), jnp.int32),
            struct((1,), jnp.int32),
        ),
        in_specs=[SM] * 3,
        out_specs=(SM,) * 3,
        name="plan",
    )(element_faces, element_type, element_count)


def rim_structs(rows, cols):
    return (
        struct((cols, FR, LANES)),
        struct((cols, FR, LANES)),
        struct((rows, FR, LANES)),
        struct((rows, FR, LANES)),
    )


def apply(flat, dims, table, own, rims, jacobians):
    rows, cols, dofs = dims
    cells = rows * cols
    out = (struct((cells, FR, LANES), jnp.float32),)
    if flat:
        out += (struct((cells, FR, LANES)),)
    out += rim_structs(rows, cols)
    area = (rows + 2) * (cols + 2) * FR
    flops = 2 * 16 * 36 * dofs * dofs * 32
    moved = jacobians.size * 2 + cells * FR * LANES * 6
    return pl.pallas_call(
        functools.partial(apply_kernel, flat, dims),
        out_shape=out,
        in_specs=[SM] * 3 + [VM] * 5 + [HBM],
        out_specs=(VM,) * len(out),
        scratch_shapes=[
            pltpu.VMEM((area, LANES), jnp.float32),
            pltpu.VMEM((area, LANES), jnp.float32),
            pltpu.VMEM((6 * dofs + 10, LANES), jnp.float32),
            pltpu.VMEM((6 * dofs + 10, LANES), jnp.float32),
            pltpu.VMEM(jacobians.shape, jnp.bfloat16),
            pltpu.SemaphoreType.DMA,
        ],
        compiler_params=pltpu.CompilerParams(vmem_limit_bytes=VMEM_LIMIT),
        cost_estimate=pl.CostEstimate(flops=flops, bytes_accessed=moved, transcendentals=0),
        name="apply_flat" if flat else "apply_tiles",
    )(*table, own, *rims, jacobians)


def middle(dims, total, rims, tiles, ids, owners):
    rows, cols, dofs = dims
    cells = rows * cols
    return pl.pallas_call(
        functools.partial(middle_kernel, dims),
        out_shape=(struct((cells, FR, LANES)),)
        + rim_structs(rows, cols)
        + (struct((owners, 2, LANES), jnp.float32),),
        in_specs=[VM] * 7,
        out_specs=(VM,) * 6,
        compiler_params=pltpu.CompilerParams(vmem_limit_bytes=VMEM_LIMIT),
        cost_estimate=pl.CostEstimate(flops=2**26, bytes_accessed=2**20, transcendentals=0),
        name="middle",
    )(total, *rims, tiles, ids)


def expand(mail, narrow, vertex_total):
    owned = vertex_total // mail.shape[0]
    return pl.pallas_call(
        expand_kernel,
        out_shape=struct((narrow, owned, vertex_total), jnp.float32),
        in_specs=[VM],
        out_specs=VM,
        scratch_shapes=[
            pltpu.VMEM((LANES, mail.shape[0]), jnp.float32),
            pltpu.VMEM((owned, 32 * mail.shape[0]), jnp.float32),
            pltpu.VMEM((32 * mail.shape[0], vertex_total), jnp.bfloat16),
        ],
        compiler_params=pltpu.CompilerParams(vmem_limit_bytes=VMEM_LIMIT),
        cost_estimate=pl.CostEstimate(flops=2**30, bytes_accessed=2**18, transcendentals=0),
        name="expand",
    )(mail)


def last(dims, total, rims, length):
    rows, cols, dofs = dims
    return pl.pallas_call(
        functools.partial(last_kernel, dims),
        out_shape=struct((rows, cols, length)),
        in_specs=[VM] * 5,
        out_specs=VM,
        scratch_shapes=[pltpu.VMEM((rows * cols * FR, LANES), jnp.float32)],
        compiler_params=pltpu.CompilerParams(vmem_limit_bytes=VMEM_LIMIT),
        name="last",
    )(total, *rims)


def exchange(to_up, to_down, to_left, to_right):
    def ring(axis):
        peers = lax.axis_size(axis)
        ahead = [(i, i + 1) for i in range(peers - 1)]
        return ahead, [(j, i) for i, j in ahead]

    ahead, back = ring("sub")
    from_up = lax.ppermute(to_down, "sub", ahead)
    from_down = lax.ppermute(to_up, "sub", back)
    ahead, back = ring("slab")
    from_left = lax.ppermute(to_right, "slab", ahead)
    from_right = lax.ppermute(to_left, "slab", back)
    return from_up, from_down, from_left, from_right


def body(coarse_basis, jacobians, element_faces, element_type, element_count, vertex_ids):
    rows, cols, length = coarse_basis.shape
    dofs = jacobians.shape[1] // 6
    dims = (rows, cols, dofs)
    owners, narrow = lax.axis_size("sub"), lax.axis_size("slab")
    ids = jnp.tile(vertex_ids, (1, 4))

    rims = exchange(coarse_basis[0], coarse_basis[rows - 1], coarse_basis[:, 0], coarse_basis[:, cols - 1])
    table = plan(element_faces, element_type, element_count)
    total, tiles, *sent = apply(True, dims, table, coarse_basis, rims, jacobians)
    first, *halo, mail = middle(dims, total, exchange(*sent), tiles, ids, owners)
    mail = lax.all_to_all(mail, "sub", 0, 0)
    rims = exchange(*halo)
    total, *sent = apply(False, dims, table, first, rims, jacobians)
    rims = exchange(*sent)
    mail, unused = lax.optimization_barrier((mail, rims[0]))
    parts = lax.all_to_all(expand(mail, narrow, rows * owners), "slab", 0, 0)
    second_image = last(dims, total, rims, length)
    return second_image, parts.sum(0)


def solution(mesh):
    return jax.shard_map(
        body,
        mesh=mesh,
        in_specs=(
            P("sub", "slab", None),
            P(),
            P(("sub", "slab"), None),
            P(("sub", "slab")),
            P(("sub", "slab")),
            P(("sub", "slab"), None),
        ),
        out_specs=(P("sub", "slab", None), P("sub", None)),
        check_vma=False,
    )
```

time: 2240 us -> 160 us (0.07)
  the two profiles are of different devices: /device:TPU:1 before, /device:TPU:127 now
where the time goes in v1:
time: 160 us; the launch traced here: 159 us
  starting transfers between devices  92.2 us (58%)
  Pallas kernels  29.6 us (18%)
  waiting for transfers between devices  24.5 us (15%)
  local copies, waits for them, and re-layouts  9.98 us (6%)
    ppermute x4, starting transfers between devices, exchange(): from_up = lax.ppermute(to_down, 'sub', ahead)  31.4 us
    all_to_all x1, starting transfers between devices, body(): mail = lax.all_to_all(mail, 'sub', 0, 0)  20.9 us
    pallas_call x2, Pallas kernels, apply(): pl.pallas_call(functools.partial(apply_kernel, flat, dims), out_shape=out...  19.9 us
    ppermute x4, starting transfers between devices, exchange(): from_left = lax.ppermute(to_right, 'slab', ahead)  16.3 us
    ppermute x4, waiting for transfers between devices, exchange(): from_down = lax.ppermute(to_up, 'sub', back)  13.9 us
    ppermute x4, starting transfers between devices, exchange(): from_down = lax.ppermute(to_up, 'sub', back)  9.65 us
    ppermute x4, waiting for transfers between devices, exchange(): from_right = lax.ppermute(to_left, 'slab', back)  9.3 us
    ppermute x4, starting transfers between devices, exchange(): from_right = lax.ppermute(to_left, 'slab', back)  8.17 us
  transfers between devices with their start and end apart: 18, of which 7 were waited for; matrix products, arithmetic and copies ran while one was open for 5% of the time, Pallas kernels for 8%

profile of v1, /device:TPU:127, one launch (start us, length us, event | category | flops | bytes accessed | tf_op | source)
XLA Modules:
  0.0 158.6 jit_solution(9581976753006345689)
XLA Ops:
  1.5 2.5 %collective-permute-start.1 = (bf16[8,4000]{1,0:T(8,128)(2,1)S(1)}, bf16[8,4000]{1,0:T(8,128)(2,1)S(1)}, u32[]{:S(2)}, u32[]{:S(2)}) collective-permute-start(bf16[8,4000]{1,0:T(8,128)(2,1)S(1)} %get-tuple-element.46), channel_id=1, source_target_pairs={{8,0},{16,8},{24,16},{32,24},{40,32},{48,40},{56,48},{64,56},{72,6... | collective-permute-start | bytes 192008 | tf_op jit(solution)/shard_map/ppermute | solution.py:364
  4.0 11.0 %collective-permute-start = (bf16[8,4000]{1,0:T(8,128)(2,1)S(1)}, bf16[8,4000]{1,0:T(8,128)(2,1)S(1)}, u32[]{:S(2)}, u32[]{:S(2)}) collective-permute-start(bf16[8,4000]{1,0:T(8,128)(2,1)S(1)} %get-tuple-element.47), channel_id=1, source_target_pairs={{0,8},{8,16},{16,24},{24,32},{32,40},{40,48},{48,56},{56,64},{64,7... | collective-permute-start | bytes 192008 | tf_op jit(solution)/shard_map/ppermute | solution.py:363
  16.1 5.1 %collective-permute-start.2 = (bf16[4,4000]{1,0:T(4,128)(2,1)S(1)}, bf16[4,4000]{1,0:T(4,128)(2,1)S(1)}, u32[]{:S(2)}, u32[]{:S(2)}) collective-permute-start(bf16[4,4000]{1,0:T(4,128)(2,1)S(1)} %bitcast.11), channel_id=1, source_target_pairs={{0,1},{1,2},{2,3},{3,4},{4,5},{5,6},{6,7},{8,9},{9,10},{10,11},{11... | collective-permute-start | bytes 96008 | tf_op jit(solution)/shard_map/ppermute | solution.py:366
  21.3 1.9 %collective-permute-start.3 = (bf16[4,4000]{1,0:T(4,128)(2,1)S(1)}, bf16[4,4000]{1,0:T(4,128)(2,1)S(1)}, u32[]{:S(2)}, u32[]{:S(2)}) collective-permute-start(bf16[4,4000]{1,0:T(4,128)(2,1)S(1)} %bitcast.12), channel_id=1, source_target_pairs={{1,0},{2,1},{3,2},{4,3},{5,4},{6,5},{7,6},{9,8},{10,9},{11,10},{12... | collective-permute-start | bytes 96008 | tf_op jit(solution)/shard_map/ppermute | solution.py:367
  25.3 5.0 %copy.11.jac_hbm = bf16[4,750,750]{2,1,0:T(8,128)(2,1)} copy(bf16[4,750,750]{2,0,1:T(4,128)(2,1)} %param.7) | data formatting | bytes 9000000 | tf_op args[1]
  30.3 2.4 %plan.1 = (s32[216]{0:T(256)}, s32[9]{0:T(128)}, s32[1]{0:T(128)}) custom-call(s32[20,6]{1,0:T(8,128)} %copy.8.faces_ref, s32[20]{0:T(128)} %type_ref.1, s32[1]{0:T(128)S(6)} %copy.19.count_ref), custom_call_target="tpu_custom_call" | custom-call | tf_op jit(solution)/shard_map/plan/pallas_call | solution.py:258
  34.1 9.9 %apply_flat.1 = (f32[32,32,128]{2,1,0:T(8,128)S(1)}, bf16[32,32,128]{2,1,0:T(8,128)(2,1)S(1)}, bf16[8,32,128]{2,1,0:T(8,128)(2,1)S(1)}, bf16[8,32,128]{2,1,0:T(8...) custom-call(s32[216]{0:T(256)S(1)} %copy-done.1, s32[9]{0:T(128)S(1)} %copy-done.3, ...), custom_call_target="tpu_custom_call" | custom-call | flops 576000000 | bytes 5286432 | tf_op jit(solution)/shard_map/apply_flat/pallas_call | solution.py:290
  46.0 3.4 %collective-permute-start.5 = (bf16[8,32,128]{2,1,0:T(8,128)(2,1)S(1)}, bf16[8,32,128]{2,1,0:T(8,128)(2,1)S(1)}, u32[]{:S(2)}, u32[]{:S(2)}) collective-permute-start(bf16[8,32,128]{2,1,0:T(8,128)(2,1)S(1)} %get-tuple-element.28), channel_id=1, source_target_pairs={{8,0},{16,8},{24,16},{32,24},{40,32},{48,40},{56,48},{64,56},{72,6... | collective-permute-start | bytes 196616 | tf_op jit(solution)/shard_map/ppermute | solution.py:364
  51.3 2.4 %collective-permute-start.7 = (bf16[4,32,128]{2,1,0:T(8,128)(2,1)S(1)}, bf16[4,32,128]{2,1,0:T(8,128)(2,1)S(1)}, u32[]{:S(2)}, u32[]{:S(2)}) collective-permute-start(bf16[4,32,128]{2,1,0:T(8,128)(2,1)S(1)} %get-tuple-element.30), channel_id=1, source_target_pairs={{1,0},{2,1},{3,2},{4,3},{5,4},{6,5},{7,6},{9,8},{10,9},{11,10},{12... | collective-permute-start | bytes 98312 | tf_op jit(solution)/shard_map/ppermute | solution.py:367
  53.8 2.7 %collective-permute-done.7.right_ref = bf16[4,32,128]{2,1,0:T(8,128)(2,1)S(1)} collective-permute-done((bf16[4,32,128]{2,1,0:T(8,128)(2,1)S(1)}, bf16[4,32,128]{2,1,0:T(8,128)(2,1)S(1)}, u32[]{:S(2)}, u32[]{:S(2)}) %collective-permute-start.7) | collective-permute-done | bytes 32800 | tf_op jit(solution)/shard_map/ppermute | solution.py:367
  56.6 4.6 %collective-permute-done.5.down_ref = bf16[8,32,128]{2,1,0:T(8,128)(2,1)S(1)} collective-permute-done((bf16[8,32,128]{2,1,0:T(8,128)(2,1)S(1)}, bf16[8,32,128]{2,1,0:T(8,128)(2,1)S(1)}, u32[]{:S(2)}, u32[]{:S(2)}) %collective-permute-start.5) | collective-permute-done | bytes 65568 | tf_op jit(solution)/shard_map/ppermute | solution.py:364
  62.5 20.9 %all-to-all-start = ((f32[128,2,128]{2,1,0:T(2,128)}), f32[128,2,128]{2,1,0:T(2,128)S(1)}, u32[]{:S(2)}, u32[]{:S(2)}) async-start(f32[128,2,128]{2,1,0:T(2,128)} %get-tuple-element.42), calls=%async_computation | async-start | bytes 262144 | tf_op jit(solution)/shard_map/all_to_all | solution.py:382
  83.4 7.0 %collective-permute-start.8 = (bf16[8,32,128]{2,1,0:T(8,128)(2,1)S(1)}, bf16[8,32,128]{2,1,0:T(8,128)(2,1)S(1)}, u32[]{:S(2)}, u32[]{:S(2)}) collective-permute-start(bf16[8,32,128]{2,1,0:T(8,128)(2,1)S(1)} %get-tuple-element.33), channel_id=1, source_target_pairs={{0,8},{8,16},{16,24},{24,32},{32,40},{40,48},{48,56},{56,64},{64,7... | collective-permute-start | bytes 196616 | tf_op jit(solution)/shard_map/ppermute | solution.py:363
  90.4 1.9 %collective-permute-start.9 = (bf16[8,32,128]{2,1,0:T(8,128)(2,1)S(1)}, bf16[8,32,128]{2,1,0:T(8,128)(2,1)S(1)}, u32[]{:S(2)}, u32[]{:S(2)}) collective-permute-start(bf16[8,32,128]{2,1,0:T(8,128)(2,1)S(1)} %get-tuple-element.34), channel_id=1, source_target_pairs={{8,0},{16,8},{24,16},{32,24},{40,32},{48,40},{56,48},{64,56},{72,6... | collective-permute-start | bytes 196616 | tf_op jit(solution)/shard_map/ppermute | solution.py:364
  92.3 6.0 %collective-permute-start.10 = (bf16[4,32,128]{2,1,0:T(8,128)(2,1)S(1)}, bf16[4,32,128]{2,1,0:T(8,128)(2,1)S(1)}, u32[]{:S(2)}, u32[]{:S(2)}) collective-permute-start(bf16[4,32,128]{2,1,0:T(8,128)(2,1)S(1)} %get-tuple-element.35), channel_id=1, source_target_pairs={{0,1},{1,2},{2,3},{3,4},{4,5},{5,6},{6,7},{8,9},{9,10},{10,11},{11... | collective-permute-start | bytes 98312 | tf_op jit(solution)/shard_map/ppermute | solution.py:366
  98.3 1.9 %collective-permute-start.11 = (bf16[4,32,128]{2,1,0:T(8,128)(2,1)S(1)}, bf16[4,32,128]{2,1,0:T(8,128)(2,1)S(1)}, u32[]{:S(2)}, u32[]{:S(2)}) collective-permute-start(bf16[4,32,128]{2,1,0:T(8,128)(2,1)S(1)} %get-tuple-element.36), channel_id=1, source_target_pairs={{1,0},{2,1},{3,2},{4,3},{5,4},{6,5},{7,6},{9,8},{10,9},{11,10},{12... | collective-permute-start | bytes 98312 | tf_op jit(solution)/shard_map/ppermute | solution.py:367
  100.3 3.3 %collective-permute-done.11.right_ref = bf16[4,32,128]{2,1,0:T(8,128)(2,1)S(1)} collective-permute-done((bf16[4,32,128]{2,1,0:T(8,128)(2,1)S(1)}, bf16[4,32,128]{2,1,0:T(8,128)(2,1)S(1)}, u32[]{:S(2)}, u32[]{:S(2)}) %collective-permute-start.11) | collective-permute-done | bytes 32800 | tf_op jit(solution)/shard_map/ppermute | solution.py:367
  103.9 9.9 %apply_tiles.1 = (f32[32,32,128]{2,1,0:T(8,128)S(1)}, bf16[8,32,128]{2,1,0:T(8,128)(2,1)S(1)}, bf16[8,32,128]{2,1,0:T(8,128)(2,1)S(1)}, bf16[4,32,128]{2,1,0:T(8,128)(2,1)S(1)}, bf16[4,32,128]{2,1,0:T(8,128)(2,1)S(1)}) custom-call(s32[216]{0:T(256)S(1)} %copy-done.2, s32[9]{0:T(128)S(1)} %copy-done.4, s32[1]{0:T(128)} %get-tuple-element.25.total_ref, ...), custom_call_target="tpu_custom_call" | custom-call | flops 576000000 | bytes 5286432 | tf_op jit(solution)/shard_map/apply_tiles/pallas_call | solution.py:290
  113.8 11.5 %collective-permute-start.12 = (bf16[8,32,128]{2,1,0:T(8,128)(2,1)S(1)}, bf16[8,32,128]{2,1,0:T(8,128)(2,1)S(1)}, u32[]{:S(2)}, u32[]{:S(2)}) collective-permute-start(bf16[8,32,128]{2,1,0:T(8,128)(2,1)S(1)} %get-tuple-element.38), channel_id=1, source_target_pairs={{0,8},{8,16},{16,24},{24,32},{32,40},{40,48},{48,56},{56,64},{64,7... | collective-permute-start | bytes 196616 | tf_op jit(solution)/shard_map/ppermute | solution.py:363
  126.7 5.2 %expand.1 = f32[8,4,512]{2,1,0:T(4,128)} custom-call(f32[128,2,128]{2,1,0:T(2,128)S(1)} %all-to-all-done.mail_ref), custom_call_target="tpu_custom_call" | custom-call | flops 1073741824 | bytes 262144 | tf_op jit(solution)/shard_map/expand/pallas_call | solution.py:327
  131.9 5.8 %all-to-all-start.1 = ((f32[8,4,512]{2,1,0:T(4,128)}), f32[8,4,512]{2,1,0:T(4,128)S(1)}, u32[]{:S(2)}, u32[]{:S(2)}) async-start(f32[8,4,512]{2,1,0:T(4,128)} %expand.1), calls=%async_computation.1 | async-start | bytes 131072 | tf_op jit(solution)/shard_map/all_to_all | solution.py:387
  139.6 3.3 %collective-permute-start.14 = (bf16[4,32,128]{2,1,0:T(8,128)(2,1)S(1)}, bf16[4,32,128]{2,1,0:T(8,128)(2,1)S(1)}, u32[]{:S(2)}, u32[]{:S(2)}) collective-permute-start(bf16[4,32,128]{2,1,0:T(8,128)(2,1)S(1)} %get-tuple-element.40), channel_id=1, source_target_pairs={{0,1},{1,2},{2,3},{3,4},{4,5},{5,6},{6,7},{8,9},{9,10},{10,11},{11... | collective-permute-start | bytes 98312 | tf_op jit(solution)/shard_map/ppermute | solution.py:366
  144.9 3.3 %collective-permute-done.15.right_ref = bf16[4,32,128]{2,1,0:T(8,128)(2,1)S(1)} collective-permute-done((bf16[4,32,128]{2,1,0:T(8,128)(2,1)S(1)}, bf16[4,32,128]{2,1,0:T(8,128)(2,1)S(1)}, u32[]{:S(2)}, u32[]{:S(2)}) %collective-permute-start.15) | collective-permute-done | bytes 32800 | tf_op jit(solution)/shard_map/ppermute | solution.py:367
  148.2 8.9 %collective-permute-done.13.down_ref = bf16[8,32,128]{2,1,0:T(8,128)(2,1)S(1)} collective-permute-done((bf16[8,32,128]{2,1,0:T(8,128)(2,1)S(1)}, bf16[8,32,128]{2,1,0:T(8,128)(2,1)S(1)}, u32[]{:S(2)}, u32[]{:S(2)}) %collective-permute-start.13) | collective-permute-done | bytes 65568 | tf_op jit(solution)/shard_map/ppermute | solution.py:364
  (39 shorter events, 17.0 us)
Async XLA Ops:
  1.5 31.2 %collective-permute-start.1 = (bf16[8,4000]{1,0:T(8,128)(2,1)S(1)}, bf16[8,4000]{1,0:T(8,128)(2,1)S(1)}, u32[]{:S(2)}, u32[]{:S(2)}) collective-permute-start(bf16[8,4000]{1,0:T(8,128)(2,1)S(1)} %get-tuple-element.46), channel_id=1, source_target_pairs={{8,0},{16,8},{24,16},{32,24},{40,32},{48,40},{56,48},{64,56},{72,6... | collective-permute-start | bytes 192008 | tf_op jit(solution)/shard_map/ppermute | solution.py:364
  4.0 28.8 %collective-permute-start = (bf16[8,4000]{1,0:T(8,128)(2,1)S(1)}, bf16[8,4000]{1,0:T(8,128)(2,1)S(1)}, u32[]{:S(2)}, u32[]{:S(2)}) collective-permute-start(bf16[8,4000]{1,0:T(8,128)(2,1)S(1)} %get-tuple-element.47), channel_id=1, source_target_pairs={{0,8},{8,16},{16,24},{24,32},{32,40},{40,48},{48,56},{56,64},{64,7... | collective-permute-start | bytes 192008 | tf_op jit(solution)/shard_map/ppermute | solution.py:363
  16.1 16.6 %collective-permute-start.2 = (bf16[4,4000]{1,0:T(4,128)(2,1)S(1)}, bf16[4,4000]{1,0:T(4,128)(2,1)S(1)}, u32[]{:S(2)}, u32[]{:S(2)}) collective-permute-start(bf16[4,4000]{1,0:T(4,128)(2,1)S(1)} %bitcast.11), channel_id=1, source_target_pairs={{0,1},{1,2},{2,3},{3,4},{4,5},{5,6},{6,7},{8,9},{9,10},{10,11},{11... | collective-permute-start | bytes 96008 | tf_op jit(solution)/shard_map/ppermute | solution.py:366
  21.3 11.4 %collective-permute-start.3 = (bf16[4,4000]{1,0:T(4,128)(2,1)S(1)}, bf16[4,4000]{1,0:T(4,128)(2,1)S(1)}, u32[]{:S(2)}, u32[]{:S(2)}) collective-permute-start(bf16[4,4000]{1,0:T(4,128)(2,1)S(1)} %bitcast.12), channel_id=1, source_target_pairs={{1,0},{2,1},{3,2},{4,3},{5,4},{6,5},{7,6},{9,8},{10,9},{11,10},{12... | collective-permute-start | bytes 96008 | tf_op jit(solution)/shard_map/ppermute | solution.py:367
  25.3 7.5 %copy-start = (bf16[4,8,4000]{2,1,0:T(8,128)(2,1)S(1)}, bf16[4,8,4000]{2,1,0:T(8,128)(2,1)}, u32[]{:S(2)}) copy-start(bf16[4,8,4000]{2,1,0:T(8,128)(2,1)} %own_ref.1) | copy-start | bytes 768004
  30.3 23.4 %copy-start.5 = (s32[1,32]{1,0:T(1,128)S(1)}, s32[1,32]{1,0:T(1,128)}, u32[]{:S(2)}) copy-start(s32[1,32]{1,0:T(1,128)} %param.11) | copy-start | bytes 388
  32.7 71.2 %copy-start.2 = (s32[216]{0:T(256)S(1)}, s32[216]{0:T(256)}, u32[]{:S(2)}) copy-start(s32[216]{0:T(256)} %get-tuple-element.23.cells_ref) | copy-start | bytes 2596
  32.7 71.1 %copy-start.4 = (s32[9]{0:T(128)S(1)}, s32[9]{0:T(128)}, u32[]{:S(2)}) copy-start(s32[9]{0:T(128)} %get-tuple-element.24.kind_ref) | copy-start | bytes 112
  32.8 0.7 copy-start.1
  33.5 0.7 copy-start.3
  44.1 12.5 %collective-permute-start.4 = (bf16[8,32,128]{2,1,0:T(8,128)(2,1)S(1)}, bf16[8,32,128]{2,1,0:T(8,128)(2,1)S(1)}, u32[]{:S(2)}, u32[]{:S(2)}) collective-permute-start(bf16[8,32,128]{2,1,0:T(8,128)(2,1)S(1)} %get-tuple-element.27), channel_id=1, source_target_pairs={{0,8},{8,16},{16,24},{24,32},{32,40},{40,48},{48,56},{56,64},{64,7... | collective-permute-start | bytes 196616 | tf_op jit(solution)/shard_map/ppermute | solution.py:363
  46.0 15.2 %collective-permute-start.5 = (bf16[8,32,128]{2,1,0:T(8,128)(2,1)S(1)}, bf16[8,32,128]{2,1,0:T(8,128)(2,1)S(1)}, u32[]{:S(2)}, u32[]{:S(2)}) collective-permute-start(bf16[8,32,128]{2,1,0:T(8,128)(2,1)S(1)} %get-tuple-element.28), channel_id=1, source_target_pairs={{8,0},{16,8},{24,16},{32,24},{40,32},{48,40},{56,48},{64,56},{72,6... | collective-permute-start | bytes 196616 | tf_op jit(solution)/shard_map/ppermute | solution.py:364
  49.4 4.4 %collective-permute-start.6 = (bf16[4,32,128]{2,1,0:T(8,128)(2,1)S(1)}, bf16[4,32,128]{2,1,0:T(8,128)(2,1)S(1)}, u32[]{:S(2)}, u32[]{:S(2)}) collective-permute-start(bf16[4,32,128]{2,1,0:T(8,128)(2,1)S(1)} %get-tuple-element.29), channel_id=1, source_target_pairs={{0,1},{1,2},{2,3},{3,4},{4,5},{5,6},{6,7},{8,9},{9,10},{10,11},{11... | collective-permute-start | bytes 98312 | tf_op jit(solution)/shard_map/ppermute | solution.py:366
  51.3 5.2 %collective-permute-start.7 = (bf16[4,32,128]{2,1,0:T(8,128)(2,1)S(1)}, bf16[4,32,128]{2,1,0:T(8,128)(2,1)S(1)}, u32[]{:S(2)}, u32[]{:S(2)}) collective-permute-start(bf16[4,32,128]{2,1,0:T(8,128)(2,1)S(1)} %get-tuple-element.30), channel_id=1, source_target_pairs={{1,0},{2,1},{3,2},{4,3},{5,4},{6,5},{7,6},{9,8},{10,9},{11,10},{12... | collective-permute-start | bytes 98312 | tf_op jit(solution)/shard_map/ppermute | solution.py:367
  62.5 64.2 %all-to-all-start = ((f32[128,2,128]{2,1,0:T(2,128)}), f32[128,2,128]{2,1,0:T(2,128)S(1)}, u32[]{:S(2)}, u32[]{:S(2)}) async-start(f32[128,2,128]{2,1,0:T(2,128)} %get-tuple-element.42), calls=%async_computation | async-start | bytes 262144 | tf_op jit(solution)/shard_map/all_to_all | solution.py:382
  83.4 20.2 %collective-permute-start.8 = (bf16[8,32,128]{2,1,0:T(8,128)(2,1)S(1)}, bf16[8,32,128]{2,1,0:T(8,128)(2,1)S(1)}, u32[]{:S(2)}, u32[]{:S(2)}) collective-permute-start(bf16[8,32,128]{2,1,0:T(8,128)(2,1)S(1)} %get-tuple-element.33), channel_id=1, source_target_pairs={{0,8},{8,16},{16,24},{24,32},{32,40},{40,48},{48,56},{56,64},{64,7... | collective-permute-start | bytes 196616 | tf_op jit(solution)/shard_map/ppermute | solution.py:363
  90.4 13.4 %collective-permute-start.9 = (bf16[8,32,128]{2,1,0:T(8,128)(2,1)S(1)}, bf16[8,32,128]{2,1,0:T(8,128)(2,1)S(1)}, u32[]{:S(2)}, u32[]{:S(2)}) collective-permute-start(bf16[8,32,128]{2,1,0:T(8,128)(2,1)S(1)} %get-tuple-element.34), channel_id=1, source_target_pairs={{8,0},{16,8},{24,16},{32,24},{40,32},{48,40},{56,48},{64,56},{72,6... | collective-permute-start | bytes 196616 | tf_op jit(solution)/shard_map/ppermute | solution.py:364
  92.3 7.9 %collective-permute-start.10 = (bf16[4,32,128]{2,1,0:T(8,128)(2,1)S(1)}, bf16[4,32,128]{2,1,0:T(8,128)(2,1)S(1)}, u32[]{:S(2)}, u32[]{:S(2)}) collective-permute-start(bf16[4,32,128]{2,1,0:T(8,128)(2,1)S(1)} %get-tuple-element.35), channel_id=1, source_target_pairs={{0,1},{1,2},{2,3},{3,4},{4,5},{5,6},{6,7},{8,9},{9,10},{10,11},{11... | collective-permute-start | bytes 98312 | tf_op jit(solution)/shard_map/ppermute | solution.py:366
  98.3 5.2 %collective-permute-start.11 = (bf16[4,32,128]{2,1,0:T(8,128)(2,1)S(1)}, bf16[4,32,128]{2,1,0:T(8,128)(2,1)S(1)}, u32[]{:S(2)}, u32[]{:S(2)}) collective-permute-start(bf16[4,32,128]{2,1,0:T(8,128)(2,1)S(1)} %get-tuple-element.36), channel_id=1, source_target_pairs={{1,0},{2,1},{3,2},{4,3},{5,4},{6,5},{7,6},{9,8},{10,9},{11,10},{12... | collective-permute-start | bytes 98312 | tf_op jit(solution)/shard_map/ppermute | solution.py:367
  113.8 12.8 %collective-permute-start.12 = (bf16[8,32,128]{2,1,0:T(8,128)(2,1)S(1)}, bf16[8,32,128]{2,1,0:T(8,128)(2,1)S(1)}, u32[]{:S(2)}, u32[]{:S(2)}) collective-permute-start(bf16[8,32,128]{2,1,0:T(8,128)(2,1)S(1)} %get-tuple-element.38), channel_id=1, source_target_pairs={{0,8},{8,16},{16,24},{24,32},{32,40},{40,48},{48,56},{56,64},{64,7... | collective-permute-start | bytes 196616 | tf_op jit(solution)/shard_map/ppermute | solution.py:363
  131.9 26.1 %all-to-all-start.1 = ((f32[8,4,512]{2,1,0:T(4,128)}), f32[8,4,512]{2,1,0:T(4,128)S(1)}, u32[]{:S(2)}, u32[]{:S(2)}) async-start(f32[8,4,512]{2,1,0:T(4,128)} %expand.1), calls=%async_computation.1 | async-start | bytes 131072 | tf_op jit(solution)/shard_map/all_to_all | solution.py:387
  137.7 19.4 %collective-permute-start.13 = (bf16[8,32,128]{2,1,0:T(8,128)(2,1)S(1)}, bf16[8,32,128]{2,1,0:T(8,128)(2,1)S(1)}, u32[]{:S(2)}, u32[]{:S(2)}) collective-permute-start(bf16[8,32,128]{2,1,0:T(8,128)(2,1)S(1)} %get-tuple-element.39), channel_id=1, source_target_pairs={{8,0},{16,8},{24,16},{32,24},{40,32},{48,40},{56,48},{64,56},{72,6... | collective-permute-start | bytes 196616 | tf_op jit(solution)/shard_map/ppermute | solution.py:364
  139.6 5.3 %collective-permute-start.14 = (bf16[4,32,128]{2,1,0:T(8,128)(2,1)S(1)}, bf16[4,32,128]{2,1,0:T(8,128)(2,1)S(1)}, u32[]{:S(2)}, u32[]{:S(2)}) collective-permute-start(bf16[4,32,128]{2,1,0:T(8,128)(2,1)S(1)} %get-tuple-element.40), channel_id=1, source_target_pairs={{0,1},{1,2},{2,3},{3,4},{4,5},{5,6},{6,7},{8,9},{9,10},{10,11},{11... | collective-permute-start | bytes 98312 | tf_op jit(solution)/shard_map/ppermute | solution.py:366
  143.0 5.2 %collective-permute-start.15 = (bf16[4,32,128]{2,1,0:T(8,128)(2,1)S(1)}, bf16[4,32,128]{2,1,0:T(8,128)(2,1)S(1)}, u32[]{:S(2)}, u32[]{:S(2)}) collective-permute-start(bf16[4,32,128]{2,1,0:T(8,128)(2,1)S(1)} %get-tuple-element.41), channel_id=1, source_target_pairs={{1,0},{2,1},{3,2},{4,3},{5,4},{6,5},{7,6},{9,8},{10,9},{11,10},{12... | collective-permute-start | bytes 98312 | tf_op jit(solution)/shard_map/ppermute | solution.py:367

commit v2 on v1

v2 whole, which is shorter than its diff:
```python
import functools
import math

import jax
import jax.numpy as jnp
from jax import lax
from jax.experimental import pallas as pl
from jax.experimental.pallas import tpu as pltpu
from jax.sharding import PartitionSpec as P

FR = 32
LANES = 128
PACK = 4
VMEM_LIMIT = 50 * 1024 * 1024


def swap_slots(values):
    slot = lax.broadcasted_iota(jnp.int32, values[0].shape, 1) // 32
    upper = slot >= 2
    odd = slot % 2 == 1
    a, b, c, d = values
    a, c = jnp.where(upper, pltpu.roll(c, 64, 1), a), jnp.where(upper, c, pltpu.roll(a, 64, 1))
    b, d = jnp.where(upper, pltpu.roll(d, 64, 1), b), jnp.where(upper, d, pltpu.roll(b, 64, 1))
    a, b = jnp.where(odd, pltpu.roll(b, 32, 1), a), jnp.where(odd, b, pltpu.roll(a, 96, 1))
    c, d = jnp.where(odd, pltpu.roll(d, 32, 1), c), jnp.where(odd, d, pltpu.roll(c, 96, 1))
    return [a, b, c, d]


def make_plan(slots, groups, faces_ref, type_ref, count_ref, table_ref):
    kind_at = groups * PACK * 6
    for i in range(kind_at):
        table_ref[i] = 0
    count = count_ref[0]
    kinds = 4

    def tally(slot, sizes):
        live = slot < count
        return tuple(
            size + (live & (type_ref[slot] == kind)).astype(jnp.int32)
            for kind, size in enumerate(sizes)
        )

    sizes = lax.fori_loop(0, slots, tally, (jnp.int32(0),) * kinds)
    firsts, place = [], jnp.int32(0)
    for size in sizes:
        firsts.append(place)
        place = place + (size + PACK - 1) // PACK * PACK
    table_ref[kind_at + groups] = place // PACK

    def put(slot, nexts):
        kind = type_ref[slot]
        position = nexts[kinds - 1]
        for other in range(kinds - 1):
            position = jnp.where(kind == other, nexts[other], position)
        table_ref[kind_at + position // PACK] = kind
        for f in range(6):
            table_ref[position * 6 + f] = faces_ref[f, slot]
        return tuple(at + (kind == other).astype(jnp.int32) for other, at in enumerate(nexts))

    lax.fori_loop(0, count, put, tuple(firsts))


def sides(side_ref, rows, cols):
    odd_row, odd_col = side_ref[0] == 1, side_ref[1] == 1
    first_row = jnp.where(odd_row, 0, rows - 1)
    first_col = jnp.where(odd_col, 0, cols - 1)
    return (first_row, rows - 1 - first_row), (first_col, cols - 1 - first_col)


def beyond(edge, length):
    return jnp.where(edge == 0, 0, length + 1)


def apply_kernel(flat, dims, groups, *refs):
    rows, cols, dofs = dims
    edge = 6 * dofs
    width = cols + 2
    if flat:
        side_ref, faces_ref, type_ref, count_ref, own_ref, *refs = refs
    else:
        side_ref, table_ref, own_ref, *refs = refs
    row_refs, col_refs, jac_hbm, t_ref = refs[0:2], refs[2:4], refs[4], refs[5]
    to_rows, to_cols = refs[6:8], refs[8:10]
    if flat:
        v_ref, table_ref = refs[10:12]
    field, totals, x_ref, y_ref, jac, sem = refs[-6:]
    fetch = pltpu.make_async_copy(jac_hbm, jac, sem)
    fetch.start()
    if flat:
        make_plan(type_ref.shape[0], groups, faces_ref, type_ref, count_ref, table_ref)
    row_edges, col_edges = sides(side_ref, rows, cols)
    out_rows = [beyond(r, rows) for r in row_edges]
    out_cols = [beyond(c, cols) for c in col_edges]

    def cell_rows(cell):
        if isinstance(cell, int):
            return slice(cell * FR, (cell + 1) * FR)
        return pl.ds(pl.multiple_of(cell * FR, FR), FR)

    zero = jnp.zeros((FR, LANES), jnp.float32)
    field[0:FR, :] = zero
    if flat:
        sources = [(own_ref.at[r], (r + 1) * width + 1, 1, cols) for r in range(rows)]
        sources += [(row_refs[n], out_rows[n] * width + 1, 1, cols) for n in range(2)]
        sources += [(col_refs[n], width + out_cols[n], width, rows) for n in range(2)]
        for ref, first, step, many in sources:
            length = ref.shape[1]
            for a in range(FR):
                high = min(LANES * (a + 1), length)
                tile = ref[:, LANES * a : high].astype(jnp.float32)
                if high < LANES * (a + 1):
                    gap = jnp.zeros((many, LANES * (a + 1) - high), jnp.float32)
                    tile = jnp.concatenate([tile, gap], axis=1)
                field[pl.ds(first * FR + a, many, stride=step * FR), :] = tile
        for r in range(rows):
            for c in range(cols):
                v_ref[r * cols + c] = field[cell_rows((r + 1) * width + c + 1), :].astype(jnp.bfloat16)
    else:
        for r in range(rows):
            for c in range(cols):
                field[cell_rows((r + 1) * width + c + 1), :] = own_ref[r * cols + c].astype(jnp.float32)
        for n in range(2):
            for c in range(cols):
                field[cell_rows(out_rows[n] * width + c + 1), :] = row_refs[n][c].astype(jnp.float32)
            for r in range(rows):
                field[cell_rows((r + 1) * width + out_cols[n]), :] = col_refs[n][r].astype(jnp.float32)
    for cell in range((rows + 2) * width):
        totals[cell_rows(cell), :] = zero
    y_ref[edge // 8 * 8 :, :] = jnp.zeros((y_ref.shape[0] - edge // 8 * 8, LANES), jnp.float32)
    fetch.wait()

    def group(g, carry):
        kind = table_ref[groups * PACK * 6 + g]
        cells = [[table_ref[(g * PACK + s) * 6 + f] for s in range(PACK)] for f in range(6)]
        for f in range(6):
            spread = swap_slots([field[cell_rows(cells[f][s]), :] for s in range(PACK)])
            for b in range(4):
                x_ref[pl.ds(f * dofs + b, FR, stride=4), :] = spread[b]
        y_ref[0:edge, :] = jnp.dot(
            jac[kind], x_ref[0:edge, :].astype(jnp.bfloat16), preferred_element_type=jnp.float32
        )
        for f in range(6):
            back = swap_slots([y_ref[pl.ds(f * dofs + b, FR, stride=4), :] for b in range(4)])
            for s in range(PACK):
                at = cell_rows(cells[f][s])
                totals[at, :] = totals[at, :] + back[s]
        return carry

    lax.fori_loop(0, table_ref[groups * PACK * 6 + groups], group, jnp.int32(0))

    for r in range(rows):
        for c in range(cols):
            t_ref[r * cols + c] = totals[cell_rows((r + 1) * width + c + 1), :]
    for n in range(2):
        for c in range(cols):
            to_rows[n][c] = totals[cell_rows(out_rows[n] * width + c + 1), :].astype(jnp.bfloat16)
        for r in range(rows):
            to_cols[n][r] = totals[cell_rows((r + 1) * width + out_cols[n]), :].astype(jnp.bfloat16)


def combine(dims, side_ref, t_ref, rims, hold):
    rows, cols, dofs = dims
    row_edges, col_edges = sides(side_ref, rows, cols)
    for cell in range(rows * cols):
        hold[cell] = t_ref[cell]
    for n in range(2):
        for c in range(cols):
            cell = row_edges[n] * cols + c
            hold[cell] = hold[cell] + rims[n][c].astype(jnp.float32)
        for r in range(rows):
            cell = r * cols + col_edges[n]
            hold[cell] = hold[cell] + rims[2 + n][r].astype(jnp.float32)
    return row_edges, col_edges


def middle_kernel(dims, side_ref, t_ref, a_ref, b_ref, c_ref, d_ref, w_ref, *refs):
    rows, cols, dofs = dims
    hold = refs[-1]
    to_rows, to_cols = refs[0:2], refs[2:4]
    row_edges, col_edges = combine(dims, side_ref, t_ref, (a_ref, b_ref, c_ref, d_ref), hold)
    row = lax.broadcasted_iota(jnp.int32, (FR, LANES), 0)
    slot = lax.broadcasted_iota(jnp.int32, (FR, LANES), 1) // 32
    real = row * 4 + slot < dofs
    for cell in range(rows * cols):
        w_ref[cell] = jnp.where(real, hold[cell], 0.0).astype(jnp.bfloat16)
    for n in range(2):
        for c in range(cols):
            to_rows[n][c] = w_ref[row_edges[n] * cols + c]
        for r in range(rows):
            to_cols[n][r] = w_ref[r * cols + col_edges[n]]


def mail_kernel(dims, v_ref, w_ref, ids_ref, mail_ref):
    rows, cols, dofs = dims
    v = v_ref[...].reshape(rows * cols * FR, LANES)
    w = w_ref[...].reshape(rows * cols * FR, LANES)
    square = lax.dot_general(v, w, (((0,), (0,)), ((), ())), preferred_element_type=jnp.float32)
    side = lax.broadcasted_iota(jnp.int32, (LANES, LANES), 1) // 32
    diagonal = lax.broadcasted_iota(jnp.int32, (LANES, LANES), 0) // 32 == side
    square = jnp.where(diagonal, square, 0.0)
    local = square[0:32] + square[32:64] + square[64:96] + square[96:128]
    local = local + pltpu.roll(local, 64, 1)
    local = (local + pltpu.roll(local, 32, 1)) * (1.0 / math.sqrt(rows * cols * dofs))
    local = jnp.where(diagonal, jnp.concatenate([local] * 4, axis=0), 0.0)
    owners = mail_ref.shape[0]
    ids = ids_ref[...]
    owner = lax.broadcasted_iota(jnp.int32, (owners, LANES), 0)
    vertex = 4 * owner + lax.broadcasted_iota(jnp.int32, (owners, LANES), 1) // 32
    place = (vertex == ids).astype(jnp.bfloat16)
    high = local.astype(jnp.bfloat16)
    low = (local - high.astype(jnp.float32)).astype(jnp.bfloat16)
    mail_ref[:, 0, :] = jnp.dot(place, high, preferred_element_type=jnp.float32) + jnp.dot(
        place, low, preferred_element_type=jnp.float32
    )
    mail_ref[:, 1, :] = jnp.broadcast_to(ids.astype(jnp.float32), (owners, LANES))


def expand_kernel(mail_ref, out_ref, turned_ref, flat_ref, hot_ref):
    senders = mail_ref.shape[0]
    vertices = out_ref.shape[2]
    ids = mail_ref[:, 1, :]
    vertex = lax.broadcasted_iota(jnp.int32, (senders, vertices), 1).astype(jnp.float32)
    turned_ref[...] = mail_ref[:, 0, :].T
    for s in range(32):
        part = slice(s * senders, (s + 1) * senders)
        flat_ref[:, part] = turned_ref[pl.ds(s, 4, stride=32), :]
        hot_ref[part, :] = (ids[:, s : s + 1] == vertex).astype(jnp.bfloat16)
    values = flat_ref[...]
    high = values.astype(jnp.bfloat16).astype(jnp.float32)
    both = jnp.concatenate([high, values - high], axis=0).astype(jnp.bfloat16)
    wide = jnp.dot(both, hot_ref[...], preferred_element_type=jnp.float32)
    total = wide[0:4] + wide[4:8]
    for j in range(out_ref.shape[0]):
        out_ref[j] = total


def last_kernel(dims, side_ref, t_ref, a_ref, b_ref, c_ref, d_ref, out_ref, sums, hold):
    rows, cols, dofs = dims
    length = out_ref.shape[2]
    combine(dims, side_ref, t_ref, (a_ref, b_ref, c_ref, d_ref), sums)
    for r in range(rows):
        for c in range(cols):
            hold[pl.ds(r * FR * cols + c, FR, stride=cols), :] = sums[r * cols + c]
    for r in range(rows):
        for a in range(FR):
            high = min(LANES * (a + 1), length)
            start = (r * FR + a) * cols
            tile = hold[start : start + cols, 0 : high - LANES * a]
            out_ref[r, :, LANES * a : high] = tile.astype(jnp.bfloat16)


VM = pl.BlockSpec(memory_space=pltpu.VMEM)
SM = pl.BlockSpec(memory_space=pltpu.SMEM)
HBM = pl.BlockSpec(memory_space=pltpu.HBM)


def struct(shape, dtype=jnp.bfloat16):
    return jax.ShapeDtypeStruct(shape, dtype)


def rim_structs(rows, cols):
    return (
        struct((cols, FR, LANES)),
        struct((cols, FR, LANES)),
        struct((rows, FR, LANES)),
        struct((rows, FR, LANES)),
    )


def apply(flat, dims, side, scalars, own, rims, jacobians):
    rows, cols, dofs = dims
    cells = rows * cols
    slots = scalars[1].shape[0] if flat else 0
    groups = (slots + 3 * 4) // PACK if flat else (scalars[0].shape[0] - 1) // (PACK * 6 + 1)
    out = (struct((cells, FR, LANES), jnp.float32),) + rim_structs(rows, cols)
    places = (VM,) * 5
    if flat:
        out += (struct((cells, FR, LANES)), struct((groups * (PACK * 6 + 1) + 1,), jnp.int32))
        places += (VM, SM)
    area = (rows + 2) * (cols + 2) * FR
    flops = 2**34
    moved = jacobians.size * 2 + cells * FR * LANES * 6
    return pl.pallas_call(
        functools.partial(apply_kernel, flat, dims, groups),
        out_shape=out,
        in_specs=[SM] * (1 + len(scalars)) + [VM] * 5 + [HBM],
        out_specs=places,
        scratch_shapes=[
            pltpu.VMEM((area, LANES), jnp.float32),
            pltpu.VMEM((area, LANES), jnp.float32),
            pltpu.VMEM((6 * dofs + 10, LANES), jnp.float32),
            pltpu.VMEM((6 * dofs + 10, LANES), jnp.float32),
            pltpu.VMEM(jacobians.shape, jnp.bfloat16),
            pltpu.SemaphoreType.DMA,
        ],
        compiler_params=pltpu.CompilerParams(vmem_limit_bytes=VMEM_LIMIT),
        cost_estimate=pl.CostEstimate(flops=flops, bytes_accessed=moved, transcendentals=0),
        name="apply_flat" if flat else "apply_tiles",
    )(side, *scalars, own, *rims, jacobians)


def middle(dims, side, total, rims):
    rows, cols, dofs = dims
    cells = rows * cols
    return pl.pallas_call(
        functools.partial(middle_kernel, dims),
        out_shape=(struct((cells, FR, LANES)),) + rim_structs(rows, cols),
        in_specs=[SM] + [VM] * 5,
        out_specs=(VM,) * 5,
        scratch_shapes=[pltpu.VMEM((cells, FR, LANES), jnp.float32)],
        compiler_params=pltpu.CompilerParams(vmem_limit_bytes=VMEM_LIMIT),
        name="middle",
    )(side, total, *rims)


def make_mail(dims, tiles, first, ids, owners):
    return pl.pallas_call(
        functools.partial(mail_kernel, dims),
        out_shape=struct((owners, 2, LANES), jnp.float32),
        in_specs=[VM] * 3,
        out_specs=VM,
        compiler_params=pltpu.CompilerParams(vmem_limit_bytes=VMEM_LIMIT),
        cost_estimate=pl.CostEstimate(flops=2**30, bytes_accessed=2**20, transcendentals=0),
        name="mail",
    )(tiles, first, ids)


def expand(mail, narrow, vertex_total):
    owned = vertex_total // mail.shape[0]
    return pl.pallas_call(
        expand_kernel,
        out_shape=struct((narrow, owned, vertex_total), jnp.float32),
        in_specs=[VM],
        out_specs=VM,
        scratch_shapes=[
            pltpu.VMEM((LANES, mail.shape[0]), jnp.float32),
            pltpu.VMEM((owned, 32 * mail.shape[0]), jnp.float32),
            pltpu.VMEM((32 * mail.shape[0], vertex_total), jnp.bfloat16),
        ],
        compiler_params=pltpu.CompilerParams(vmem_limit_bytes=VMEM_LIMIT),
        cost_estimate=pl.CostEstimate(flops=2**30, bytes_accessed=2**18, transcendentals=0),
        name="expand",
    )(mail)


def last(dims, side, total, rims, length):
    rows, cols, dofs = dims
    cells = rows * cols
    return pl.pallas_call(
        functools.partial(last_kernel, dims),
        out_shape=struct((rows, cols, length)),
        in_specs=[SM] + [VM] * 5,
        out_specs=VM,
        scratch_shapes=[
            pltpu.VMEM((cells, FR, LANES), jnp.float32),
            pltpu.VMEM((cells * FR, LANES), jnp.float32),
        ],
        compiler_params=pltpu.CompilerParams(vmem_limit_bytes=VMEM_LIMIT),
        cost_estimate=pl.CostEstimate(flops=2**34, bytes_accessed=2**20, transcendentals=0),
        name="last",
    )(side, total, *rims)


def exchange(row_first, row_second, col_first, col_second):
    def swap(value, axis, start):
        peers = lax.axis_size(axis)
        pairs = [(i, i + 1) for i in range(start, peers - 1, 2)]
        return lax.ppermute(value, axis, pairs + [(j, i) for i, j in pairs])

    second = swap(row_second, "sub", 1)
    return (
        swap(row_first, "sub", 0),
        second,
        swap(col_first, "slab", 0),
        swap(col_second, "slab", 1),
    )


def body(coarse_basis, jacobians, element_faces, element_type, element_count, vertex_ids):
    rows, cols, length = coarse_basis.shape
    dofs = jacobians.shape[1] // 6
    dims = (rows, cols, dofs)
    owners, narrow = lax.axis_size("sub"), lax.axis_size("slab")
    ids = jnp.tile(vertex_ids, (1, 4))
    odd_row, odd_col = lax.axis_index("sub") & 1, lax.axis_index("slab") & 1
    side = jnp.stack([odd_row, odd_col])

    ends = coarse_basis[0], coarse_basis[rows - 1], coarse_basis[:, 0], coarse_basis[:, cols - 1]
    rims = exchange(
        jnp.where(odd_row == 1, ends[0], ends[1]),
        jnp.where(odd_row == 1, ends[1], ends[0]),
        jnp.where(odd_col == 1, ends[2], ends[3]),
        jnp.where(odd_col == 1, ends[3], ends[2]),
    )
    scalars = (element_faces.T, element_type, element_count)
    total, *sent, tiles, table = apply(True, dims, side, scalars, coarse_basis, rims, jacobians)
    first, *halo = middle(dims, side, total, exchange(*sent))
    rims = exchange(*halo)
    tiles, unused = lax.optimization_barrier((tiles, rims[2]))
    mail = lax.all_to_all(make_mail(dims, tiles, first, ids, owners), "sub", 0, 0)
    total, *sent = apply(False, dims, side, (table,), first, rims, jacobians)
    rims = exchange(*sent)
    mail, unused = lax.optimization_barrier((mail, rims[2]))
    parts = lax.all_to_all(expand(mail, narrow, rows * owners), "slab", 0, 0)
    second_image = last(dims, side, total, rims, length)
    return second_image, parts.sum(0)


def solution(mesh):
    return jax.shard_map(
        body,
        mesh=mesh,
        in_specs=(
            P("sub", "slab", None),
            P(),
            P(("sub", "slab"), None),
            P(("sub", "slab")),
            P(("sub", "slab")),
            P(("sub", "slab"), None),
        ),
        out_specs=(P("sub", "slab", None), P("sub", None)),
        check_vma=False,
    )
```

time: 160 us -> 133 us (0.83)
  the two profiles are of different devices: /device:TPU:127 before, /device:TPU:62 now
where the time goes in v2:
time: 133 us; the launch traced here: 132 us
  starting transfers between devices  87.4 us (66%)
  Pallas kernels  27.9 us (21%)
  waiting for transfers between devices  7.65 us (6%)
  local copies, waits for them, and re-layouts  6.24 us (5%)
  other arithmetic  1.68 us (1%)
  between operations  1.63 us (1%)
    ppermute x16, starting transfers between devices, swap(): return lax.ppermute(value, axis, pairs + [(j, i) for i, j in pairs])  60.3 us
    all_to_all x1, starting transfers between devices, body(): lax.all_to_all(make_mail(dims, tiles, first, ids, owners), 'sub', 0, 0)  22.7 us
    pallas_call x2, Pallas kernels, apply(): pl.pallas_call(functools.partial(apply_kernel, flat, dims, groups), out_s...  19.2 us
    pallas_call x1, Pallas kernels, expand(): pl.pallas_call(expand_kernel, out_shape=struct((narrow, owned, vertex_tot...  5.24 us
    unnamed x9, local copies, waits for them, and re-layouts  5.02 us
    all_to_all x1, waiting for transfers between devices, body(): parts = lax.all_to_all(expand(mail, narrow, rows * owners), 'slab', 0, 0)  4.44 us
    all_to_all x1, starting transfers between devices, body(): parts = lax.all_to_all(expand(mail, narrow, rows * owners), 'slab', 0, 0)  4.4 us
    ppermute x16, waiting for transfers between devices, swap(): return lax.ppermute(value, axis, pairs + [(j, i) for i, j in pairs])  3.21 us
  transfers between devices with their start and end apart: 18, of which 3 were waited for; matrix products, arithmetic and copies ran while one was open for 5% of the time, Pallas kernels for 13%

profile of v2, /device:TPU:62, one launch (start us, length us, event | category | flops | bytes accessed | tf_op | source)
XLA Modules:
  0.0 132.5 jit_solution(5184787849535560984)
XLA Ops:
  0.6 1.1 fusion
  1.9 1.9 %collective-permute-start.2 = (bf16[4,4000]{1,0:T(4,128)(2,1)S(1)}, bf16[4,4000]{1,0:T(4,128)(2,1)S(1)}, u32[]{:S(2)}, u32[]{:S(2)}) collective-permute-start(bf16[4,4000]{1,0:T(4,128)(2,1)S(1)} %get-tuple-element.45), channel_id=1, source_target_pairs={{0,1},{2,3},{4,5},{6,7},{1,0},{3,2},{5,4},{7,6},{8,9},{10,11},{12,... | collective-permute-start | bytes 96008 | tf_op jit(solution)/shard_map/ppermute | solution.py:368
  4.5 0.9 select_bitcast_fusion
  5.4 2.9 %collective-permute-start = (bf16[8,4000]{1,0:T(8,128)(2,1)S(1)}, bf16[8,4000]{1,0:T(8,128)(2,1)S(1)}, u32[]{:S(2)}, u32[]{:S(2)}) collective-permute-start(bf16[8,4000]{1,0:T(8,128)(2,1)S(1)} %get-tuple-element.43), channel_id=1, source_target_pairs={{0,8},{16,24},{32,40},{48,56},{64,72},{80,88},{96,104},{112,120},{... | collective-permute-start | bytes 192008 | tf_op jit(solution)/shard_map/ppermute | solution.py:368
  8.3 10.7 %collective-permute-start.1 = (bf16[8,4000]{1,0:T(8,128)(2,1)S(1)}, bf16[8,4000]{1,0:T(8,128)(2,1)S(1)}, u32[]{:S(2)}, u32[]{:S(2)}) collective-permute-start(bf16[8,4000]{1,0:T(8,128)(2,1)S(1)} %get-tuple-element.42), channel_id=1, source_target_pairs={{8,16},{24,32},{40,48},{56,64},{72,80},{88,96},{104,112},{120,128}... | collective-permute-start | bytes 192008 | tf_op jit(solution)/shard_map/ppermute | solution.py:368
  19.1 5.0 %copy.10.refs_9_.refs_7_ = bf16[4,750,750]{2,1,0:T(8,128)(2,1)} copy(bf16[4,750,750]{2,0,1:T(4,128)(2,1)} %param.7) | data formatting | bytes 9000000 | tf_op args[1]
  24.8 9.9 %apply_flat.1 = (f32[32,32,128]{2,1,0:T(8,128)S(1)}, bf16[8,32,128]{2,1,0:T(8,128)(2,1)S(1)}, bf16[8,32,128]{2,1,0:T(8,128)(2,1)S(1)}, bf16[4,32,128]{2,1,0:T(8,...) custom-call(s32[2]{0:T(128)S(1)} %pad_add_fusion.refs_0_.side_ref, ...), custom_call_target="tpu_custom_call" | custom-call | flops 17179869184 | bytes 5286432 | tf_op jit(solution)/shard_map/apply_flat/pallas_call | solution.py:283
  34.7 1.9 %collective-permute-start.4 = (bf16[8,32,128]{2,1,0:T(8,128)(2,1)S(1)}, bf16[8,32,128]{2,1,0:T(8,128)(2,1)S(1)}, u32[]{:S(2)}, u32[]{:S(2)}) collective-permute-start(bf16[8,32,128]{2,1,0:T(8,128)(2,1)S(1)} %get-tuple-element.23), channel_id=1, source_target_pairs={{0,8},{16,24},{32,40},{48,56},{64,72},{80,88},{96,104},{112,120},{... | collective-permute-start | bytes 196616 | tf_op jit(solution)/shard_map/ppermute | solution.py:368
  36.7 8.5 %collective-permute-start.5 = (bf16[8,32,128]{2,1,0:T(8,128)(2,1)S(1)}, bf16[8,32,128]{2,1,0:T(8,128)(2,1)S(1)}, u32[]{:S(2)}, u32[]{:S(2)}) collective-permute-start(bf16[8,32,128]{2,1,0:T(8,128)(2,1)S(1)} %get-tuple-element.24), channel_id=1, source_target_pairs={{8,16},{24,32},{40,48},{56,64},{72,80},{88,96},{104,112},{120,128}... | collective-permute-start | bytes 196616 | tf_op jit(solution)/shard_map/ppermute | solution.py:368
  45.2 1.9 %collective-permute-start.6 = (bf16[4,32,128]{2,1,0:T(8,128)(2,1)S(1)}, bf16[4,32,128]{2,1,0:T(8,128)(2,1)S(1)}, u32[]{:S(2)}, u32[]{:S(2)}) collective-permute-start(bf16[4,32,128]{2,1,0:T(8,128)(2,1)S(1)} %get-tuple-element.25), channel_id=1, source_target_pairs={{0,1},{2,3},{4,5},{6,7},{1,0},{3,2},{5,4},{7,6},{8,9},{10,11},{12,... | collective-permute-start | bytes 98312 | tf_op jit(solution)/shard_map/ppermute | solution.py:368
  48.3 2.7 %collective-permute-done.5.b_ref = bf16[8,32,128]{2,1,0:T(8,128)(2,1)S(1)} collective-permute-done((bf16[8,32,128]{2,1,0:T(8,128)(2,1)S(1)}, bf16[8,32,128]{2,1,0:T(8,128)(2,1)S(1)}, u32[]{:S(2)}, u32[]{:S(2)}) %collective-permute-start.5) | collective-permute-done | bytes 65568 | tf_op jit(solution)/shard_map/ppermute | solution.py:368
  51.6 6.4 %collective-permute-start.10 = (bf16[4,32,128]{2,1,0:T(8,128)(2,1)S(1)}, bf16[4,32,128]{2,1,0:T(8,128)(2,1)S(1)}, u32[]{:S(2)}, u32[]{:S(2)}) collective-permute-start(bf16[4,32,128]{2,1,0:T(8,128)(2,1)S(1)} %get-tuple-element.30), channel_id=1, source_target_pairs={{0,1},{2,3},{4,5},{6,7},{1,0},{3,2},{5,4},{7,6},{8,9},{10,11},{12,... | collective-permute-start | bytes 98312 | tf_op jit(solution)/shard_map/ppermute | solution.py:368
  58.1 1.9 %collective-permute-start.8 = (bf16[8,32,128]{2,1,0:T(8,128)(2,1)S(1)}, bf16[8,32,128]{2,1,0:T(8,128)(2,1)S(1)}, u32[]{:S(2)}, u32[]{:S(2)}) collective-permute-start(bf16[8,32,128]{2,1,0:T(8,128)(2,1)S(1)} %get-tuple-element.28), channel_id=1, source_target_pairs={{0,8},{16,24},{32,40},{48,56},{64,72},{80,88},{96,104},{112,120},{... | collective-permute-start | bytes 196616 | tf_op jit(solution)/shard_map/ppermute | solution.py:368
  60.0 6.1 %collective-permute-start.9 = (bf16[8,32,128]{2,1,0:T(8,128)(2,1)S(1)}, bf16[8,32,128]{2,1,0:T(8,128)(2,1)S(1)}, u32[]{:S(2)}, u32[]{:S(2)}) collective-permute-start(bf16[8,32,128]{2,1,0:T(8,128)(2,1)S(1)} %get-tuple-element.29), channel_id=1, source_target_pairs={{8,16},{24,32},{40,48},{56,64},{72,80},{88,96},{104,112},{120,128}... | collective-permute-start | bytes 196616 | tf_op jit(solution)/shard_map/ppermute | solution.py:368
  66.8 1.3 mail.1
  68.0 22.7 %all-to-all-start = ((f32[128,2,128]{2,1,0:T(2,128)}), f32[128,2,128]{2,1,0:T(2,128)S(1)}, u32[]{:S(2)}, u32[]{:S(2)}) async-start(f32[128,2,128]{2,1,0:T(2,128)} %mail.1), calls=%async_computation | async-start | bytes 262144 | tf_op jit(solution)/shard_map/all_to_all | solution.py:400
  90.8 9.3 %apply_tiles.1 = (f32[32,32,128]{2,1,0:T(8,128)S(1)}, bf16[8,32,128]{2,1,0:T(8,128)(2,1)S(1)}, bf16[8,32,128]{2,1,0:T(8,128)(2,1)S(1)}, bf16[4,32,128]{2,1,0:T(8,128)(2,1)S(1)}, bf16[4,32,128]{2,1,0:T(8,128)(2,1)S(1)}) custom-call(s32[2]{0:T(128)S(1)} %pad_add_fusion.refs_0_.side_ref, s32[201]{0:T(256)S(1)} %get-tuple-element.21.refs_1_, ...), custom_call_target="tpu_custom_call" | custom-call | flops 17179869184 | bytes 5286432 | tf_op jit(solution)/shard_map/apply_tiles/pallas_call | solution.py:283
  100.1 1.9 %collective-permute-start.14 = (bf16[4,32,128]{2,1,0:T(8,128)(2,1)S(1)}, bf16[4,32,128]{2,1,0:T(8,128)(2,1)S(1)}, u32[]{:S(2)}, u32[]{:S(2)}) collective-permute-start(bf16[4,32,128]{2,1,0:T(8,128)(2,1)S(1)} %get-tuple-element.35), channel_id=1, source_target_pairs={{0,1},{2,3},{4,5},{6,7},{1,0},{3,2},{5,4},{7,6},{8,9},{10,11},{12,... | collective-permute-start | bytes 98312 | tf_op jit(solution)/shard_map/ppermute | solution.py:368
  102.0 5.7 %collective-permute-start.12 = (bf16[8,32,128]{2,1,0:T(8,128)(2,1)S(1)}, bf16[8,32,128]{2,1,0:T(8,128)(2,1)S(1)}, u32[]{:S(2)}, u32[]{:S(2)}) collective-permute-start(bf16[8,32,128]{2,1,0:T(8,128)(2,1)S(1)} %get-tuple-element.33), channel_id=1, source_target_pairs={{0,8},{16,24},{32,40},{48,56},{64,72},{80,88},{96,104},{112,120},{... | collective-permute-start | bytes 196616 | tf_op jit(solution)/shard_map/ppermute | solution.py:368
  107.7 7.9 %collective-permute-start.13 = (bf16[8,32,128]{2,1,0:T(8,128)(2,1)S(1)}, bf16[8,32,128]{2,1,0:T(8,128)(2,1)S(1)}, u32[]{:S(2)}, u32[]{:S(2)}) collective-permute-start(bf16[8,32,128]{2,1,0:T(8,128)(2,1)S(1)} %get-tuple-element.34), channel_id=1, source_target_pairs={{8,16},{24,32},{40,48},{56,64},{72,80},{88,96},{104,112},{120,128}... | collective-permute-start | bytes 196616 | tf_op jit(solution)/shard_map/ppermute | solution.py:368
  116.3 5.2 %expand.1 = f32[8,4,512]{2,1,0:T(4,128)} custom-call(f32[128,2,128]{2,1,0:T(2,128)S(1)} %all-to-all-done.mail_ref), custom_call_target="tpu_custom_call" | custom-call | flops 1073741824 | bytes 262144 | tf_op jit(solution)/shard_map/expand/pallas_call | solution.py:330
  121.6 4.4 %all-to-all-start.1 = ((f32[8,4,512]{2,1,0:T(4,128)}), f32[8,4,512]{2,1,0:T(4,128)S(1)}, u32[]{:S(2)}, u32[]{:S(2)}) async-start(f32[8,4,512]{2,1,0:T(4,128)} %expand.1), calls=%async_computation.1 | async-start | bytes 131072 | tf_op jit(solution)/shard_map/all_to_all | solution.py:404
  126.0 1.5 %last.1 = bf16[4,8,4000]{2,1,0:T(8,128)(2,1)} custom-call(s32[2]{0:T(128)S(1)} %pad_add_fusion.refs_0_.side_ref, f32[32,32,128]{2,1,0:T(8,128)S(1)} %get-tuple-element.32.t_ref, bf16[8,32,128]{2,1,0:T(8,128)(2,1)S(1)} %collective-permute-done.12.a_ref, bf16[8,32,128]{2,1,0:T(8,128)(2,1)S(1)} %collective-permute-done.13.b_ref, ...), custom_call_target="tpu_custom_call" | custom-call | flops 17179869184 | bytes 1048576 | tf_op jit(solution)/shard_map/last/pallas_call | solution.py:349
  127.4 4.4 %all-to-all-done.1 = f32[8,4,512]{2,1,0:T(4,128)S(1)} async-done(((f32[8,4,512]{2,1,0:T(4,128)}), f32[8,4,512]{2,1,0:T(4,128)S(1)}, u32[]{:S(2)}, u32[]{:S(2)}) %all-to-all-start.1) | async-done | bytes 65568 | tf_op jit(solution)/shard_map/all_to_all | solution.py:404
  (34 shorter events, 4.8 us)
Async XLA Ops:
  1.9 22.8 %collective-permute-start.2 = (bf16[4,4000]{1,0:T(4,128)(2,1)S(1)}, bf16[4,4000]{1,0:T(4,128)(2,1)S(1)}, u32[]{:S(2)}, u32[]{:S(2)}) collective-permute-start(bf16[4,4000]{1,0:T(4,128)(2,1)S(1)} %get-tuple-element.45), channel_id=1, source_target_pairs={{0,1},{2,3},{4,5},{6,7},{1,0},{3,2},{5,4},{7,6},{8,9},{10,11},{12,... | collective-permute-start | bytes 96008 | tf_op jit(solution)/shard_map/ppermute | solution.py:368
  3.8 20.9 %collective-permute-start.3 = (bf16[4,4000]{1,0:T(4,128)(2,1)S(1)}, bf16[4,4000]{1,0:T(4,128)(2,1)S(1)}, u32[]{:S(2)}, u32[]{:S(2)}) collective-permute-start(bf16[4,4000]{1,0:T(4,128)(2,1)S(1)} %get-tuple-element.44), channel_id=1, source_target_pairs={{1,2},{3,4},{5,6},{2,1},{4,3},{6,5},{9,10},{11,12},{13,14},{10,9},... | collective-permute-start | bytes 96008 | tf_op jit(solution)/shard_map/ppermute | solution.py:368
  5.4 19.4 %copy-start = (bf16[4,8,4000]{2,1,0:T(8,128)(2,1)S(1)}, bf16[4,8,4000]{2,1,0:T(8,128)(2,1)}, u32[]{:S(2)}) copy-start(bf16[4,8,4000]{2,1,0:T(8,128)(2,1)} %refs_4_.1) | copy-start | bytes 768004
  5.4 19.4 %copy-start.1 = (s32[20,6]{0,1:T(8,128)S(1)}, s32[20,6]{0,1:T(8,128)}, u32[]{:S(2)}) copy-start(s32[20,6]{0,1:T(8,128)} %param.8) | copy-start | bytes 1444
  5.4 19.4 %copy-start.2 = (s32[20]{0:T(128)S(1)}, s32[20]{0:T(128)}, u32[]{:S(2)}) copy-start(s32[20]{0:T(128)} %refs_2_.1) | copy-start | bytes 244
  5.4 19.3 %collective-permute-start = (bf16[8,4000]{1,0:T(8,128)(2,1)S(1)}, bf16[8,4000]{1,0:T(8,128)(2,1)S(1)}, u32[]{:S(2)}, u32[]{:S(2)}) collective-permute-start(bf16[8,4000]{1,0:T(8,128)(2,1)S(1)} %get-tuple-element.43), channel_id=1, source_target_pairs={{0,8},{16,24},{32,40},{48,56},{64,72},{80,88},{96,104},{112,120},{... | collective-permute-start | bytes 192008 | tf_op jit(solution)/shard_map/ppermute | solution.py:368
  8.3 16.5 %collective-permute-start.1 = (bf16[8,4000]{1,0:T(8,128)(2,1)S(1)}, bf16[8,4000]{1,0:T(8,128)(2,1)S(1)}, u32[]{:S(2)}, u32[]{:S(2)}) collective-permute-start(bf16[8,4000]{1,0:T(8,128)(2,1)S(1)} %get-tuple-element.42), channel_id=1, source_target_pairs={{8,16},{24,32},{40,48},{56,64},{72,80},{88,96},{104,112},{120,128}... | collective-permute-start | bytes 192008 | tf_op jit(solution)/shard_map/ppermute | solution.py:368
  24.8 33.2 %copy-start.3 = (s32[1,32]{1,0:T(1,128)S(1)}, s32[1,32]{1,0:T(1,128)}, u32[]{:S(2)}) copy-start(s32[1,32]{1,0:T(1,128)} %param.11) | copy-start | bytes 388
  34.7 13.5 %collective-permute-start.4 = (bf16[8,32,128]{2,1,0:T(8,128)(2,1)S(1)}, bf16[8,32,128]{2,1,0:T(8,128)(2,1)S(1)}, u32[]{:S(2)}, u32[]{:S(2)}) collective-permute-start(bf16[8,32,128]{2,1,0:T(8,128)(2,1)S(1)} %get-tuple-element.23), channel_id=1, source_target_pairs={{0,8},{16,24},{32,40},{48,56},{64,72},{80,88},{96,104},{112,120},{... | collective-permute-start | bytes 196616 | tf_op jit(solution)/shard_map/ppermute | solution.py:368
  36.7 14.3 %collective-permute-start.5 = (bf16[8,32,128]{2,1,0:T(8,128)(2,1)S(1)}, bf16[8,32,128]{2,1,0:T(8,128)(2,1)S(1)}, u32[]{:S(2)}, u32[]{:S(2)}) collective-permute-start(bf16[8,32,128]{2,1,0:T(8,128)(2,1)S(1)} %get-tuple-element.24), channel_id=1, source_target_pairs={{8,16},{24,32},{40,48},{56,64},{72,80},{88,96},{104,112},{120,128}... | collective-permute-start | bytes 196616 | tf_op jit(solution)/shard_map/ppermute | solution.py:368
  45.2 3.1 %collective-permute-start.6 = (bf16[4,32,128]{2,1,0:T(8,128)(2,1)S(1)}, bf16[4,32,128]{2,1,0:T(8,128)(2,1)S(1)}, u32[]{:S(2)}, u32[]{:S(2)}) collective-permute-start(bf16[4,32,128]{2,1,0:T(8,128)(2,1)S(1)} %get-tuple-element.25), channel_id=1, source_target_pairs={{0,1},{2,3},{4,5},{6,7},{1,0},{3,2},{5,4},{7,6},{8,9},{10,11},{12,... | collective-permute-start | bytes 98312 | tf_op jit(solution)/shard_map/ppermute | solution.py:368
  47.1 1.2 collective-permute-start.7
  51.6 15.1 %collective-permute-start.10 = (bf16[4,32,128]{2,1,0:T(8,128)(2,1)S(1)}, bf16[4,32,128]{2,1,0:T(8,128)(2,1)S(1)}, u32[]{:S(2)}, u32[]{:S(2)}) collective-permute-start(bf16[4,32,128]{2,1,0:T(8,128)(2,1)S(1)} %get-tuple-element.30), channel_id=1, source_target_pairs={{0,1},{2,3},{4,5},{6,7},{1,0},{3,2},{5,4},{7,6},{8,9},{10,11},{12,... | collective-permute-start | bytes 98312 | tf_op jit(solution)/shard_map/ppermute | solution.py:368
  58.1 32.7 %collective-permute-start.8 = (bf16[8,32,128]{2,1,0:T(8,128)(2,1)S(1)}, bf16[8,32,128]{2,1,0:T(8,128)(2,1)S(1)}, u32[]{:S(2)}, u32[]{:S(2)}) collective-permute-start(bf16[8,32,128]{2,1,0:T(8,128)(2,1)S(1)} %get-tuple-element.28), channel_id=1, source_target_pairs={{0,8},{16,24},{32,40},{48,56},{64,72},{80,88},{96,104},{112,120},{... | collective-permute-start | bytes 196616 | tf_op jit(solution)/shard_map/ppermute | solution.py:368
  60.0 30.8 %collective-permute-start.9 = (bf16[8,32,128]{2,1,0:T(8,128)(2,1)S(1)}, bf16[8,32,128]{2,1,0:T(8,128)(2,1)S(1)}, u32[]{:S(2)}, u32[]{:S(2)}) collective-permute-start(bf16[8,32,128]{2,1,0:T(8,128)(2,1)S(1)} %get-tuple-element.29), channel_id=1, source_target_pairs={{8,16},{24,32},{40,48},{56,64},{72,80},{88,96},{104,112},{120,128}... | collective-permute-start | bytes 196616 | tf_op jit(solution)/shard_map/ppermute | solution.py:368
  66.1 24.7 %collective-permute-start.11 = (bf16[4,32,128]{2,1,0:T(8,128)(2,1)S(1)}, bf16[4,32,128]{2,1,0:T(8,128)(2,1)S(1)}, u32[]{:S(2)}, u32[]{:S(2)}) collective-permute-start(bf16[4,32,128]{2,1,0:T(8,128)(2,1)S(1)} %get-tuple-element.31), channel_id=1, source_target_pairs={{1,2},{3,4},{5,6},{2,1},{4,3},{6,5},{9,10},{11,12},{13,14},{10,9},... | collective-permute-start | bytes 98312 | tf_op jit(solution)/shard_map/ppermute | solution.py:368
  68.0 48.3 %all-to-all-start = ((f32[128,2,128]{2,1,0:T(2,128)}), f32[128,2,128]{2,1,0:T(2,128)S(1)}, u32[]{:S(2)}, u32[]{:S(2)}) async-start(f32[128,2,128]{2,1,0:T(2,128)} %mail.1), calls=%async_computation | async-start | bytes 262144 | tf_op jit(solution)/shard_map/all_to_all | solution.py:400
  100.1 16.2 %collective-permute-start.14 = (bf16[4,32,128]{2,1,0:T(8,128)(2,1)S(1)}, bf16[4,32,128]{2,1,0:T(8,128)(2,1)S(1)}, u32[]{:S(2)}, u32[]{:S(2)}) collective-permute-start(bf16[4,32,128]{2,1,0:T(8,128)(2,1)S(1)} %get-tuple-element.35), channel_id=1, source_target_pairs={{0,1},{2,3},{4,5},{6,7},{1,0},{3,2},{5,4},{7,6},{8,9},{10,11},{12,... | collective-permute-start | bytes 98312 | tf_op jit(solution)/shard_map/ppermute | solution.py:368
  102.0 23.9 %collective-permute-start.12 = (bf16[8,32,128]{2,1,0:T(8,128)(2,1)S(1)}, bf16[8,32,128]{2,1,0:T(8,128)(2,1)S(1)}, u32[]{:S(2)}, u32[]{:S(2)}) collective-permute-start(bf16[8,32,128]{2,1,0:T(8,128)(2,1)S(1)} %get-tuple-element.33), channel_id=1, source_target_pairs={{0,8},{16,24},{32,40},{48,56},{64,72},{80,88},{96,104},{112,120},{... | collective-permute-start | bytes 196616 | tf_op jit(solution)/shard_map/ppermute | solution.py:368
  107.7 18.3 %collective-permute-start.13 = (bf16[8,32,128]{2,1,0:T(8,128)(2,1)S(1)}, bf16[8,32,128]{2,1,0:T(8,128)(2,1)S(1)}, u32[]{:S(2)}, u32[]{:S(2)}) collective-permute-start(bf16[8,32,128]{2,1,0:T(8,128)(2,1)S(1)} %get-tuple-element.34), channel_id=1, source_target_pairs={{8,16},{24,32},{40,48},{56,64},{72,80},{88,96},{104,112},{120,128}... | collective-permute-start | bytes 196616 | tf_op jit(solution)/shard_map/ppermute | solution.py:368
  115.6 10.3 %collective-permute-start.15 = (bf16[4,32,128]{2,1,0:T(8,128)(2,1)S(1)}, bf16[4,32,128]{2,1,0:T(8,128)(2,1)S(1)}, u32[]{:S(2)}, u32[]{:S(2)}) collective-permute-start(bf16[4,32,128]{2,1,0:T(8,128)(2,1)S(1)} %get-tuple-element.36), channel_id=1, source_target_pairs={{1,2},{3,4},{5,6},{2,1},{4,3},{6,5},{9,10},{11,12},{13,14},{10,9},... | collective-permute-start | bytes 98312 | tf_op jit(solution)/shard_map/ppermute | solution.py:368
  121.6 10.3 %all-to-all-start.1 = ((f32[8,4,512]{2,1,0:T(4,128)}), f32[8,4,512]{2,1,0:T(4,128)S(1)}, u32[]{:S(2)}, u32[]{:S(2)}) async-start(f32[8,4,512]{2,1,0:T(4,128)} %expand.1), calls=%async_computation.1 | async-start | bytes 131072 | tf_op jit(solution)/shard_map/all_to_all | solution.py:404

commit v3 on v2

--- a/solution.py
+++ b/solution.py
@@ -42,10 +42,10 @@
 
     sizes = lax.fori_loop(0, slots, tally, (jnp.int32(0),) * kinds)
     firsts, place = [], jnp.int32(0)
-    for size in sizes:
+    for kind, size in enumerate(sizes):
         firsts.append(place)
         place = place + (size + PACK - 1) // PACK * PACK
-    table_ref[kind_at + groups] = place // PACK
+        table_ref[kind_at + groups + kind] = place // PACK
 
     def put(slot, nexts):
         kind = type_ref[slot]
@@ -64,7 +64,7 @@
     odd_row, odd_col = side_ref[0] == 1, side_ref[1] == 1
     first_row = jnp.where(odd_row, 0, rows - 1)
     first_col = jnp.where(odd_col, 0, cols - 1)
-    return (first_row, rows - 1 - first_row), (first_col, cols - 1 - first_col)
+    return (rows - 1 - first_row, first_row), (first_col, cols - 1 - first_col)
 
 
 def beyond(edge, length):
@@ -83,9 +83,12 @@
     to_rows, to_cols = refs[6:8], refs[8:10]
     if flat:
         v_ref, table_ref = refs[10:12]
-    field, totals, x_ref, y_ref, jac, sem = refs[-6:]
-    fetch = pltpu.make_async_copy(jac_hbm, jac, sem)
-    fetch.start()
+    field, totals, *pairs, jac, sem = refs[-8:]
+    xs, ys = pairs[0:2], pairs[2:4]
+    kinds = jac.shape[0]
+    fetches = [pltpu.make_async_copy(jac_hbm.at[t], jac.at[t], sem.at[t]) for t in range(kinds)]
+    for fetch in fetches:
+        fetch.start()
     if flat:
         make_plan(type_ref.shape[0], groups, faces_ref, type_ref, count_ref, table_ref)
     row_edges, col_edges = sides(side_ref, rows, cols)
@@ -126,27 +129,45 @@
                 field[cell_rows((r + 1) * width + out_cols[n]), :] = col_refs[n][r].astype(jnp.float32)
     for cell in range((rows + 2) * width):
         totals[cell_rows(cell), :] = zero
-    y_ref[edge // 8 * 8 :, :] = jnp.zeros((y_ref.shape[0] - edge // 8 * 8, LANES), jnp.float32)
-    fetch.wait()
-
-    def group(g, carry):
+    for y in ys:
+        y[edge // 8 * 8 :, :] = jnp.zeros((y.shape[0] - edge // 8 * 8, LANES), jnp.float32)
+
+    def gather(g, x):
+        for f in range(6):
+            at = [cell_rows(table_ref[(g * PACK + s) * 6 + f]) for s in range(PACK)]
+            spread = swap_slots([field[at[s], :] for s in range(PACK)])
+            for b in range(4):
+                x[pl.ds(f * dofs + b, FR, stride=4), :] = spread[b]
+
+    def multiply(g, x, y):
         kind = table_ref[groups * PACK * 6 + g]
-        cells = [[table_ref[(g * PACK + s) * 6 + f] for s in range(PACK)] for f in range(6)]
+        y[0:edge, :] = jnp.dot(
+            jac[kind], x[0:edge, :].astype(jnp.bfloat16), preferred_element_type=jnp.float32
+        )
+
+    def scatter(g, y):
         for f in range(6):
-            spread = swap_slots([field[cell_rows(cells[f][s]), :] for s in range(PACK)])
-            for b in range(4):
-                x_ref[pl.ds(f * dofs + b, FR, stride=4), :] = spread[b]
-        y_ref[0:edge, :] = jnp.dot(
-            jac[kind], x_ref[0:edge, :].astype(jnp.bfloat16), preferred_element_type=jnp.float32
-        )
-        for f in range(6):
-            back = swap_slots([y_ref[pl.ds(f * dofs + b, FR, stride=4), :] for b in range(4)])
+            back = swap_slots([y[pl.ds(f * dofs + b, FR, stride=4), :] for b in range(4)])
             for s in range(PACK):
-                at = cell_rows(cells[f][s])
+                at = cell_rows(table_ref[(g * PACK + s) * 6 + f])
                 totals[at, :] = totals[at, :] + back[s]
+
+    def pair(m, carry):
+        gather(2 * m, xs[0])
+        gather(2 * m + 1, xs[1])
+        multiply(2 * m, xs[0], ys[0])
+        multiply(2 * m + 1, xs[1], ys[1])
+        scatter(2 * m, ys[0])
+        scatter(2 * m + 1, ys[1])
         return carry
 
-    lax.fori_loop(0, table_ref[groups * PACK * 6 + groups], group, jnp.int32(0))
+    done = jnp.int32(0)
+    for t in range(kinds):
+        fetches[t].wait()
+        ready = table_ref[groups * (PACK * 6 + 1) + t]
+        upto = (ready + 1) // 2 if t == kinds - 1 else ready // 2
+        lax.fori_loop(done, upto, pair, jnp.int32(0))
+        done = upto
 
     for r in range(rows):
         for c in range(cols):
@@ -215,23 +236,34 @@
     mail_ref[:, 1, :] = jnp.broadcast_to(ids.astype(jnp.float32), (owners, LANES))
 
 
-def expand_kernel(mail_ref, out_ref, turned_ref, flat_ref, hot_ref):
+def expand_kernel(mail_ref, out_ref, turned_ref, where_ref, flat_ref, at_ref, hot_ref):
     senders = mail_ref.shape[0]
     vertices = out_ref.shape[2]
-    ids = mail_ref[:, 1, :]
-    vertex = lax.broadcasted_iota(jnp.int32, (senders, vertices), 1).astype(jnp.float32)
+    parts = (vertices + LANES - 1) // LANES
+    low = lax.broadcasted_iota(jnp.int32, (LANES, senders), 0)
     turned_ref[...] = mail_ref[:, 0, :].T
+    where_ref[...] = mail_ref[:, 1, :].T.astype(jnp.int32)
     for s in range(32):
         part = slice(s * senders, (s + 1) * senders)
         flat_ref[:, part] = turned_ref[pl.ds(s, 4, stride=32), :]
-        hot_ref[part, :] = (ids[:, s : s + 1] == vertex).astype(jnp.bfloat16)
+        ids = where_ref[s : s + 1, :]
+        at_ref[:, part] = ids // LANES
+        hot_ref[:, part] = (ids % LANES == low).astype(jnp.bfloat16)
     values = flat_ref[...]
     high = values.astype(jnp.bfloat16).astype(jnp.float32)
-    both = jnp.concatenate([high, values - high], axis=0).astype(jnp.bfloat16)
-    wide = jnp.dot(both, hot_ref[...], preferred_element_type=jnp.float32)
-    total = wide[0:4] + wide[4:8]
-    for j in range(out_ref.shape[0]):
-        out_ref[j] = total
+    block = at_ref[...]
+    left = [
+        jnp.where(block == h, piece, 0.0) for piece in (high, values - high) for h in range(parts)
+    ]
+    left = jnp.concatenate(left, axis=0).astype(jnp.bfloat16)
+    wide = lax.dot_general(
+        left, hot_ref[...], (((1,), (1,)), ((), ())), preferred_element_type=jnp.float32
+    )
+    for h in range(parts):
+        total = wide[4 * h : 4 * h + 4] + wide[4 * (parts + h) : 4 * (parts + h) + 4]
+        high = min(LANES * (h + 1), vertices)
+        for j in range(out_ref.shape[0]):
+            out_ref[j, :, LANES * h : high] = total[:, 0 : high - LANES * h]
 
 
 def last_kernel(dims, side_ref, t_ref, a_ref, b_ref, c_ref, d_ref, out_ref, sums, hold):
@@ -271,11 +303,11 @@
     rows, cols, dofs = dims
     cells = rows * cols
     slots = scalars[1].shape[0] if flat else 0
-    groups = (slots + 3 * 4) // PACK if flat else (scalars[0].shape[0] - 1) // (PACK * 6 + 1)
+    groups = (slots + 3 * 4) // PACK // 2 * 2 if flat else (scalars[0].shape[0] - jacobians.shape[0]) // (PACK * 6 + 1)
     out = (struct((cells, FR, LANES), jnp.float32),) + rim_structs(rows, cols)
     places = (VM,) * 5
     if flat:
-        out += (struct((cells, FR, LANES)), struct((groups * (PACK * 6 + 1) + 1,), jnp.int32))
+        out += (struct((cells, FR, LANES)), struct((groups * (PACK * 6 + 1) + jacobians.shape[0],), jnp.int32))
         places += (VM, SM)
     area = (rows + 2) * (cols + 2) * FR
     flops = 2**34
@@ -288,10 +320,9 @@
         scratch_shapes=[
             pltpu.VMEM((area, LANES), jnp.float32),
             pltpu.VMEM((area, LANES), jnp.float32),
-            pltpu.VMEM((6 * dofs + 10, LANES), jnp.float32),
-            pltpu.VMEM((6 * dofs + 10, LANES), jnp.float32),
+            *[pltpu.VMEM((6 * dofs + 10, LANES), jnp.float32)] * 4,
             pltpu.VMEM(jacobians.shape, jnp.bfloat16),
-            pltpu.SemaphoreType.DMA,
+            pltpu.SemaphoreType.DMA((jacobians.shape[0],)),
         ],
         compiler_params=pltpu.CompilerParams(vmem_limit_bytes=VMEM_LIMIT),
         cost_estimate=pl.CostEstimate(flops=flops, bytes_accessed=moved, transcendentals=0),
@@ -334,8 +365,10 @@
         out_specs=VM,
         scratch_shapes=[
             pltpu.VMEM((LANES, mail.shape[0]), jnp.float32),
+            pltpu.VMEM((LANES, mail.shape[0]), jnp.int32),
             pltpu.VMEM((owned, 32 * mail.shape[0]), jnp.float32),
-            pltpu.VMEM((32 * mail.shape[0], vertex_total), jnp.bfloat16),
+            pltpu.VMEM((1, 32 * mail.shape[0]), jnp.int32),
+            pltpu.VMEM((LANES, 32 * mail.shape[0]), jnp.bfloat16),
         ],
         compiler_params=pltpu.CompilerParams(vmem_limit_bytes=VMEM_LIMIT),
         cost_estimate=pl.CostEstimate(flops=2**30, bytes_accessed=2**18, transcendentals=0),
@@ -361,16 +394,15 @@
     )(side, total, *rims)
 
 
-def exchange(row_first, row_second, col_first, col_second):
+def exchange(row_second, row_first, col_first, col_second):
     def swap(value, axis, start):
         peers = lax.axis_size(axis)
         pairs = [(i, i + 1) for i in range(start, peers - 1, 2)]
         return lax.ppermute(value, axis, pairs + [(j, i) for i, j in pairs])
 
-    second = swap(row_second, "sub", 1)
     return (
+        swap(row_second, "sub", 1),
         swap(row_first, "sub", 0),
-        second,
         swap(col_first, "slab", 0),
         swap(col_second, "slab", 1),
     )
@@ -387,8 +419,8 @@
 
     ends = coarse_basis[0], coarse_basis[rows - 1], coarse_basis[:, 0], coarse_basis[:, cols - 1]
     rims = exchange(
+        jnp.where(odd_row == 1, ends[1], ends[0]),
         jnp.where(odd_row == 1, ends[0], ends[1]),
-        jnp.where(odd_row == 1, ends[1], ends[0]),
         jnp.where(odd_col == 1, ends[2], ends[3]),
         jnp.where(odd_col == 1, ends[3], ends[2]),
     )
@@ -396,11 +428,11 @@
     total, *sent, tiles, table = apply(True, dims, side, scalars, coarse_basis, rims, jacobians)
     first, *halo = middle(dims, side, total, exchange(*sent))
     rims = exchange(*halo)
-    tiles, unused = lax.optimization_barrier((tiles, rims[2]))
+    tiles, unused = lax.optimization_barrier((tiles, rims[0]))
     mail = lax.all_to_all(make_mail(dims, tiles, first, ids, owners), "sub", 0, 0)
     total, *sent = apply(False, dims, side, (table,), first, rims, jacobians)
     rims = exchange(*sent)
-    mail, unused = lax.optimization_barrier((mail, rims[2]))
+    mail, unused = lax.optimization_barrier((mail, rims[0]))
     parts = lax.all_to_all(expand(mail, narrow, rows * owners), "slab", 0, 0)
     second_image = last(dims, side, total, rims, length)
     return second_image, parts.sum(0)

time: 133 us -> 129 us (0.970)
  Pallas kernels: 27.9 us -> 19.2 us
  starting transfers between devices: 87.4 us -> 91.8 us
    all_to_all x1, starting transfers between devices: 4.4 us -> 9.35 us  [body(): parts = lax.all_to_all(expand(mail, narrow, rows * owners), 'slab', 0, 0)]
    pallas_call x2, Pallas kernels: 19.2 us -> 14.3 us  [apply(): pl.pallas_call(functools.partial(apply_kernel, flat, dims, groups), out_s...]
    pallas_call x1, Pallas kernels: 5.24 us -> 1.53 us  [expand(): pl.pallas_call(expand_kernel, out_shape=struct((narrow, owned, vertex_tot...]
    ppermute x16, starting transfers between devices: 60.3 us -> 58 us  [swap(): return lax.ppermute(value, axis, pairs + [(j, i) for i, j in pairs])]
    all_to_all x1, starting transfers between devices: 22.7 us -> 24.4 us  [body(): lax.all_to_all(make_mail(dims, tiles, first, ids, owners), 'sub', 0, 0)]
  transfers between devices with their start and end apart: 18 -> 18, of which waited for: 3 -> 4; matrix products, arithmetic and copies ran while one was open for 5% -> 5% of each run, Pallas kernels for 13% -> 9%
where the time goes in v3:
time: 129 us; the launch traced here: 128 us
  starting transfers between devices  91.8 us (71%)
  Pallas kernels  19.2 us (15%)
  waiting for transfers between devices  7.22 us (6%)
  local copies, waits for them, and re-layouts  6.24 us (5%)
  other arithmetic  1.68 us (1%)
  between operations  1.62 us (1%)
    ppermute x16, starting transfers between devices, swap(): return lax.ppermute(value, axis, pairs + [(j, i) for i, j in pairs])  58 us
    all_to_all x1, starting transfers between devices, body(): lax.all_to_all(make_mail(dims, tiles, first, ids, owners), 'sub', 0, 0)  24.4 us
    pallas_call x2, Pallas kernels, apply(): pl.pallas_call(functools.partial(apply_kernel, flat, dims, groups), out_s...  14.3 us
    all_to_all x1, starting transfers between devices, body(): parts = lax.all_to_all(expand(mail, narrow, rows * owners), 'slab', 0, 0)  9.35 us
    unnamed x9, local copies, waits for them, and re-layouts  5.02 us
    all_to_all x1, waiting for transfers between devices, body(): parts = lax.all_to_all(expand(mail, narrow, rows * owners), 'slab', 0, 0)  4.44 us
    ppermute x16, waiting for transfers between devices, swap(): return lax.ppermute(value, axis, pairs + [(j, i) for i, j in pairs])  2.78 us
  transfers between devices with their start and end apart: 18, of which 4 were waited for; matrix products, arithmetic and copies ran while one was open for 5% of the time, Pallas kernels for 9%

profile of v3, /device:TPU:62, one launch (start us, length us, event | category | flops | bytes accessed | tf_op | source)
XLA Modules:
  0.0 127.8 jit_solution(498562069888646267)
XLA Ops:
  0.6 1.1 fusion
  1.9 1.9 %collective-permute-start.2 = (bf16[4,4000]{1,0:T(4,128)(2,1)S(1)}, bf16[4,4000]{1,0:T(4,128)(2,1)S(1)}, u32[]{:S(2)}, u32[]{:S(2)}) collective-permute-start(bf16[4,4000]{1,0:T(4,128)(2,1)S(1)} %get-tuple-element.45), channel_id=1, source_target_pairs={{0,1},{2,3},{4,5},{6,7},{1,0},{3,2},{5,4},{7,6},{8,9},{10,11},{12,... | collective-permute-start | bytes 96008 | tf_op jit(solution)/shard_map/ppermute | solution.py:401
  5.4 10.2 %collective-permute-start = (bf16[8,4000]{1,0:T(8,128)(2,1)S(1)}, bf16[8,4000]{1,0:T(8,128)(2,1)S(1)}, u32[]{:S(2)}, u32[]{:S(2)}) collective-permute-start(bf16[8,4000]{1,0:T(8,128)(2,1)S(1)} %get-tuple-element.43), channel_id=1, source_target_pairs={{8,16},{24,32},{40,48},{56,64},{72,80},{88,96},{104,112},{120,128}... | collective-permute-start | bytes 192008 | tf_op jit(solution)/shard_map/ppermute | solution.py:401
  15.6 1.9 %collective-permute-start.1 = (bf16[8,4000]{1,0:T(8,128)(2,1)S(1)}, bf16[8,4000]{1,0:T(8,128)(2,1)S(1)}, u32[]{:S(2)}, u32[]{:S(2)}) collective-permute-start(bf16[8,4000]{1,0:T(8,128)(2,1)S(1)} %get-tuple-element.42), channel_id=1, source_target_pairs={{0,8},{16,24},{32,40},{48,56},{64,72},{80,88},{96,104},{112,120},{... | collective-permute-start | bytes 192008 | tf_op jit(solution)/shard_map/ppermute | solution.py:401
  17.6 5.0 %copy.10.refs_9_.refs_7_ = bf16[4,750,750]{2,1,0:T(8,128)(2,1)} copy(bf16[4,750,750]{2,0,1:T(4,128)(2,1)} %param.7) | data formatting | bytes 9000000 | tf_op args[1]
  23.3 7.5 %apply_flat.1 = (f32[32,32,128]{2,1,0:T(8,128)S(1)}, bf16[8,32,128]{2,1,0:T(8,128)(2,1)S(1)}, bf16[8,32,128]{2,1,0:T(8,128)(2,1)S(1)}, bf16[4,32,128]{2,1,0:T(8,...) custom-call(s32[2]{0:T(128)S(1)} %pad_add_fusion.refs_0_.side_ref, ...), custom_call_target="tpu_custom_call" | custom-call | flops 17179869184 | bytes 5286432 | tf_op jit(solution)/shard_map/apply_flat/pallas_call | solution.py:315
  30.8 6.6 %collective-permute-start.4 = (bf16[8,32,128]{2,1,0:T(8,128)(2,1)S(1)}, bf16[8,32,128]{2,1,0:T(8,128)(2,1)S(1)}, u32[]{:S(2)}, u32[]{:S(2)}) collective-permute-start(bf16[8,32,128]{2,1,0:T(8,128)(2,1)S(1)} %get-tuple-element.23), channel_id=1, source_target_pairs={{8,16},{24,32},{40,48},{56,64},{72,80},{88,96},{104,112},{120,128}... | collective-permute-start | bytes 196616 | tf_op jit(solution)/shard_map/ppermute | solution.py:401
  37.4 1.9 %collective-permute-start.5 = (bf16[8,32,128]{2,1,0:T(8,128)(2,1)S(1)}, bf16[8,32,128]{2,1,0:T(8,128)(2,1)S(1)}, u32[]{:S(2)}, u32[]{:S(2)}) collective-permute-start(bf16[8,32,128]{2,1,0:T(8,128)(2,1)S(1)} %get-tuple-element.24), channel_id=1, source_target_pairs={{0,8},{16,24},{32,40},{48,56},{64,72},{80,88},{96,104},{112,120},{... | collective-permute-start | bytes 196616 | tf_op jit(solution)/shard_map/ppermute | solution.py:401
  39.3 3.3 %collective-permute-start.6 = (bf16[4,32,128]{2,1,0:T(8,128)(2,1)S(1)}, bf16[4,32,128]{2,1,0:T(8,128)(2,1)S(1)}, u32[]{:S(2)}, u32[]{:S(2)}) collective-permute-start(bf16[4,32,128]{2,1,0:T(8,128)(2,1)S(1)} %get-tuple-element.25), channel_id=1, source_target_pairs={{0,1},{2,3},{4,5},{6,7},{1,0},{3,2},{5,4},{7,6},{8,9},{10,11},{12,... | collective-permute-start | bytes 98312 | tf_op jit(solution)/shard_map/ppermute | solution.py:401
  43.4 1.6 %collective-permute-done.4.a_ref = bf16[8,32,128]{2,1,0:T(8,128)(2,1)S(1)} collective-permute-done((bf16[8,32,128]{2,1,0:T(8,128)(2,1)S(1)}, bf16[8,32,128]{2,1,0:T(8,128)(2,1)S(1)}, u32[]{:S(2)}, u32[]{:S(2)}) %collective-permute-start.4) | collective-permute-done | bytes 65568 | tf_op jit(solution)/shard_map/ppermute | solution.py:401
  45.8 9.0 %collective-permute-start.8 = (bf16[8,32,128]{2,1,0:T(8,128)(2,1)S(1)}, bf16[8,32,128]{2,1,0:T(8,128)(2,1)S(1)}, u32[]{:S(2)}, u32[]{:S(2)}) collective-permute-start(bf16[8,32,128]{2,1,0:T(8,128)(2,1)S(1)} %get-tuple-element.28), channel_id=1, source_target_pairs={{8,16},{24,32},{40,48},{56,64},{72,80},{88,96},{104,112},{120,128}... | collective-permute-start | bytes 196616 | tf_op jit(solution)/shard_map/ppermute | solution.py:401
  54.9 1.9 %collective-permute-start.9 = (bf16[8,32,128]{2,1,0:T(8,128)(2,1)S(1)}, bf16[8,32,128]{2,1,0:T(8,128)(2,1)S(1)}, u32[]{:S(2)}, u32[]{:S(2)}) collective-permute-start(bf16[8,32,128]{2,1,0:T(8,128)(2,1)S(1)} %get-tuple-element.29), channel_id=1, source_target_pairs={{0,8},{16,24},{32,40},{48,56},{64,72},{80,88},{96,104},{112,120},{... | collective-permute-start | bytes 196616 | tf_op jit(solution)/shard_map/ppermute | solution.py:401
  56.8 6.0 %collective-permute-start.10 = (bf16[4,32,128]{2,1,0:T(8,128)(2,1)S(1)}, bf16[4,32,128]{2,1,0:T(8,128)(2,1)S(1)}, u32[]{:S(2)}, u32[]{:S(2)}) collective-permute-start(bf16[4,32,128]{2,1,0:T(8,128)(2,1)S(1)} %get-tuple-element.30), channel_id=1, source_target_pairs={{0,1},{2,3},{4,5},{6,7},{1,0},{3,2},{5,4},{7,6},{8,9},{10,11},{12,... | collective-permute-start | bytes 98312 | tf_op jit(solution)/shard_map/ppermute | solution.py:401
  63.5 1.3 mail.1
  64.8 24.4 %all-to-all-start = ((f32[128,2,128]{2,1,0:T(2,128)}), f32[128,2,128]{2,1,0:T(2,128)S(1)}, u32[]{:S(2)}, u32[]{:S(2)}) async-start(f32[128,2,128]{2,1,0:T(2,128)} %mail.1), calls=%async_computation | async-start | bytes 262144 | tf_op jit(solution)/shard_map/all_to_all | solution.py:432
  89.2 6.8 %apply_tiles.1 = (f32[32,32,128]{2,1,0:T(8,128)S(1)}, bf16[8,32,128]{2,1,0:T(8,128)(2,1)S(1)}, bf16[8,32,128]{2,1,0:T(8,128)(2,1)S(1)}, bf16[4,32,128]{2,1,0:T(8,128)(2,1)S(1)}, bf16[4,32,128]{2,1,0:T(8,128)(2,1)S(1)}) custom-call(s32[2]{0:T(128)S(1)} %pad_add_fusion.refs_0_.side_ref, s32[204]{0:T(256)S(1)} %get-tuple-element.21.refs_1_, ...), custom_call_target="tpu_custom_call" | custom-call | flops 17179869184 | bytes 5286432 | tf_op jit(solution)/shard_map/apply_tiles/pallas_call | solution.py:315
  96.0 7.3 %collective-permute-start.12 = (bf16[8,32,128]{2,1,0:T(8,128)(2,1)S(1)}, bf16[8,32,128]{2,1,0:T(8,128)(2,1)S(1)}, u32[]{:S(2)}, u32[]{:S(2)}) collective-permute-start(bf16[8,32,128]{2,1,0:T(8,128)(2,1)S(1)} %get-tuple-element.33), channel_id=1, source_target_pairs={{8,16},{24,32},{40,48},{56,64},{72,80},{88,96},{104,112},{120,128}... | collective-permute-start | bytes 196616 | tf_op jit(solution)/shard_map/ppermute | solution.py:401
  103.3 1.9 %collective-permute-start.13 = (bf16[8,32,128]{2,1,0:T(8,128)(2,1)S(1)}, bf16[8,32,128]{2,1,0:T(8,128)(2,1)S(1)}, u32[]{:S(2)}, u32[]{:S(2)}) collective-permute-start(bf16[8,32,128]{2,1,0:T(8,128)(2,1)S(1)} %get-tuple-element.34), channel_id=1, source_target_pairs={{0,8},{16,24},{32,40},{48,56},{64,72},{80,88},{96,104},{112,120},{... | collective-permute-start | bytes 196616 | tf_op jit(solution)/shard_map/ppermute | solution.py:401
  105.3 3.4 %collective-permute-start.14 = (bf16[4,32,128]{2,1,0:T(8,128)(2,1)S(1)}, bf16[4,32,128]{2,1,0:T(8,128)(2,1)S(1)}, u32[]{:S(2)}, u32[]{:S(2)}) collective-permute-start(bf16[4,32,128]{2,1,0:T(8,128)(2,1)S(1)} %get-tuple-element.35), channel_id=1, source_target_pairs={{0,1},{2,3},{4,5},{6,7},{1,0},{3,2},{5,4},{7,6},{8,9},{10,11},{12,... | collective-permute-start | bytes 98312 | tf_op jit(solution)/shard_map/ppermute | solution.py:401
  109.4 0.9 collective-permute-done.12.a_ref
  110.3 1.5 %expand.1 = f32[8,4,512]{2,1,0:T(4,128)} custom-call(f32[128,2,128]{2,1,0:T(2,128)S(1)} %all-to-all-done.mail_ref), custom_call_target="tpu_custom_call" | custom-call | flops 1073741824 | bytes 262144 | tf_op jit(solution)/shard_map/expand/pallas_call | solution.py:361
  111.9 9.4 %all-to-all-start.1 = ((f32[8,4,512]{2,1,0:T(4,128)}), f32[8,4,512]{2,1,0:T(4,128)S(1)}, u32[]{:S(2)}, u32[]{:S(2)}) async-start(f32[8,4,512]{2,1,0:T(4,128)} %expand.1), calls=%async_computation.1 | async-start | bytes 131072 | tf_op jit(solution)/shard_map/all_to_all | solution.py:436
  121.2 1.4 %last.1 = bf16[4,8,4000]{2,1,0:T(8,128)(2,1)} custom-call(s32[2]{0:T(128)S(1)} %pad_add_fusion.refs_0_.side_ref, f32[32,32,128]{2,1,0:T(8,128)S(1)} %get-tuple-element.32.t_ref, bf16[8,32,128]{2,1,0:T(8,128)(2,1)S(1)} %collective-permute-done.12.a_ref, bf16[8,32,128]{2,1,0:T(8,128)(2,1)S(1)} %collective-permute-done.13.b_ref, ...), custom_call_target="tpu_custom_call" | custom-call | flops 17179869184 | bytes 1048576 | tf_op jit(solution)/shard_map/last/pallas_call | solution.py:382
  122.7 4.4 %all-to-all-done.1 = f32[8,4,512]{2,1,0:T(4,128)S(1)} async-done(((f32[8,4,512]{2,1,0:T(4,128)}), f32[8,4,512]{2,1,0:T(4,128)S(1)}, u32[]{:S(2)}, u32[]{:S(2)}) %all-to-all-start.1) | async-done | bytes 65568 | tf_op jit(solution)/shard_map/all_to_all | solution.py:436
  (34 shorter events, 5.3 us)
Async XLA Ops:
  1.9 21.4 %collective-permute-start.2 = (bf16[4,4000]{1,0:T(4,128)(2,1)S(1)}, bf16[4,4000]{1,0:T(4,128)(2,1)S(1)}, u32[]{:S(2)}, u32[]{:S(2)}) collective-permute-start(bf16[4,4000]{1,0:T(4,128)(2,1)S(1)} %get-tuple-element.45), channel_id=1, source_target_pairs={{0,1},{2,3},{4,5},{6,7},{1,0},{3,2},{5,4},{7,6},{8,9},{10,11},{12,... | collective-permute-start | bytes 96008 | tf_op jit(solution)/shard_map/ppermute | solution.py:401
  3.8 19.4 %collective-permute-start.3 = (bf16[4,4000]{1,0:T(4,128)(2,1)S(1)}, bf16[4,4000]{1,0:T(4,128)(2,1)S(1)}, u32[]{:S(2)}, u32[]{:S(2)}) collective-permute-start(bf16[4,4000]{1,0:T(4,128)(2,1)S(1)} %get-tuple-element.44), channel_id=1, source_target_pairs={{1,2},{3,4},{5,6},{2,1},{4,3},{6,5},{9,10},{11,12},{13,14},{10,9},... | collective-permute-start | bytes 96008 | tf_op jit(solution)/shard_map/ppermute | solution.py:401
  5.4 17.9 %copy-start = (bf16[4,8,4000]{2,1,0:T(8,128)(2,1)S(1)}, bf16[4,8,4000]{2,1,0:T(8,128)(2,1)}, u32[]{:S(2)}) copy-start(bf16[4,8,4000]{2,1,0:T(8,128)(2,1)} %refs_4_.1) | copy-start | bytes 768004
  5.4 17.9 %copy-start.1 = (s32[20,6]{0,1:T(8,128)S(1)}, s32[20,6]{0,1:T(8,128)}, u32[]{:S(2)}) copy-start(s32[20,6]{0,1:T(8,128)} %param.8) | copy-start | bytes 1444
  5.4 17.9 %copy-start.2 = (s32[20]{0:T(128)S(1)}, s32[20]{0:T(128)}, u32[]{:S(2)}) copy-start(s32[20]{0:T(128)} %refs_2_.1) | copy-start | bytes 244
  5.4 17.9 %collective-permute-start = (bf16[8,4000]{1,0:T(8,128)(2,1)S(1)}, bf16[8,4000]{1,0:T(8,128)(2,1)S(1)}, u32[]{:S(2)}, u32[]{:S(2)}) collective-permute-start(bf16[8,4000]{1,0:T(8,128)(2,1)S(1)} %get-tuple-element.43), channel_id=1, source_target_pairs={{8,16},{24,32},{40,48},{56,64},{72,80},{88,96},{104,112},{120,128}... | collective-permute-start | bytes 192008 | tf_op jit(solution)/shard_map/ppermute | solution.py:401
  15.6 7.7 %collective-permute-start.1 = (bf16[8,4000]{1,0:T(8,128)(2,1)S(1)}, bf16[8,4000]{1,0:T(8,128)(2,1)S(1)}, u32[]{:S(2)}, u32[]{:S(2)}) collective-permute-start(bf16[8,4000]{1,0:T(8,128)(2,1)S(1)} %get-tuple-element.42), channel_id=1, source_target_pairs={{0,8},{16,24},{32,40},{48,56},{64,72},{80,88},{96,104},{112,120},{... | collective-permute-start | bytes 192008 | tf_op jit(solution)/shard_map/ppermute | solution.py:401
  23.3 31.5 %copy-start.3 = (s32[1,32]{1,0:T(1,128)S(1)}, s32[1,32]{1,0:T(1,128)}, u32[]{:S(2)}) copy-start(s32[1,32]{1,0:T(1,128)} %param.11) | copy-start | bytes 388
  30.8 14.3 %collective-permute-start.4 = (bf16[8,32,128]{2,1,0:T(8,128)(2,1)S(1)}, bf16[8,32,128]{2,1,0:T(8,128)(2,1)S(1)}, u32[]{:S(2)}, u32[]{:S(2)}) collective-permute-start(bf16[8,32,128]{2,1,0:T(8,128)(2,1)S(1)} %get-tuple-element.23), channel_id=1, source_target_pairs={{8,16},{24,32},{40,48},{56,64},{72,80},{88,96},{104,112},{120,128}... | collective-permute-start | bytes 196616 | tf_op jit(solution)/shard_map/ppermute | solution.py:401
  37.4 7.7 %collective-permute-start.5 = (bf16[8,32,128]{2,1,0:T(8,128)(2,1)S(1)}, bf16[8,32,128]{2,1,0:T(8,128)(2,1)S(1)}, u32[]{:S(2)}, u32[]{:S(2)}) collective-permute-start(bf16[8,32,128]{2,1,0:T(8,128)(2,1)S(1)} %get-tuple-element.24), channel_id=1, source_target_pairs={{0,8},{16,24},{32,40},{48,56},{64,72},{80,88},{96,104},{112,120},{... | collective-permute-start | bytes 196616 | tf_op jit(solution)/shard_map/ppermute | solution.py:401
  39.3 4.1 %collective-permute-start.6 = (bf16[4,32,128]{2,1,0:T(8,128)(2,1)S(1)}, bf16[4,32,128]{2,1,0:T(8,128)(2,1)S(1)}, u32[]{:S(2)}, u32[]{:S(2)}) collective-permute-start(bf16[4,32,128]{2,1,0:T(8,128)(2,1)S(1)} %get-tuple-element.25), channel_id=1, source_target_pairs={{0,1},{2,3},{4,5},{6,7},{1,0},{3,2},{5,4},{7,6},{8,9},{10,11},{12,... | collective-permute-start | bytes 98312 | tf_op jit(solution)/shard_map/ppermute | solution.py:401
  42.6 0.8 collective-permute-start.7
  45.8 17.7 %collective-permute-start.8 = (bf16[8,32,128]{2,1,0:T(8,128)(2,1)S(1)}, bf16[8,32,128]{2,1,0:T(8,128)(2,1)S(1)}, u32[]{:S(2)}, u32[]{:S(2)}) collective-permute-start(bf16[8,32,128]{2,1,0:T(8,128)(2,1)S(1)} %get-tuple-element.28), channel_id=1, source_target_pairs={{8,16},{24,32},{40,48},{56,64},{72,80},{88,96},{104,112},{120,128}... | collective-permute-start | bytes 196616 | tf_op jit(solution)/shard_map/ppermute | solution.py:401
  54.9 34.3 %collective-permute-start.9 = (bf16[8,32,128]{2,1,0:T(8,128)(2,1)S(1)}, bf16[8,32,128]{2,1,0:T(8,128)(2,1)S(1)}, u32[]{:S(2)}, u32[]{:S(2)}) collective-permute-start(bf16[8,32,128]{2,1,0:T(8,128)(2,1)S(1)} %get-tuple-element.29), channel_id=1, source_target_pairs={{0,8},{16,24},{32,40},{48,56},{64,72},{80,88},{96,104},{112,120},{... | collective-permute-start | bytes 196616 | tf_op jit(solution)/shard_map/ppermute | solution.py:401
  56.8 32.4 %collective-permute-start.10 = (bf16[4,32,128]{2,1,0:T(8,128)(2,1)S(1)}, bf16[4,32,128]{2,1,0:T(8,128)(2,1)S(1)}, u32[]{:S(2)}, u32[]{:S(2)}) collective-permute-start(bf16[4,32,128]{2,1,0:T(8,128)(2,1)S(1)} %get-tuple-element.30), channel_id=1, source_target_pairs={{0,1},{2,3},{4,5},{6,7},{1,0},{3,2},{5,4},{7,6},{8,9},{10,11},{12,... | collective-permute-start | bytes 98312 | tf_op jit(solution)/shard_map/ppermute | solution.py:401
  62.8 26.4 %collective-permute-start.11 = (bf16[4,32,128]{2,1,0:T(8,128)(2,1)S(1)}, bf16[4,32,128]{2,1,0:T(8,128)(2,1)S(1)}, u32[]{:S(2)}, u32[]{:S(2)}) collective-permute-start(bf16[4,32,128]{2,1,0:T(8,128)(2,1)S(1)} %get-tuple-element.31), channel_id=1, source_target_pairs={{1,2},{3,4},{5,6},{2,1},{4,3},{6,5},{9,10},{11,12},{13,14},{10,9},... | collective-permute-start | bytes 98312 | tf_op jit(solution)/shard_map/ppermute | solution.py:401
  64.8 45.6 %all-to-all-start = ((f32[128,2,128]{2,1,0:T(2,128)}), f32[128,2,128]{2,1,0:T(2,128)S(1)}, u32[]{:S(2)}, u32[]{:S(2)}) async-start(f32[128,2,128]{2,1,0:T(2,128)} %mail.1), calls=%async_computation | async-start | bytes 262144 | tf_op jit(solution)/shard_map/all_to_all | solution.py:432
  96.0 14.3 %collective-permute-start.12 = (bf16[8,32,128]{2,1,0:T(8,128)(2,1)S(1)}, bf16[8,32,128]{2,1,0:T(8,128)(2,1)S(1)}, u32[]{:S(2)}, u32[]{:S(2)}) collective-permute-start(bf16[8,32,128]{2,1,0:T(8,128)(2,1)S(1)} %get-tuple-element.33), channel_id=1, source_target_pairs={{8,16},{24,32},{40,48},{56,64},{72,80},{88,96},{104,112},{120,128}... | collective-permute-start | bytes 196616 | tf_op jit(solution)/shard_map/ppermute | solution.py:401
  103.3 17.9 %collective-permute-start.13 = (bf16[8,32,128]{2,1,0:T(8,128)(2,1)S(1)}, bf16[8,32,128]{2,1,0:T(8,128)(2,1)S(1)}, u32[]{:S(2)}, u32[]{:S(2)}) collective-permute-start(bf16[8,32,128]{2,1,0:T(8,128)(2,1)S(1)} %get-tuple-element.34), channel_id=1, source_target_pairs={{0,8},{16,24},{32,40},{48,56},{64,72},{80,88},{96,104},{112,120},{... | collective-permute-start | bytes 196616 | tf_op jit(solution)/shard_map/ppermute | solution.py:401
  105.3 15.9 %collective-permute-start.14 = (bf16[4,32,128]{2,1,0:T(8,128)(2,1)S(1)}, bf16[4,32,128]{2,1,0:T(8,128)(2,1)S(1)}, u32[]{:S(2)}, u32[]{:S(2)}) collective-permute-start(bf16[4,32,128]{2,1,0:T(8,128)(2,1)S(1)} %get-tuple-element.35), channel_id=1, source_target_pairs={{0,1},{2,3},{4,5},{6,7},{1,0},{3,2},{5,4},{7,6},{8,9},{10,11},{12,... | collective-permute-start | bytes 98312 | tf_op jit(solution)/shard_map/ppermute | solution.py:401
  108.7 12.5 %collective-permute-start.15 = (bf16[4,32,128]{2,1,0:T(8,128)(2,1)S(1)}, bf16[4,32,128]{2,1,0:T(8,128)(2,1)S(1)}, u32[]{:S(2)}, u32[]{:S(2)}) collective-permute-start(bf16[4,32,128]{2,1,0:T(8,128)(2,1)S(1)} %get-tuple-element.36), channel_id=1, source_target_pairs={{1,2},{3,4},{5,6},{2,1},{4,3},{6,5},{9,10},{11,12},{13,14},{10,9},... | collective-permute-start | bytes 98312 | tf_op jit(solution)/shard_map/ppermute | solution.py:401
  111.9 15.3 %all-to-all-start.1 = ((f32[8,4,512]{2,1,0:T(4,128)}), f32[8,4,512]{2,1,0:T(4,128)S(1)}, u32[]{:S(2)}, u32[]{:S(2)}) async-start(f32[8,4,512]{2,1,0:T(4,128)} %expand.1), calls=%async_computation.1 | async-start | bytes 131072 | tf_op jit(solution)/shard_map/all_to_all | solution.py:436

commit v4 on v3

--- a/solution.py
+++ b/solution.py
@@ -71,6 +71,14 @@
     return jnp.where(edge == 0, 0, length + 1)
 
 
+def near_views(side_ref, rows, refs):
+    far_ref, block_ref, second_ref = refs
+    me = side_ref[0] * 2 + side_ref[1]
+    row = jnp.where(side_ref[0] == 1, me - 2, me + 2)
+    col = jnp.where(side_ref[1] == 1, me - 1, me + 1)
+    return (far_ref, block_ref.at[row]), (block_ref.at[col], second_ref)
+
+
 def apply_kernel(flat, dims, groups, *refs):
     rows, cols, dofs = dims
     edge = 6 * dofs
@@ -79,10 +87,15 @@
         side_ref, faces_ref, type_ref, count_ref, own_ref, *refs = refs
     else:
         side_ref, table_ref, own_ref, *refs = refs
-    row_refs, col_refs, jac_hbm, t_ref = refs[0:2], refs[2:4], refs[4], refs[5]
-    to_rows, to_cols = refs[6:8], refs[8:10]
     if flat:
-        v_ref, table_ref = refs[10:12]
+        row_refs, col_refs = refs[0:2], refs[2:4]
+        v_ref, table_ref = refs[9:11]
+        jac_hbm, t_ref, *sent = refs[4:9]
+    else:
+        row_refs, col_refs = near_views(side_ref, rows, refs[0:3])
+        jac_hbm, t_ref, *sent = refs[3:8]
+    sent[1][...] = jnp.zeros_like(sent[1])
+    to_rows, to_cols = near_views(side_ref, rows, sent)
     field, totals, *pairs, jac, sem = refs[-8:]
     xs, ys = pairs[0:2], pairs[2:4]
     kinds = jac.shape[0]
@@ -179,26 +192,28 @@
             to_cols[n][r] = totals[cell_rows((r + 1) * width + out_cols[n]), :].astype(jnp.bfloat16)
 
 
-def combine(dims, side_ref, t_ref, rims, hold):
-    rows, cols, dofs = dims
+def combine(dims, side_ref, t_ref, refs, hold):
+    rows, cols, dofs = dims
+    row_refs, col_refs = near_views(side_ref, rows, refs)
     row_edges, col_edges = sides(side_ref, rows, cols)
     for cell in range(rows * cols):
         hold[cell] = t_ref[cell]
     for n in range(2):
         for c in range(cols):
             cell = row_edges[n] * cols + c
-            hold[cell] = hold[cell] + rims[n][c].astype(jnp.float32)
+            hold[cell] = hold[cell] + row_refs[n][c].astype(jnp.float32)
         for r in range(rows):
             cell = r * cols + col_edges[n]
-            hold[cell] = hold[cell] + rims[2 + n][r].astype(jnp.float32)
+            hold[cell] = hold[cell] + col_refs[n][r].astype(jnp.float32)
     return row_edges, col_edges
 
 
-def middle_kernel(dims, side_ref, t_ref, a_ref, b_ref, c_ref, d_ref, w_ref, *refs):
+def middle_kernel(dims, side_ref, t_ref, a_ref, b_ref, c_ref, w_ref, *refs):
     rows, cols, dofs = dims
     hold = refs[-1]
-    to_rows, to_cols = refs[0:2], refs[2:4]
-    row_edges, col_edges = combine(dims, side_ref, t_ref, (a_ref, b_ref, c_ref, d_ref), hold)
+    refs[1][...] = jnp.zeros_like(refs[1])
+    to_rows, to_cols = near_views(side_ref, rows, refs[0:3])
+    row_edges, col_edges = combine(dims, side_ref, t_ref, (a_ref, b_ref, c_ref), hold)
     row = lax.broadcasted_iota(jnp.int32, (FR, LANES), 0)
     slot = lax.broadcasted_iota(jnp.int32, (FR, LANES), 1) // 32
     real = row * 4 + slot < dofs
@@ -266,10 +281,10 @@
             out_ref[j, :, LANES * h : high] = total[:, 0 : high - LANES * h]
 
 
-def last_kernel(dims, side_ref, t_ref, a_ref, b_ref, c_ref, d_ref, out_ref, sums, hold):
+def last_kernel(dims, side_ref, t_ref, a_ref, b_ref, c_ref, out_ref, sums, hold):
     rows, cols, dofs = dims
     length = out_ref.shape[2]
-    combine(dims, side_ref, t_ref, (a_ref, b_ref, c_ref, d_ref), sums)
+    combine(dims, side_ref, t_ref, (a_ref, b_ref, c_ref), sums)
     for r in range(rows):
         for c in range(cols):
             hold[pl.ds(r * FR * cols + c, FR, stride=cols), :] = sums[r * cols + c]
@@ -293,8 +308,7 @@
 def rim_structs(rows, cols):
     return (
         struct((cols, FR, LANES)),
-        struct((cols, FR, LANES)),
-        struct((rows, FR, LANES)),
+        struct((4, max(rows, cols), FR, LANES)),
         struct((rows, FR, LANES)),
     )
 
@@ -305,7 +319,7 @@
     slots = scalars[1].shape[0] if flat else 0
     groups = (slots + 3 * 4) // PACK // 2 * 2 if flat else (scalars[0].shape[0] - jacobians.shape[0]) // (PACK * 6 + 1)
     out = (struct((cells, FR, LANES), jnp.float32),) + rim_structs(rows, cols)
-    places = (VM,) * 5
+    places = (VM,) * 4
     if flat:
         out += (struct((cells, FR, LANES)), struct((groups * (PACK * 6 + 1) + jacobians.shape[0],), jnp.int32))
         places += (VM, SM)
@@ -315,7 +329,7 @@
     return pl.pallas_call(
         functools.partial(apply_kernel, flat, dims, groups),
         out_shape=out,
-        in_specs=[SM] * (1 + len(scalars)) + [VM] * 5 + [HBM],
+        in_specs=[SM] * (1 + len(scalars)) + [VM] * (1 + len(rims)) + [HBM],
         out_specs=places,
         scratch_shapes=[
             pltpu.VMEM((area, LANES), jnp.float32),
@@ -336,8 +350,8 @@
     return pl.pallas_call(
         functools.partial(middle_kernel, dims),
         out_shape=(struct((cells, FR, LANES)),) + rim_structs(rows, cols),
-        in_specs=[SM] + [VM] * 5,
-        out_specs=(VM,) * 5,
+        in_specs=[SM] + [VM] * 4,
+        out_specs=(VM,) * 4,
         scratch_shapes=[pltpu.VMEM((cells, FR, LANES), jnp.float32)],
         compiler_params=pltpu.CompilerParams(vmem_limit_bytes=VMEM_LIMIT),
         name="middle",
@@ -382,7 +396,7 @@
     return pl.pallas_call(
         functools.partial(last_kernel, dims),
         out_shape=struct((rows, cols, length)),
-        in_specs=[SM] + [VM] * 5,
+        in_specs=[SM] + [VM] * 4,
         out_specs=VM,
         scratch_shapes=[
             pltpu.VMEM((cells, FR, LANES), jnp.float32),
@@ -394,16 +408,22 @@
     )(side, total, *rims)
 
 
-def exchange(row_second, row_first, col_first, col_second):
-    def swap(value, axis, start):
-        peers = lax.axis_size(axis)
-        pairs = [(i, i + 1) for i in range(start, peers - 1, 2)]
-        return lax.ppermute(value, axis, pairs + [(j, i) for i, j in pairs])
-
+def swap(value, axis, start):
+    peers = lax.axis_size(axis)
+    pairs = [(i, i + 1) for i in range(start, peers - 1, 2)]
+    return lax.ppermute(value, axis, pairs + [(j, i) for i, j in pairs])
+
+
+def exchange(far, block, col_second):
+    wide, narrow = lax.axis_size("sub"), lax.axis_size("slab")
+    blocks = [
+        [(i + di) * narrow + j + dj for di in range(2) for dj in range(2)]
+        for i in range(0, wide, 2)
+        for j in range(0, narrow, 2)
+    ]
     return (
-        swap(row_second, "sub", 1),
-        swap(row_first, "sub", 0),
-        swap(col_first, "slab", 0),
+        swap(far, "sub", 1),
+        lax.all_to_all(block, ("sub", "slab"), 0, 0, axis_index_groups=blocks),
         swap(col_second, "slab", 1),
     )
 
@@ -418,11 +438,11 @@
     side = jnp.stack([odd_row, odd_col])
 
     ends = coarse_basis[0], coarse_basis[rows - 1], coarse_basis[:, 0], coarse_basis[:, cols - 1]
-    rims = exchange(
-        jnp.where(odd_row == 1, ends[1], ends[0]),
-        jnp.where(odd_row == 1, ends[0], ends[1]),
-        jnp.where(odd_col == 1, ends[2], ends[3]),
-        jnp.where(odd_col == 1, ends[3], ends[2]),
+    rims = (
+        swap(jnp.where(odd_row == 1, ends[1], ends[0]), "sub", 1),
+        swap(jnp.where(odd_row == 1, ends[0], ends[1]), "sub", 0),
+        swap(jnp.where(odd_col == 1, ends[2], ends[3]), "slab", 0),
+        swap(jnp.where(odd_col == 1, ends[3], ends[2]), "slab", 1),
     )
     scalars = (element_faces.T, element_type, element_count)
     total, *sent, tiles, table = apply(True, dims, side, scalars, coarse_basis, rims, jacobians)

time: 129 us -> 148 us (1.15)
  waiting for transfers between devices: 7.22 us -> 41.8 us
  starting transfers between devices: 91.8 us -> 75.2 us
    ppermute x16 -> x10, starting transfers between devices: 58 us -> 30.1 us  [swap(): return lax.ppermute(value, axis, pairs + [(j, i) for i, j in pairs])]
    ppermute x16 -> x10, waiting for transfers between devices: 2.78 us -> 28.9 us  [swap(): return lax.ppermute(value, axis, pairs + [(j, i) for i, j in pairs])]
    all_to_all x0 -> x3, starting transfers between devices: none -> 14 us  [exchange(): lax.all_to_all(block, ('sub', 'slab'), 0, 0, axis_index_groups=blocks)]
    all_to_all x1, waiting for transfers between devices: 0.01 us -> 8.52 us  [body(): lax.all_to_all(make_mail(dims, tiles, first, ids, owners), 'sub', 0, 0)]
    all_to_all x1, starting transfers between devices: 9.35 us -> 3.35 us  [body(): parts = lax.all_to_all(expand(mail, narrow, rows * owners), 'slab', 0, 0)]
    all_to_all x1, starting transfers between devices: 24.4 us -> 27.8 us  [body(): lax.all_to_all(make_mail(dims, tiles, first, ids, owners), 'sub', 0, 0)]
  transfers between devices with their start and end apart: 18 -> 15, of which waited for: 4 -> 5; matrix products, arithmetic and copies ran while one was open for 5% -> 4% of each run, Pallas kernels for 9% -> 8%
where the time goes in v4:
time: 148 us; the launch traced here: 147 us
  starting transfers between devices  75.2 us (51%)
  waiting for transfers between devices  41.8 us (28%)
  Pallas kernels  20.4 us (14%)
  local copies, waits for them, and re-layouts  6.24 us (4%)
  other arithmetic  1.68 us (1%)
  between operations  1.56 us (1%)
    ppermute x10, starting transfers between devices, swap(): return lax.ppermute(value, axis, pairs + [(j, i) for i, j in pairs])  30.1 us
    ppermute x10, waiting for transfers between devices, swap(): return lax.ppermute(value, axis, pairs + [(j, i) for i, j in pairs])  28.9 us
    all_to_all x1, starting transfers between devices, body(): lax.all_to_all(make_mail(dims, tiles, first, ids, owners), 'sub', 0, 0)  27.8 us
    pallas_call x2, Pallas kernels, apply(): pl.pallas_call(functools.partial(apply_kernel, flat, dims, groups), out_s...  14.7 us
    all_to_all x3, starting transfers between devices, exchange(): lax.all_to_all(block, ('sub', 'slab'), 0, 0, axis_index_groups=blocks)  14 us
    all_to_all x1, waiting for transfers between devices, body(): lax.all_to_all(make_mail(dims, tiles, first, ids, owners), 'sub', 0, 0)  8.52 us
    unnamed x9, local copies, waits for them, and re-layouts  5.02 us
    all_to_all x1, waiting for transfers between devices, body(): parts = lax.all_to_all(expand(mail, narrow, rows * owners), 'slab', 0, 0)  4.39 us
  transfers between devices with their start and end apart: 15, of which 5 were waited for; matrix products, arithmetic and copies ran while one was open for 4% of the time, Pallas kernels for 8%

profile of v4, /device:TPU:62, one launch (start us, length us, event | category | flops | bytes accessed | tf_op | source)
XLA Modules:
  0.0 146.9 jit_solution(1786283111541869956)
XLA Ops:
  0.6 1.1 fusion
  1.9 1.9 %collective-permute-start.2 = (bf16[4,4000]{1,0:T(4,128)(2,1)S(1)}, bf16[4,4000]{1,0:T(4,128)(2,1)S(1)}, u32[]{:S(2)}, u32[]{:S(2)}) collective-permute-start(bf16[4,4000]{1,0:T(4,128)(2,1)S(1)} %get-tuple-element.39), channel_id=1, source_target_pairs={{0,1},{2,3},{4,5},{6,7},{1,0},{3,2},{5,4},{7,6},{8,9},{10,11},{12,... | collective-permute-start | bytes 96008 | tf_op jit(solution)/shard_map/ppermute | solution.py:414
  5.4 10.2 %collective-permute-start = (bf16[8,4000]{1,0:T(8,128)(2,1)S(1)}, bf16[8,4000]{1,0:T(8,128)(2,1)S(1)}, u32[]{:S(2)}, u32[]{:S(2)}) collective-permute-start(bf16[8,4000]{1,0:T(8,128)(2,1)S(1)} %get-tuple-element.37), channel_id=1, source_target_pairs={{8,16},{24,32},{40,48},{56,64},{72,80},{88,96},{104,112},{120,128}... | collective-permute-start | bytes 192008 | tf_op jit(solution)/shard_map/ppermute | solution.py:414
  15.6 1.9 %collective-permute-start.1 = (bf16[8,4000]{1,0:T(8,128)(2,1)S(1)}, bf16[8,4000]{1,0:T(8,128)(2,1)S(1)}, u32[]{:S(2)}, u32[]{:S(2)}) collective-permute-start(bf16[8,4000]{1,0:T(8,128)(2,1)S(1)} %get-tuple-element.36), channel_id=1, source_target_pairs={{0,8},{16,24},{32,40},{48,56},{64,72},{80,88},{96,104},{112,120},{... | collective-permute-start | bytes 192008 | tf_op jit(solution)/shard_map/ppermute | solution.py:414
  17.6 5.0 %copy.10.refs_9_.refs_6_ = bf16[4,750,750]{2,1,0:T(8,128)(2,1)} copy(bf16[4,750,750]{2,0,1:T(4,128)(2,1)} %param.7) | data formatting | bytes 9000000 | tf_op args[1]
  23.3 7.4 %apply_flat.1 = (f32[32,32,128]{2,1,0:T(8,128)S(1)}, bf16[8,32,128]{2,1,0:T(8,128)(2,1)S(1)}, bf16[4,8,32,128]{3,2,1,0:T(8,128)(2,1)}, bf16[4,32,128]{2,1,0:T(8,...) custom-call(s32[2]{0:T(128)S(1)} %pad_add_fusion.refs_0_.side_ref, s32[6,20]{1,0:T(8,128)S(1)} %bitcast.12, ...), custom_call_target="tpu_custom_call" | custom-call | flops 17179869184 | bytes 5286432 | tf_op jit(solution)/shard_map/apply_flat/pallas_call | solution.py:329
  30.7 6.6 %all-to-all-start = ((bf16[4,8,32,128]{3,2,1,0:T(8,128)(2,1)}), bf16[4,8,32,128]{3,2,1,0:T(8,128)(2,1)S(1)}, u32[]{:S(2)}, u32[]{:S(2)}) async-start(bf16[4,8,32,128]{3,2,1,0:T(8,128)(2,1)} %get-tuple-element.21), calls=%async_computation | async-start | bytes 524288 | tf_op jit(solution)/shard_map/all_to_all | solution.py:426
  37.4 3.5 %collective-permute-start.4 = (bf16[8,32,128]{2,1,0:T(8,128)(2,1)S(1)}, bf16[8,32,128]{2,1,0:T(8,128)(2,1)S(1)}, u32[]{:S(2)}, u32[]{:S(2)}) collective-permute-start(bf16[8,32,128]{2,1,0:T(8,128)(2,1)S(1)} %get-tuple-element.20), channel_id=1, source_target_pairs={{8,16},{24,32},{40,48},{56,64},{72,80},{88,96},{104,112},{120,128}... | collective-permute-start | bytes 196616 | tf_op jit(solution)/shard_map/ppermute | solution.py:414
  41.6 10.3 %collective-permute-done.4.a_ref = bf16[8,32,128]{2,1,0:T(8,128)(2,1)S(1)} collective-permute-done((bf16[8,32,128]{2,1,0:T(8,128)(2,1)S(1)}, bf16[8,32,128]{2,1,0:T(8,128)(2,1)S(1)}, u32[]{:S(2)}, u32[]{:S(2)}) %collective-permute-start.4) | collective-permute-done | bytes 65568 | tf_op jit(solution)/shard_map/ppermute | solution.py:414
  51.8 1.4 middle.1
  53.2 3.4 %all-to-all-start.1 = ((bf16[4,8,32,128]{3,2,1,0:T(8,128)(2,1)}), bf16[4,8,32,128]{3,2,1,0:T(8,128)(2,1)S(1)}, u32[]{:S(2)}, u32[]{:S(2)}) async-start(bf16[4,8,32,128]{3,2,1,0:T(8,128)(2,1)} %get-tuple-element.25), calls=%async_computation.1 | async-start | bytes 524288 | tf_op jit(solution)/shard_map/all_to_all | solution.py:426
  56.6 3.8 %collective-permute-start.6 = (bf16[8,32,128]{2,1,0:T(8,128)(2,1)S(1)}, bf16[8,32,128]{2,1,0:T(8,128)(2,1)S(1)}, u32[]{:S(2)}, u32[]{:S(2)}) collective-permute-start(bf16[8,32,128]{2,1,0:T(8,128)(2,1)S(1)} %get-tuple-element.24), channel_id=1, source_target_pairs={{8,16},{24,32},{40,48},{56,64},{72,80},{88,96},{104,112},{120,128}... | collective-permute-start | bytes 196616 | tf_op jit(solution)/shard_map/ppermute | solution.py:414
  61.2 9.7 %collective-permute-done.6.refs_3_ = bf16[8,32,128]{2,1,0:T(8,128)(2,1)S(1)} collective-permute-done((bf16[8,32,128]{2,1,0:T(8,128)(2,1)S(1)}, bf16[8,32,128]{2,1,0:T(8,128)(2,1)S(1)}, u32[]{:S(2)}, u32[]{:S(2)}) %collective-permute-start.6) | collective-permute-done | bytes 65568 | tf_op jit(solution)/shard_map/ppermute | solution.py:414
  70.9 1.3 mail.1
  72.2 27.8 %all-to-all-start.3 = ((f32[128,2,128]{2,1,0:T(2,128)}), f32[128,2,128]{2,1,0:T(2,128)S(1)}, u32[]{:S(2)}, u32[]{:S(2)}) async-start(f32[128,2,128]{2,1,0:T(2,128)} %mail.1), calls=%async_computation.3 | async-start | bytes 262144 | tf_op jit(solution)/shard_map/all_to_all | solution.py:452
  100.0 7.3 %apply_tiles.1 = (f32[32,32,128]{2,1,0:T(8,128)S(1)}, bf16[8,32,128]{2,1,0:T(8,128)(2,1)S(1)}, bf16[4,8,32,128]{3,2,1,0:T(8,128)(2,1)}, bf16[4,32,128]{2,1,0:T(8,128)(2,1)S(1)}) custom-call(s32[2]{0:T(128)S(1)} %pad_add_fusion.refs_0_.side_ref, s32[204]{0:T(256)S(1)} %get-tuple-element.18.refs_1_, bf16[32,32,128]{2,1,0:T(8,128)(2,1)S(1)} %get-tuple-element.23.refs_2_.w_ref, ...), custom_call_target="tpu_custom_call" | custom-call | flops 17179869184 | bytes 5286432 | tf_op jit(solution)/shard_map/apply_tiles/pallas_call | solution.py:329
  107.4 8.5 %all-to-all-done.3.mail_ref = f32[128,2,128]{2,1,0:T(2,128)S(1)} async-done(((f32[128,2,128]{2,1,0:T(2,128)}), f32[128,2,128]{2,1,0:T(2,128)S(1)}, u32[]{:S(2)}, u32[]{:S(2)}) %all-to-all-start.3) | async-done | bytes 131104 | tf_op jit(solution)/shard_map/all_to_all | solution.py:452
  115.9 4.0 %all-to-all-start.2 = ((bf16[4,8,32,128]{3,2,1,0:T(8,128)(2,1)}), bf16[4,8,32,128]{3,2,1,0:T(8,128)(2,1)S(1)}, u32[]{:S(2)}, u32[]{:S(2)}) async-start(bf16[4,8,32,128]{3,2,1,0:T(8,128)(2,1)} %get-tuple-element.29), calls=%async_computation.2 | async-start | bytes 524288 | tf_op jit(solution)/shard_map/all_to_all | solution.py:426
  119.9 6.2 %collective-permute-start.8 = (bf16[8,32,128]{2,1,0:T(8,128)(2,1)S(1)}, bf16[8,32,128]{2,1,0:T(8,128)(2,1)S(1)}, u32[]{:S(2)}, u32[]{:S(2)}) collective-permute-start(bf16[8,32,128]{2,1,0:T(8,128)(2,1)S(1)} %get-tuple-element.28), channel_id=1, source_target_pairs={{8,16},{24,32},{40,48},{56,64},{72,80},{88,96},{104,112},{120,128}... | collective-permute-start | bytes 196616 | tf_op jit(solution)/shard_map/ppermute | solution.py:414
  126.7 8.9 %collective-permute-done.8.a_ref = bf16[8,32,128]{2,1,0:T(8,128)(2,1)S(1)} collective-permute-done((bf16[8,32,128]{2,1,0:T(8,128)(2,1)S(1)}, bf16[8,32,128]{2,1,0:T(8,128)(2,1)S(1)}, u32[]{:S(2)}, u32[]{:S(2)}) %collective-permute-start.8) | collective-permute-done | bytes 65568 | tf_op jit(solution)/shard_map/ppermute | solution.py:414
  135.5 1.5 %expand.1 = f32[8,4,512]{2,1,0:T(4,128)} custom-call(f32[128,2,128]{2,1,0:T(2,128)S(1)} %all-to-all-done.3.mail_ref), custom_call_target="tpu_custom_call" | custom-call | flops 1073741824 | bytes 262144 | tf_op jit(solution)/shard_map/expand/pallas_call | solution.py:375
  137.1 3.4 %all-to-all-start.4 = ((f32[8,4,512]{2,1,0:T(4,128)}), f32[8,4,512]{2,1,0:T(4,128)S(1)}, u32[]{:S(2)}, u32[]{:S(2)}) async-start(f32[8,4,512]{2,1,0:T(4,128)} %expand.1), calls=%async_computation.4 | async-start | bytes 131072 | tf_op jit(solution)/shard_map/all_to_all | solution.py:456
  140.4 1.4 last.1
  141.9 4.4 %all-to-all-done.4 = f32[8,4,512]{2,1,0:T(4,128)S(1)} async-done(((f32[8,4,512]{2,1,0:T(4,128)}), f32[8,4,512]{2,1,0:T(4,128)S(1)}, u32[]{:S(2)}, u32[]{:S(2)}) %all-to-all-start.4) | async-done | bytes 65568 | tf_op jit(solution)/shard_map/all_to_all | solution.py:456
  (28 shorter events, 4.5 us)
Async XLA Ops:
  1.9 21.4 %collective-permute-start.2 = (bf16[4,4000]{1,0:T(4,128)(2,1)S(1)}, bf16[4,4000]{1,0:T(4,128)(2,1)S(1)}, u32[]{:S(2)}, u32[]{:S(2)}) collective-permute-start(bf16[4,4000]{1,0:T(4,128)(2,1)S(1)} %get-tuple-element.39), channel_id=1, source_target_pairs={{0,1},{2,3},{4,5},{6,7},{1,0},{3,2},{5,4},{7,6},{8,9},{10,11},{12,... | collective-permute-start | bytes 96008 | tf_op jit(solution)/shard_map/ppermute | solution.py:414
  3.8 19.4 %collective-permute-start.3 = (bf16[4,4000]{1,0:T(4,128)(2,1)S(1)}, bf16[4,4000]{1,0:T(4,128)(2,1)S(1)}, u32[]{:S(2)}, u32[]{:S(2)}) collective-permute-start(bf16[4,4000]{1,0:T(4,128)(2,1)S(1)} %get-tuple-element.38), channel_id=1, source_target_pairs={{1,2},{3,4},{5,6},{2,1},{4,3},{6,5},{9,10},{11,12},{13,14},{10,9},... | collective-permute-start | bytes 96008 | tf_op jit(solution)/shard_map/ppermute | solution.py:414
  5.4 17.9 %copy-start = (bf16[4,8,4000]{2,1,0:T(8,128)(2,1)S(1)}, bf16[4,8,4000]{2,1,0:T(8,128)(2,1)}, u32[]{:S(2)}) copy-start(bf16[4,8,4000]{2,1,0:T(8,128)(2,1)} %refs_4_.1) | copy-start | bytes 768004
  5.4 17.9 %copy-start.1 = (s32[20,6]{0,1:T(8,128)S(1)}, s32[20,6]{0,1:T(8,128)}, u32[]{:S(2)}) copy-start(s32[20,6]{0,1:T(8,128)} %param.8) | copy-start | bytes 1444
  5.4 17.9 %copy-start.2 = (s32[20]{0:T(128)S(1)}, s32[20]{0:T(128)}, u32[]{:S(2)}) copy-start(s32[20]{0:T(128)} %refs_2_.1) | copy-start | bytes 244
  5.4 17.9 %collective-permute-start = (bf16[8,4000]{1,0:T(8,128)(2,1)S(1)}, bf16[8,4000]{1,0:T(8,128)(2,1)S(1)}, u32[]{:S(2)}, u32[]{:S(2)}) collective-permute-start(bf16[8,4000]{1,0:T(8,128)(2,1)S(1)} %get-tuple-element.37), channel_id=1, source_target_pairs={{8,16},{24,32},{40,48},{56,64},{72,80},{88,96},{104,112},{120,128}... | collective-permute-start | bytes 192008 | tf_op jit(solution)/shard_map/ppermute | solution.py:414
  15.6 7.7 %collective-permute-start.1 = (bf16[8,4000]{1,0:T(8,128)(2,1)S(1)}, bf16[8,4000]{1,0:T(8,128)(2,1)S(1)}, u32[]{:S(2)}, u32[]{:S(2)}) collective-permute-start(bf16[8,4000]{1,0:T(8,128)(2,1)S(1)} %get-tuple-element.36), channel_id=1, source_target_pairs={{0,8},{16,24},{32,40},{48,56},{64,72},{80,88},{96,104},{112,120},{... | collective-permute-start | bytes 192008 | tf_op jit(solution)/shard_map/ppermute | solution.py:414
  23.3 37.1 %copy-start.3 = (s32[1,32]{1,0:T(1,128)S(1)}, s32[1,32]{1,0:T(1,128)}, u32[]{:S(2)}) copy-start(s32[1,32]{1,0:T(1,128)} %param.11) | copy-start | bytes 388
  30.7 21.1 %all-to-all-start = ((bf16[4,8,32,128]{3,2,1,0:T(8,128)(2,1)}), bf16[4,8,32,128]{3,2,1,0:T(8,128)(2,1)S(1)}, u32[]{:S(2)}, u32[]{:S(2)}) async-start(bf16[4,8,32,128]{3,2,1,0:T(8,128)(2,1)} %get-tuple-element.21), calls=%async_computation | async-start | bytes 524288 | tf_op jit(solution)/shard_map/all_to_all | solution.py:426
  37.4 14.4 %collective-permute-start.4 = (bf16[8,32,128]{2,1,0:T(8,128)(2,1)S(1)}, bf16[8,32,128]{2,1,0:T(8,128)(2,1)S(1)}, u32[]{:S(2)}, u32[]{:S(2)}) collective-permute-start(bf16[8,32,128]{2,1,0:T(8,128)(2,1)S(1)} %get-tuple-element.20), channel_id=1, source_target_pairs={{8,16},{24,32},{40,48},{56,64},{72,80},{88,96},{104,112},{120,128}... | collective-permute-start | bytes 196616 | tf_op jit(solution)/shard_map/ppermute | solution.py:414
  40.9 0.7 collective-permute-start.5
  53.2 19.0 %all-to-all-start.1 = ((bf16[4,8,32,128]{3,2,1,0:T(8,128)(2,1)}), bf16[4,8,32,128]{3,2,1,0:T(8,128)(2,1)S(1)}, u32[]{:S(2)}, u32[]{:S(2)}) async-start(bf16[4,8,32,128]{3,2,1,0:T(8,128)(2,1)} %get-tuple-element.25), calls=%async_computation.1 | async-start | bytes 524288 | tf_op jit(solution)/shard_map/all_to_all | solution.py:426
  56.6 14.3 %collective-permute-start.6 = (bf16[8,32,128]{2,1,0:T(8,128)(2,1)S(1)}, bf16[8,32,128]{2,1,0:T(8,128)(2,1)S(1)}, u32[]{:S(2)}, u32[]{:S(2)}) collective-permute-start(bf16[8,32,128]{2,1,0:T(8,128)(2,1)S(1)} %get-tuple-element.24), channel_id=1, source_target_pairs={{8,16},{24,32},{40,48},{56,64},{72,80},{88,96},{104,112},{120,128}... | collective-permute-start | bytes 196616 | tf_op jit(solution)/shard_map/ppermute | solution.py:414
  60.5 39.5 %collective-permute-start.7 = (bf16[4,32,128]{2,1,0:T(8,128)(2,1)S(1)}, bf16[4,32,128]{2,1,0:T(8,128)(2,1)S(1)}, u32[]{:S(2)}, u32[]{:S(2)}) collective-permute-start(bf16[4,32,128]{2,1,0:T(8,128)(2,1)S(1)} %get-tuple-element.26), channel_id=1, source_target_pairs={{1,2},{3,4},{5,6},{2,1},{4,3},{6,5},{9,10},{11,12},{13,14},{10,9},... | collective-permute-start | bytes 98312 | tf_op jit(solution)/shard_map/ppermute | solution.py:414
  72.2 43.7 %all-to-all-start.3 = ((f32[128,2,128]{2,1,0:T(2,128)}), f32[128,2,128]{2,1,0:T(2,128)S(1)}, u32[]{:S(2)}, u32[]{:S(2)}) async-start(f32[128,2,128]{2,1,0:T(2,128)} %mail.1), calls=%async_computation.3 | async-start | bytes 262144 | tf_op jit(solution)/shard_map/all_to_all | solution.py:452
  115.9 21.2 %all-to-all-start.2 = ((bf16[4,8,32,128]{3,2,1,0:T(8,128)(2,1)}), bf16[4,8,32,128]{3,2,1,0:T(8,128)(2,1)S(1)}, u32[]{:S(2)}, u32[]{:S(2)}) async-start(bf16[4,8,32,128]{3,2,1,0:T(8,128)(2,1)} %get-tuple-element.29), calls=%async_computation.2 | async-start | bytes 524288 | tf_op jit(solution)/shard_map/all_to_all | solution.py:426
  119.9 15.7 %collective-permute-start.8 = (bf16[8,32,128]{2,1,0:T(8,128)(2,1)S(1)}, bf16[8,32,128]{2,1,0:T(8,128)(2,1)S(1)}, u32[]{:S(2)}, u32[]{:S(2)}) collective-permute-start(bf16[8,32,128]{2,1,0:T(8,128)(2,1)S(1)} %get-tuple-element.28), channel_id=1, source_target_pairs={{8,16},{24,32},{40,48},{56,64},{72,80},{88,96},{104,112},{120,128}... | collective-permute-start | bytes 196616 | tf_op jit(solution)/shard_map/ppermute | solution.py:414
  126.0 14.4 %collective-permute-start.9 = (bf16[4,32,128]{2,1,0:T(8,128)(2,1)S(1)}, bf16[4,32,128]{2,1,0:T(8,128)(2,1)S(1)}, u32[]{:S(2)}, u32[]{:S(2)}) collective-permute-start(bf16[4,32,128]{2,1,0:T(8,128)(2,1)S(1)} %get-tuple-element.30), channel_id=1, source_target_pairs={{1,2},{3,4},{5,6},{2,1},{4,3},{6,5},{9,10},{11,12},{13,14},{10,9},... | collective-permute-start | bytes 98312 | tf_op jit(solution)/shard_map/ppermute | solution.py:414
  137.1 9.2 %all-to-all-start.4 = ((f32[8,4,512]{2,1,0:T(4,128)}), f32[8,4,512]{2,1,0:T(4,128)S(1)}, u32[]{:S(2)}, u32[]{:S(2)}) async-start(f32[8,4,512]{2,1,0:T(4,128)} %expand.1), calls=%async_computation.4 | async-start | bytes 131072 | tf_op jit(solution)/shard_map/all_to_all | solution.py:456

commit v5 on v3

--- a/solution.py
+++ b/solution.py
@@ -230,10 +230,12 @@
     place = (vertex == ids).astype(jnp.bfloat16)
     high = local.astype(jnp.bfloat16)
     low = (local - high.astype(jnp.float32)).astype(jnp.bfloat16)
-    mail_ref[:, 0, :] = jnp.dot(place, high, preferred_element_type=jnp.float32) + jnp.dot(
+    values = jnp.dot(place, high, preferred_element_type=jnp.float32) + jnp.dot(
         place, low, preferred_element_type=jnp.float32
     )
-    mail_ref[:, 1, :] = jnp.broadcast_to(ids.astype(jnp.float32), (owners, LANES))
+    lane = lax.broadcasted_iota(jnp.int32, (owners, LANES), 1)
+    halves = jnp.where(lane < 32, ids // 256, ids % 256).astype(jnp.float32)
+    mail_ref[...] = jnp.stack([values, halves], axis=1).astype(jnp.bfloat16)
 
 
 def expand_kernel(mail_ref, out_ref, turned_ref, where_ref, flat_ref, at_ref, hot_ref):
@@ -241,8 +243,10 @@
     vertices = out_ref.shape[2]
     parts = (vertices + LANES - 1) // LANES
     low = lax.broadcasted_iota(jnp.int32, (LANES, senders), 0)
-    turned_ref[...] = mail_ref[:, 0, :].T
-    where_ref[...] = mail_ref[:, 1, :].T.astype(jnp.int32)
+    mail = mail_ref[...].astype(jnp.float32)
+    turned_ref[...] = mail[:, 0, :].T
+    halves = mail[:, 1, :].T.astype(jnp.int32)
+    where_ref[...] = halves[0:32] * 256 + halves[32:64]
     for s in range(32):
         part = slice(s * senders, (s + 1) * senders)
         flat_ref[:, part] = turned_ref[pl.ds(s, 4, stride=32), :]
@@ -250,17 +254,14 @@
         at_ref[:, part] = ids // LANES
         hot_ref[:, part] = (ids % LANES == low).astype(jnp.bfloat16)
     values = flat_ref[...]
-    high = values.astype(jnp.bfloat16).astype(jnp.float32)
     block = at_ref[...]
-    left = [
-        jnp.where(block == h, piece, 0.0) for piece in (high, values - high) for h in range(parts)
-    ]
+    left = [jnp.where(block == h, values, 0.0) for h in range(parts)]
     left = jnp.concatenate(left, axis=0).astype(jnp.bfloat16)
     wide = lax.dot_general(
         left, hot_ref[...], (((1,), (1,)), ((), ())), preferred_element_type=jnp.float32
     )
     for h in range(parts):
-        total = wide[4 * h : 4 * h + 4] + wide[4 * (parts + h) : 4 * (parts + h) + 4]
+        total = wide[4 * h : 4 * h + 4]
         high = min(LANES * (h + 1), vertices)
         for j in range(out_ref.shape[0]):
             out_ref[j, :, LANES * h : high] = total[:, 0 : high - LANES * h]
@@ -347,7 +348,7 @@
 def make_mail(dims, tiles, first, ids, owners):
     return pl.pallas_call(
         functools.partial(mail_kernel, dims),
-        out_shape=struct((owners, 2, LANES), jnp.float32),
+        out_shape=struct((owners, 2, LANES)),
         in_specs=[VM] * 3,
         out_specs=VM,
         compiler_params=pltpu.CompilerParams(vmem_limit_bytes=VMEM_LIMIT),
@@ -365,7 +366,7 @@
         out_specs=VM,
         scratch_shapes=[
             pltpu.VMEM((LANES, mail.shape[0]), jnp.float32),
-            pltpu.VMEM((LANES, mail.shape[0]), jnp.int32),
+            pltpu.VMEM((32, mail.shape[0]), jnp.int32),
             pltpu.VMEM((owned, 32 * mail.shape[0]), jnp.float32),
             pltpu.VMEM((1, 32 * mail.shape[0]), jnp.int32),
             pltpu.VMEM((LANES, 32 * mail.shape[0]), jnp.bfloat16),

time: 129 us -> 127 us (0.984)
  starting transfers between devices: 91.8 us -> 87.8 us
  Pallas kernels: 19.2 us -> 22.1 us
    all_to_all x1, starting transfers between devices: 9.35 us -> 4.89 us  [body(): parts = lax.all_to_all(expand(mail, narrow, rows * owners), 'slab', 0, 0)]
    pallas_call x2, Pallas kernels: 14.3 us -> 17.1 us  [apply(): pl.pallas_call(functools.partial(apply_kernel, flat, dims, groups), out_s...]
  transfers between devices with their start and end apart: 18 -> 18, of which waited for: 4 -> 4; matrix products, arithmetic and copies ran while one was open for 5% -> 5% of each run, Pallas kernels for 9% -> 10%
where the time goes in v5:
time: 127 us; the launch traced here: 126 us
  starting transfers between devices  87.8 us (69%)
  Pallas kernels  22.1 us (17%)
  waiting for transfers between devices  6.47 us (5%)
  local copies, waits for them, and re-layouts  6.24 us (5%)
  other arithmetic  1.68 us (1%)
  between operations  1.62 us (1%)
    ppermute x16, starting transfers between devices, swap(): return lax.ppermute(value, axis, pairs + [(j, i) for i, j in pairs])  58.5 us
    all_to_all x1, starting transfers between devices, body(): lax.all_to_all(make_mail(dims, tiles, first, ids, owners), 'sub', 0, 0)  24.4 us
    pallas_call x2, Pallas kernels, apply(): pl.pallas_call(functools.partial(apply_kernel, flat, dims, groups), out_s...  17.1 us
    unnamed x9, local copies, waits for them, and re-layouts  5.02 us
    all_to_all x1, starting transfers between devices, body(): parts = lax.all_to_all(expand(mail, narrow, rows * owners), 'slab', 0, 0)  4.89 us
    all_to_all x1, waiting for transfers between devices, body(): parts = lax.all_to_all(expand(mail, narrow, rows * owners), 'slab', 0, 0)  4.44 us
  transfers between devices with their start and end apart: 18, of which 4 were waited for; matrix products, arithmetic and copies ran while one was open for 5% of the time, Pallas kernels for 10%

profile of v5, /device:TPU:62, one launch (start us, length us, event | category | flops | bytes accessed | tf_op | source)
XLA Modules:
  0.0 125.9 jit_solution(8140872548466902226)
XLA Ops:
  0.6 1.1 fusion
  1.9 1.9 %collective-permute-start.2 = (bf16[4,4000]{1,0:T(4,128)(2,1)S(1)}, bf16[4,4000]{1,0:T(4,128)(2,1)S(1)}, u32[]{:S(2)}, u32[]{:S(2)}) collective-permute-start(bf16[4,4000]{1,0:T(4,128)(2,1)S(1)} %get-tuple-element.45), channel_id=1, source_target_pairs={{0,1},{2,3},{4,5},{6,7},{1,0},{3,2},{5,4},{7,6},{8,9},{10,11},{12,... | collective-permute-start | bytes 96008 | tf_op jit(solution)/shard_map/ppermute | solution.py:402
  4.5 0.9 select_bitcast_fusion
  5.4 10.2 %collective-permute-start = (bf16[8,4000]{1,0:T(8,128)(2,1)S(1)}, bf16[8,4000]{1,0:T(8,128)(2,1)S(1)}, u32[]{:S(2)}, u32[]{:S(2)}) collective-permute-start(bf16[8,4000]{1,0:T(8,128)(2,1)S(1)} %get-tuple-element.43), channel_id=1, source_target_pairs={{8,16},{24,32},{40,48},{56,64},{72,80},{88,96},{104,112},{120,128}... | collective-permute-start | bytes 192008 | tf_op jit(solution)/shard_map/ppermute | solution.py:402
  15.6 1.9 %collective-permute-start.1 = (bf16[8,4000]{1,0:T(8,128)(2,1)S(1)}, bf16[8,4000]{1,0:T(8,128)(2,1)S(1)}, u32[]{:S(2)}, u32[]{:S(2)}) collective-permute-start(bf16[8,4000]{1,0:T(8,128)(2,1)S(1)} %get-tuple-element.42), channel_id=1, source_target_pairs={{0,8},{16,24},{32,40},{48,56},{64,72},{80,88},{96,104},{112,120},{... | collective-permute-start | bytes 192008 | tf_op jit(solution)/shard_map/ppermute | solution.py:402
  17.6 5.0 %copy.10.refs_9_.refs_7_ = bf16[4,750,750]{2,1,0:T(8,128)(2,1)} copy(bf16[4,750,750]{2,0,1:T(4,128)(2,1)} %param.7) | data formatting | bytes 9000000 | tf_op args[1]
  23.3 8.9 %apply_flat.1 = (f32[32,32,128]{2,1,0:T(8,128)S(1)}, bf16[8,32,128]{2,1,0:T(8,128)(2,1)S(1)}, bf16[8,32,128]{2,1,0:T(8,128)(2,1)S(1)}, bf16[4,32,128]{2,1,0:T(8,...) custom-call(s32[2]{0:T(128)S(1)} %pad_add_fusion.refs_0_.side_ref, ...), custom_call_target="tpu_custom_call" | custom-call | flops 17179869184 | bytes 5286432 | tf_op jit(solution)/shard_map/apply_flat/pallas_call | solution.py:316
  32.2 5.1 %collective-permute-start.4 = (bf16[8,32,128]{2,1,0:T(8,128)(2,1)S(1)}, bf16[8,32,128]{2,1,0:T(8,128)(2,1)S(1)}, u32[]{:S(2)}, u32[]{:S(2)}) collective-permute-start(bf16[8,32,128]{2,1,0:T(8,128)(2,1)S(1)} %get-tuple-element.23), channel_id=1, source_target_pairs={{8,16},{24,32},{40,48},{56,64},{72,80},{88,96},{104,112},{120,128}... | collective-permute-start | bytes 196616 | tf_op jit(solution)/shard_map/ppermute | solution.py:402
  37.3 1.9 %collective-permute-start.5 = (bf16[8,32,128]{2,1,0:T(8,128)(2,1)S(1)}, bf16[8,32,128]{2,1,0:T(8,128)(2,1)S(1)}, u32[]{:S(2)}, u32[]{:S(2)}) collective-permute-start(bf16[8,32,128]{2,1,0:T(8,128)(2,1)S(1)} %get-tuple-element.24), channel_id=1, source_target_pairs={{0,8},{16,24},{32,40},{48,56},{64,72},{80,88},{96,104},{112,120},{... | collective-permute-start | bytes 196616 | tf_op jit(solution)/shard_map/ppermute | solution.py:402
  39.3 5.9 %collective-permute-start.6 = (bf16[4,32,128]{2,1,0:T(8,128)(2,1)S(1)}, bf16[4,32,128]{2,1,0:T(8,128)(2,1)S(1)}, u32[]{:S(2)}, u32[]{:S(2)}) collective-permute-start(bf16[4,32,128]{2,1,0:T(8,128)(2,1)S(1)} %get-tuple-element.25), channel_id=1, source_target_pairs={{0,1},{2,3},{4,5},{6,7},{1,0},{3,2},{5,4},{7,6},{8,9},{10,11},{12,... | collective-permute-start | bytes 98312 | tf_op jit(solution)/shard_map/ppermute | solution.py:402
  47.2 6.1 %collective-permute-start.8 = (bf16[8,32,128]{2,1,0:T(8,128)(2,1)S(1)}, bf16[8,32,128]{2,1,0:T(8,128)(2,1)S(1)}, u32[]{:S(2)}, u32[]{:S(2)}) collective-permute-start(bf16[8,32,128]{2,1,0:T(8,128)(2,1)S(1)} %get-tuple-element.28), channel_id=1, source_target_pairs={{8,16},{24,32},{40,48},{56,64},{72,80},{88,96},{104,112},{120,128}... | collective-permute-start | bytes 196616 | tf_op jit(solution)/shard_map/ppermute | solution.py:402
  53.4 1.9 %collective-permute-start.9 = (bf16[8,32,128]{2,1,0:T(8,128)(2,1)S(1)}, bf16[8,32,128]{2,1,0:T(8,128)(2,1)S(1)}, u32[]{:S(2)}, u32[]{:S(2)}) collective-permute-start(bf16[8,32,128]{2,1,0:T(8,128)(2,1)S(1)} %get-tuple-element.29), channel_id=1, source_target_pairs={{0,8},{16,24},{32,40},{48,56},{64,72},{80,88},{96,104},{112,120},{... | collective-permute-start | bytes 196616 | tf_op jit(solution)/shard_map/ppermute | solution.py:402
  55.3 7.1 %collective-permute-start.10 = (bf16[4,32,128]{2,1,0:T(8,128)(2,1)S(1)}, bf16[4,32,128]{2,1,0:T(8,128)(2,1)S(1)}, u32[]{:S(2)}, u32[]{:S(2)}) collective-permute-start(bf16[4,32,128]{2,1,0:T(8,128)(2,1)S(1)} %get-tuple-element.30), channel_id=1, source_target_pairs={{0,1},{2,3},{4,5},{6,7},{1,0},{3,2},{5,4},{7,6},{8,9},{10,11},{12,... | collective-permute-start | bytes 98312 | tf_op jit(solution)/shard_map/ppermute | solution.py:402
  63.2 1.3 %mail.1 = bf16[128,2,128]{2,1,0:T(2,128)(2,1)} custom-call(bf16[32,32,128]{2,1,0:T(8,128)(2,1)S(1)} %get-tuple-element.38.v_ref, bf16[32,32,128]{2,1,0:T(8,128)(2,1)S(1)} %get-tuple-element.27.refs_2_.w_ref, s32[1,128]{1,0:T(1,128)S(1)} %tile.13.ids_ref), custom_call_target="tpu_custom_call" | custom-call | flops 1073741824 | bytes 1048576 | tf_op jit(solution)/shard_map/mail/pallas_call | solution.py:349
  64.5 24.4 %all-to-all-start = ((bf16[128,2,128]{2,1,0:T(2,128)(2,1)}), bf16[128,2,128]{2,1,0:T(2,128)(2,1)S(1)}, u32[]{:S(2)}, u32[]{:S(2)}) async-start(bf16[128,2,128]{2,1,0:T(2,128)(2,1)} %mail.1), calls=%async_computation | async-start | bytes 131072 | tf_op jit(solution)/shard_map/all_to_all | solution.py:433
  88.9 8.2 %apply_tiles.1 = (f32[32,32,128]{2,1,0:T(8,128)S(1)}, bf16[8,32,128]{2,1,0:T(8,128)(2,1)S(1)}, bf16[8,32,128]{2,1,0:T(8,128)(2,1)S(1)}, bf16[4,32,128]{2,1,0:T(8,128)(2,1)S(1)}, bf16[4,32,128]{2,1,0:T(8,128)(2,1)S(1)}) custom-call(s32[2]{0:T(128)S(1)} %pad_add_fusion.refs_0_.side_ref, s32[204]{0:T(256)S(1)} %get-tuple-element.21.refs_1_, ...), custom_call_target="tpu_custom_call" | custom-call | flops 17179869184 | bytes 5286432 | tf_op jit(solution)/shard_map/apply_tiles/pallas_call | solution.py:316
  97.1 5.9 %collective-permute-start.12 = (bf16[8,32,128]{2,1,0:T(8,128)(2,1)S(1)}, bf16[8,32,128]{2,1,0:T(8,128)(2,1)S(1)}, u32[]{:S(2)}, u32[]{:S(2)}) collective-permute-start(bf16[8,32,128]{2,1,0:T(8,128)(2,1)S(1)} %get-tuple-element.33), channel_id=1, source_target_pairs={{8,16},{24,32},{40,48},{56,64},{72,80},{88,96},{104,112},{120,128}... | collective-permute-start | bytes 196616 | tf_op jit(solution)/shard_map/ppermute | solution.py:402
  103.0 1.9 %collective-permute-start.13 = (bf16[8,32,128]{2,1,0:T(8,128)(2,1)S(1)}, bf16[8,32,128]{2,1,0:T(8,128)(2,1)S(1)}, u32[]{:S(2)}, u32[]{:S(2)}) collective-permute-start(bf16[8,32,128]{2,1,0:T(8,128)(2,1)S(1)} %get-tuple-element.34), channel_id=1, source_target_pairs={{0,8},{16,24},{32,40},{48,56},{64,72},{80,88},{96,104},{112,120},{... | collective-permute-start | bytes 196616 | tf_op jit(solution)/shard_map/ppermute | solution.py:402
  104.9 6.0 %collective-permute-start.14 = (bf16[4,32,128]{2,1,0:T(8,128)(2,1)S(1)}, bf16[4,32,128]{2,1,0:T(8,128)(2,1)S(1)}, u32[]{:S(2)}, u32[]{:S(2)}) collective-permute-start(bf16[4,32,128]{2,1,0:T(8,128)(2,1)S(1)} %get-tuple-element.35), channel_id=1, source_target_pairs={{0,1},{2,3},{4,5},{6,7},{1,0},{3,2},{5,4},{7,6},{8,9},{10,11},{12,... | collective-permute-start | bytes 98312 | tf_op jit(solution)/shard_map/ppermute | solution.py:402
  111.6 1.3 %collective-permute-done.12.a_ref = bf16[8,32,128]{2,1,0:T(8,128)(2,1)S(1)} collective-permute-done((bf16[8,32,128]{2,1,0:T(8,128)(2,1)S(1)}, bf16[8,32,128]{2,1,0:T(8,128)(2,1)S(1)}, u32[]{:S(2)}, u32[]{:S(2)}) %collective-permute-start.12) | collective-permute-done | bytes 65568 | tf_op jit(solution)/shard_map/ppermute | solution.py:402
  112.9 1.5 %expand.1 = f32[8,4,512]{2,1,0:T(4,128)} custom-call(bf16[128,2,128]{2,1,0:T(2,128)(2,1)S(1)} %all-to-all-done.mail_ref), custom_call_target="tpu_custom_call" | custom-call | flops 1073741824 | bytes 262144 | tf_op jit(solution)/shard_map/expand/pallas_call | solution.py:362
  114.4 4.9 %all-to-all-start.1 = ((f32[8,4,512]{2,1,0:T(4,128)}), f32[8,4,512]{2,1,0:T(4,128)S(1)}, u32[]{:S(2)}, u32[]{:S(2)}) async-start(f32[8,4,512]{2,1,0:T(4,128)} %expand.1), calls=%async_computation.1 | async-start | bytes 131072 | tf_op jit(solution)/shard_map/all_to_all | solution.py:437
  119.4 1.4 %last.1 = bf16[4,8,4000]{2,1,0:T(8,128)(2,1)} custom-call(s32[2]{0:T(128)S(1)} %pad_add_fusion.refs_0_.side_ref, f32[32,32,128]{2,1,0:T(8,128)S(1)} %get-tuple-element.32.t_ref, bf16[8,32,128]{2,1,0:T(8,128)(2,1)S(1)} %collective-permute-done.12.a_ref, bf16[8,32,128]{2,1,0:T(8,128)(2,1)S(1)} %collective-permute-done.13.b_ref, ...), custom_call_target="tpu_custom_call" | custom-call | flops 17179869184 | bytes 1048576 | tf_op jit(solution)/shard_map/last/pallas_call | solution.py:383
  120.8 4.4 %all-to-all-done.1 = f32[8,4,512]{2,1,0:T(4,128)S(1)} async-done(((f32[8,4,512]{2,1,0:T(4,128)}), f32[8,4,512]{2,1,0:T(4,128)S(1)}, u32[]{:S(2)}, u32[]{:S(2)}) %all-to-all-start.1) | async-done | bytes 65568 | tf_op jit(solution)/shard_map/all_to_all | solution.py:437
  (34 shorter events, 4.9 us)
Async XLA Ops:
  1.9 21.4 %collective-permute-start.2 = (bf16[4,4000]{1,0:T(4,128)(2,1)S(1)}, bf16[4,4000]{1,0:T(4,128)(2,1)S(1)}, u32[]{:S(2)}, u32[]{:S(2)}) collective-permute-start(bf16[4,4000]{1,0:T(4,128)(2,1)S(1)} %get-tuple-element.45), channel_id=1, source_target_pairs={{0,1},{2,3},{4,5},{6,7},{1,0},{3,2},{5,4},{7,6},{8,9},{10,11},{12,... | collective-permute-start | bytes 96008 | tf_op jit(solution)/shard_map/ppermute | solution.py:402
  3.8 19.4 %collective-permute-start.3 = (bf16[4,4000]{1,0:T(4,128)(2,1)S(1)}, bf16[4,4000]{1,0:T(4,128)(2,1)S(1)}, u32[]{:S(2)}, u32[]{:S(2)}) collective-permute-start(bf16[4,4000]{1,0:T(4,128)(2,1)S(1)} %get-tuple-element.44), channel_id=1, source_target_pairs={{1,2},{3,4},{5,6},{2,1},{4,3},{6,5},{9,10},{11,12},{13,14},{10,9},... | collective-permute-start | bytes 96008 | tf_op jit(solution)/shard_map/ppermute | solution.py:402
  5.4 17.9 %copy-start = (bf16[4,8,4000]{2,1,0:T(8,128)(2,1)S(1)}, bf16[4,8,4000]{2,1,0:T(8,128)(2,1)}, u32[]{:S(2)}) copy-start(bf16[4,8,4000]{2,1,0:T(8,128)(2,1)} %refs_4_.1) | copy-start | bytes 768004
  5.4 17.9 %copy-start.1 = (s32[20,6]{0,1:T(8,128)S(1)}, s32[20,6]{0,1:T(8,128)}, u32[]{:S(2)}) copy-start(s32[20,6]{0,1:T(8,128)} %param.8) | copy-start | bytes 1444
  5.4 17.9 %copy-start.2 = (s32[20]{0:T(128)S(1)}, s32[20]{0:T(128)}, u32[]{:S(2)}) copy-start(s32[20]{0:T(128)} %refs_2_.1) | copy-start | bytes 244
  5.4 17.9 %collective-permute-start = (bf16[8,4000]{1,0:T(8,128)(2,1)S(1)}, bf16[8,4000]{1,0:T(8,128)(2,1)S(1)}, u32[]{:S(2)}, u32[]{:S(2)}) collective-permute-start(bf16[8,4000]{1,0:T(8,128)(2,1)S(1)} %get-tuple-element.43), channel_id=1, source_target_pairs={{8,16},{24,32},{40,48},{56,64},{72,80},{88,96},{104,112},{120,128}... | collective-permute-start | bytes 192008 | tf_op jit(solution)/shard_map/ppermute | solution.py:402
  15.6 7.7 %collective-permute-start.1 = (bf16[8,4000]{1,0:T(8,128)(2,1)S(1)}, bf16[8,4000]{1,0:T(8,128)(2,1)S(1)}, u32[]{:S(2)}, u32[]{:S(2)}) collective-permute-start(bf16[8,4000]{1,0:T(8,128)(2,1)S(1)} %get-tuple-element.42), channel_id=1, source_target_pairs={{0,8},{16,24},{32,40},{48,56},{64,72},{80,88},{96,104},{112,120},{... | collective-permute-start | bytes 192008 | tf_op jit(solution)/shard_map/ppermute | solution.py:402
  23.3 30.0 %copy-start.3 = (s32[1,32]{1,0:T(1,128)S(1)}, s32[1,32]{1,0:T(1,128)}, u32[]{:S(2)}) copy-start(s32[1,32]{1,0:T(1,128)} %param.11) | copy-start | bytes 388
  32.2 14.3 %collective-permute-start.4 = (bf16[8,32,128]{2,1,0:T(8,128)(2,1)S(1)}, bf16[8,32,128]{2,1,0:T(8,128)(2,1)S(1)}, u32[]{:S(2)}, u32[]{:S(2)}) collective-permute-start(bf16[8,32,128]{2,1,0:T(8,128)(2,1)S(1)} %get-tuple-element.23), channel_id=1, source_target_pairs={{8,16},{24,32},{40,48},{56,64},{72,80},{88,96},{104,112},{120,128}... | collective-permute-start | bytes 196616 | tf_op jit(solution)/shard_map/ppermute | solution.py:402
  37.3 9.2 %collective-permute-start.5 = (bf16[8,32,128]{2,1,0:T(8,128)(2,1)S(1)}, bf16[8,32,128]{2,1,0:T(8,128)(2,1)S(1)}, u32[]{:S(2)}, u32[]{:S(2)}) collective-permute-start(bf16[8,32,128]{2,1,0:T(8,128)(2,1)S(1)} %get-tuple-element.24), channel_id=1, source_target_pairs={{0,8},{16,24},{32,40},{48,56},{64,72},{80,88},{96,104},{112,120},{... | collective-permute-start | bytes 196616 | tf_op jit(solution)/shard_map/ppermute | solution.py:402
  39.3 6.8 %collective-permute-start.6 = (bf16[4,32,128]{2,1,0:T(8,128)(2,1)S(1)}, bf16[4,32,128]{2,1,0:T(8,128)(2,1)S(1)}, u32[]{:S(2)}, u32[]{:S(2)}) collective-permute-start(bf16[4,32,128]{2,1,0:T(8,128)(2,1)S(1)} %get-tuple-element.25), channel_id=1, source_target_pairs={{0,1},{2,3},{4,5},{6,7},{1,0},{3,2},{5,4},{7,6},{8,9},{10,11},{12,... | collective-permute-start | bytes 98312 | tf_op jit(solution)/shard_map/ppermute | solution.py:402
  45.2 0.8 collective-permute-start.7
  47.2 16.0 %collective-permute-start.8 = (bf16[8,32,128]{2,1,0:T(8,128)(2,1)S(1)}, bf16[8,32,128]{2,1,0:T(8,128)(2,1)S(1)}, u32[]{:S(2)}, u32[]{:S(2)}) collective-permute-start(bf16[8,32,128]{2,1,0:T(8,128)(2,1)S(1)} %get-tuple-element.28), channel_id=1, source_target_pairs={{8,16},{24,32},{40,48},{56,64},{72,80},{88,96},{104,112},{120,128}... | collective-permute-start | bytes 196616 | tf_op jit(solution)/shard_map/ppermute | solution.py:402
  53.4 35.4 %collective-permute-start.9 = (bf16[8,32,128]{2,1,0:T(8,128)(2,1)S(1)}, bf16[8,32,128]{2,1,0:T(8,128)(2,1)S(1)}, u32[]{:S(2)}, u32[]{:S(2)}) collective-permute-start(bf16[8,32,128]{2,1,0:T(8,128)(2,1)S(1)} %get-tuple-element.29), channel_id=1, source_target_pairs={{0,8},{16,24},{32,40},{48,56},{64,72},{80,88},{96,104},{112,120},{... | collective-permute-start | bytes 196616 | tf_op jit(solution)/shard_map/ppermute | solution.py:402
  55.3 33.5 %collective-permute-start.10 = (bf16[4,32,128]{2,1,0:T(8,128)(2,1)S(1)}, bf16[4,32,128]{2,1,0:T(8,128)(2,1)S(1)}, u32[]{:S(2)}, u32[]{:S(2)}) collective-permute-start(bf16[4,32,128]{2,1,0:T(8,128)(2,1)S(1)} %get-tuple-element.30), channel_id=1, source_target_pairs={{0,1},{2,3},{4,5},{6,7},{1,0},{3,2},{5,4},{7,6},{8,9},{10,11},{12,... | collective-permute-start | bytes 98312 | tf_op jit(solution)/shard_map/ppermute | solution.py:402
  62.5 26.4 %collective-permute-start.11 = (bf16[4,32,128]{2,1,0:T(8,128)(2,1)S(1)}, bf16[4,32,128]{2,1,0:T(8,128)(2,1)S(1)}, u32[]{:S(2)}, u32[]{:S(2)}) collective-permute-start(bf16[4,32,128]{2,1,0:T(8,128)(2,1)S(1)} %get-tuple-element.31), channel_id=1, source_target_pairs={{1,2},{3,4},{5,6},{2,1},{4,3},{6,5},{9,10},{11,12},{13,14},{10,9},... | collective-permute-start | bytes 98312 | tf_op jit(solution)/shard_map/ppermute | solution.py:402
  64.5 48.5 %all-to-all-start = ((bf16[128,2,128]{2,1,0:T(2,128)(2,1)}), bf16[128,2,128]{2,1,0:T(2,128)(2,1)S(1)}, u32[]{:S(2)}, u32[]{:S(2)}) async-start(bf16[128,2,128]{2,1,0:T(2,128)(2,1)} %mail.1), calls=%async_computation | async-start | bytes 131072 | tf_op jit(solution)/shard_map/all_to_all | solution.py:433
  97.1 15.8 %collective-permute-start.12 = (bf16[8,32,128]{2,1,0:T(8,128)(2,1)S(1)}, bf16[8,32,128]{2,1,0:T(8,128)(2,1)S(1)}, u32[]{:S(2)}, u32[]{:S(2)}) collective-permute-start(bf16[8,32,128]{2,1,0:T(8,128)(2,1)S(1)} %get-tuple-element.33), channel_id=1, source_target_pairs={{8,16},{24,32},{40,48},{56,64},{72,80},{88,96},{104,112},{120,128}... | collective-permute-start | bytes 196616 | tf_op jit(solution)/shard_map/ppermute | solution.py:402
  103.0 16.4 %collective-permute-start.13 = (bf16[8,32,128]{2,1,0:T(8,128)(2,1)S(1)}, bf16[8,32,128]{2,1,0:T(8,128)(2,1)S(1)}, u32[]{:S(2)}, u32[]{:S(2)}) collective-permute-start(bf16[8,32,128]{2,1,0:T(8,128)(2,1)S(1)} %get-tuple-element.34), channel_id=1, source_target_pairs={{0,8},{16,24},{32,40},{48,56},{64,72},{80,88},{96,104},{112,120},{... | collective-permute-start | bytes 196616 | tf_op jit(solution)/shard_map/ppermute | solution.py:402
  104.9 14.4 %collective-permute-start.14 = (bf16[4,32,128]{2,1,0:T(8,128)(2,1)S(1)}, bf16[4,32,128]{2,1,0:T(8,128)(2,1)S(1)}, u32[]{:S(2)}, u32[]{:S(2)}) collective-permute-start(bf16[4,32,128]{2,1,0:T(8,128)(2,1)S(1)} %get-tuple-element.35), channel_id=1, source_target_pairs={{0,1},{2,3},{4,5},{6,7},{1,0},{3,2},{5,4},{7,6},{8,9},{10,11},{12,... | collective-permute-start | bytes 98312 | tf_op jit(solution)/shard_map/ppermute | solution.py:402
  110.9 8.4 %collective-permute-start.15 = (bf16[4,32,128]{2,1,0:T(8,128)(2,1)S(1)}, bf16[4,32,128]{2,1,0:T(8,128)(2,1)S(1)}, u32[]{:S(2)}, u32[]{:S(2)}) collective-permute-start(bf16[4,32,128]{2,1,0:T(8,128)(2,1)S(1)} %get-tuple-element.36), channel_id=1, source_target_pairs={{1,2},{3,4},{5,6},{2,1},{4,3},{6,5},{9,10},{11,12},{13,14},{10,9},... | collective-permute-start | bytes 98312 | tf_op jit(solution)/shard_map/ppermute | solution.py:402
  114.4 10.8 %all-to-all-start.1 = ((f32[8,4,512]{2,1,0:T(4,128)}), f32[8,4,512]{2,1,0:T(4,128)S(1)}, u32[]{:S(2)}, u32[]{:S(2)}) async-start(f32[8,4,512]{2,1,0:T(4,128)} %expand.1), calls=%async_computation.1 | async-start | bytes 131072 | tf_op jit(solution)/shard_map/all_to_all | solution.py:437

commit v6 on v5

--- a/solution.py
+++ b/solution.py
@@ -11,7 +11,8 @@
 FR = 32
 LANES = 128
 PACK = 4
-VMEM_LIMIT = 50 * 1024 * 1024
+VMEM_LIMIT = 20 * 1024 * 1024
+WIDE_LIMIT = 50 * 1024 * 1024
 
 
 def swap_slots(values):
@@ -83,10 +84,16 @@
     to_rows, to_cols = refs[6:8], refs[8:10]
     if flat:
         v_ref, table_ref = refs[10:12]
-    field, totals, *pairs, jac, sem = refs[-8:]
+    if flat:
+        field, totals, *pairs = refs[-6:]
+        jac = jac_hbm
+    else:
+        field, totals, *pairs, jac, sem = refs[-8:]
     xs, ys = pairs[0:2], pairs[2:4]
     kinds = jac.shape[0]
-    fetches = [pltpu.make_async_copy(jac_hbm.at[t], jac.at[t], sem.at[t]) for t in range(kinds)]
+    fetches = []
+    if not flat:
+        fetches = [pltpu.make_async_copy(jac_hbm.at[t], jac.at[t], sem.at[t]) for t in range(kinds)]
     for fetch in fetches:
         fetch.start()
     if flat:
@@ -162,8 +169,9 @@
         return carry
 
     done = jnp.int32(0)
-    for t in range(kinds):
-        fetches[t].wait()
+    for t in range(kinds - 1 if flat else 0, kinds):
+        if not flat:
+            fetches[t].wait()
         ready = table_ref[groups * (PACK * 6 + 1) + t]
         upto = (ready + 1) // 2 if t == kinds - 1 else ready // 2
         lax.fori_loop(done, upto, pair, jnp.int32(0))
@@ -311,21 +319,21 @@
         out += (struct((cells, FR, LANES)), struct((groups * (PACK * 6 + 1) + jacobians.shape[0],), jnp.int32))
         places += (VM, SM)
     area = (rows + 2) * (cols + 2) * FR
+    held = [pltpu.VMEM(jacobians.shape, jnp.bfloat16), pltpu.SemaphoreType.DMA((jacobians.shape[0],))]
     flops = 2**34
     moved = jacobians.size * 2 + cells * FR * LANES * 6
     return pl.pallas_call(
         functools.partial(apply_kernel, flat, dims, groups),
         out_shape=out,
-        in_specs=[SM] * (1 + len(scalars)) + [VM] * 5 + [HBM],
+        in_specs=[SM] * (1 + len(scalars)) + [VM] * 5 + [VM if flat else HBM],
         out_specs=places,
         scratch_shapes=[
             pltpu.VMEM((area, LANES), jnp.float32),
             pltpu.VMEM((area, LANES), jnp.float32),
             *[pltpu.VMEM((6 * dofs + 10, LANES), jnp.float32)] * 4,
-            pltpu.VMEM(jacobians.shape, jnp.bfloat16),
-            pltpu.SemaphoreType.DMA((jacobians.shape[0],)),
+            *([] if flat else held),
         ],
-        compiler_params=pltpu.CompilerParams(vmem_limit_bytes=VMEM_LIMIT),
+        compiler_params=pltpu.CompilerParams(vmem_limit_bytes=VMEM_LIMIT if flat else WIDE_LIMIT),
         cost_estimate=pl.CostEstimate(flops=flops, bytes_accessed=moved, transcendentals=0),
         name="apply_flat" if flat else "apply_tiles",
     )(side, *scalars, own, *rims, jacobians)

time: 127 us -> 127 us (level)
  Pallas kernels: 22.1 us -> 18.9 us
  waiting for transfers between devices: 6.47 us -> 9.35 us
  local copies, waits for them, and re-layouts: 6.24 us -> 4.15 us
  starting transfers between devices: 87.8 us -> 89.8 us
    pallas_call x2, Pallas kernels: 17.1 us -> 14 us  [apply(): pl.pallas_call(functools.partial(apply_kernel, flat, dims, groups), out_s...]
    ppermute x16, waiting for transfers between devices: 2.02 us -> 4.91 us  [swap(): return lax.ppermute(value, axis, pairs + [(j, i) for i, j in pairs])]
    unnamed x9 -> x11, local copies, waits for them, and re-layouts: 5.02 us -> 2.92 us
    all_to_all x1, starting transfers between devices: 24.4 us -> 26.1 us  [body(): lax.all_to_all(make_mail(dims, tiles, first, ids, owners), 'sub', 0, 0)]
  transfers between devices with their start and end apart: 18 -> 18, of which waited for: 4 -> 5; matrix products, arithmetic and copies ran while one was open for 5% -> 3% of each run, Pallas kernels for 10% -> 9%
where the time goes in v6:
time: 127 us; the launch traced here: 126 us
  starting transfers between devices  89.8 us (71%)
  Pallas kernels  18.9 us (15%)
  waiting for transfers between devices  9.35 us (7%)
  local copies, waits for them, and re-layouts  4.15 us (3%)
  other arithmetic  1.68 us (1%)
  between operations  1.6 us (1%)
    ppermute x16, starting transfers between devices, swap(): return lax.ppermute(value, axis, pairs + [(j, i) for i, j in pairs])  57.6 us
    all_to_all x1, starting transfers between devices, body(): lax.all_to_all(make_mail(dims, tiles, first, ids, owners), 'sub', 0, 0)  26.1 us
    pallas_call x2, Pallas kernels, apply(): pl.pallas_call(functools.partial(apply_kernel, flat, dims, groups), out_s...  14 us
    all_to_all x1, starting transfers between devices, body(): parts = lax.all_to_all(expand(mail, narrow, rows * owners), 'slab', 0, 0)  6.06 us
    ppermute x16, waiting for transfers between devices, swap(): return lax.ppermute(value, axis, pairs + [(j, i) for i, j in pairs])  4.91 us
    all_to_all x1, waiting for transfers between devices, body(): parts = lax.all_to_all(expand(mail, narrow, rows * owners), 'slab', 0, 0)  4.44 us
    unnamed x11, local copies, waits for them, and re-layouts  2.92 us
  transfers between devices with their start and end apart: 18, of which 5 were waited for; matrix products, arithmetic and copies ran while one was open for 3% of the time, Pallas kernels for 9%

profile of v6, /device:TPU:62, one launch (start us, length us, event | category | flops | bytes accessed | tf_op | source)
XLA Modules:
  0.0 125.5 jit_solution(14353619198547363550)
XLA Ops:
  0.6 1.1 fusion
  1.9 1.9 %collective-permute-start.2 = (bf16[4,4000]{1,0:T(4,128)(2,1)S(1)}, bf16[4,4000]{1,0:T(4,128)(2,1)S(1)}, u32[]{:S(2)}, u32[]{:S(2)}) collective-permute-start(bf16[4,4000]{1,0:T(4,128)(2,1)S(1)} %get-tuple-element.45), channel_id=1, source_target_pairs={{0,1},{2,3},{4,5},{6,7},{1,0},{3,2},{5,4},{7,6},{8,9},{10,11},{12,... | collective-permute-start | bytes 96008 | tf_op jit(solution)/shard_map/ppermute | solution.py:410
  5.4 10.2 %collective-permute-start = (bf16[8,4000]{1,0:T(8,128)(2,1)S(1)}, bf16[8,4000]{1,0:T(8,128)(2,1)S(1)}, u32[]{:S(2)}, u32[]{:S(2)}) collective-permute-start(bf16[8,4000]{1,0:T(8,128)(2,1)S(1)} %get-tuple-element.43), channel_id=1, source_target_pairs={{8,16},{24,32},{40,48},{56,64},{72,80},{88,96},{104,112},{120,128}... | collective-permute-start | bytes 192008 | tf_op jit(solution)/shard_map/ppermute | solution.py:410
  15.6 1.9 %collective-permute-start.1 = (bf16[8,4000]{1,0:T(8,128)(2,1)S(1)}, bf16[8,4000]{1,0:T(8,128)(2,1)S(1)}, u32[]{:S(2)}, u32[]{:S(2)}) collective-permute-start(bf16[8,4000]{1,0:T(8,128)(2,1)S(1)} %get-tuple-element.42), channel_id=1, source_target_pairs={{0,8},{16,24},{32,40},{48,56},{64,72},{80,88},{96,104},{112,120},{... | collective-permute-start | bytes 192008 | tf_op jit(solution)/shard_map/ppermute | solution.py:410
  17.6 2.9 %copy.10.refs_9_.refs_7_ = bf16[4,750,750]{2,1,0:T(8,128)(2,1)S(1)} copy(bf16[4,750,750]{2,0,1:T(4,128)(2,1)} %param.7) | data formatting | bytes 9000000 | tf_op args[1]
  21.8 7.1 %apply_flat.1 = (f32[32,32,128]{2,1,0:T(8,128)S(1)}, bf16[8,32,128]{2,1,0:T(8,128)(2,1)S(1)}, bf16[8,32,128]{2,1,0:T(8,128)(2,1)S(1)}, bf16[4,32,128]{2,1,0:T(8,...) custom-call(s32[2]{0:T(128)S(1)} %pad_add_fusion.refs_0_.side_ref, ...), custom_call_target="tpu_custom_call" | custom-call | flops 17179869184 | bytes 5286432 | tf_op jit(solution)/shard_map/apply_flat/pallas_call | solution.py:325
  28.9 9.8 %collective-permute-start.4 = (bf16[8,32,128]{2,1,0:T(8,128)(2,1)S(1)}, bf16[8,32,128]{2,1,0:T(8,128)(2,1)S(1)}, u32[]{:S(2)}, u32[]{:S(2)}) collective-permute-start(bf16[8,32,128]{2,1,0:T(8,128)(2,1)S(1)} %get-tuple-element.23), channel_id=1, source_target_pairs={{8,16},{24,32},{40,48},{56,64},{72,80},{88,96},{104,112},{120,128}... | collective-permute-start | bytes 196616 | tf_op jit(solution)/shard_map/ppermute | solution.py:410
  38.8 1.9 %collective-permute-start.5 = (bf16[8,32,128]{2,1,0:T(8,128)(2,1)S(1)}, bf16[8,32,128]{2,1,0:T(8,128)(2,1)S(1)}, u32[]{:S(2)}, u32[]{:S(2)}) collective-permute-start(bf16[8,32,128]{2,1,0:T(8,128)(2,1)S(1)} %get-tuple-element.24), channel_id=1, source_target_pairs={{0,8},{16,24},{32,40},{48,56},{64,72},{80,88},{96,104},{112,120},{... | collective-permute-start | bytes 196616 | tf_op jit(solution)/shard_map/ppermute | solution.py:410
  40.7 1.9 %collective-permute-start.6 = (bf16[4,32,128]{2,1,0:T(8,128)(2,1)S(1)}, bf16[4,32,128]{2,1,0:T(8,128)(2,1)S(1)}, u32[]{:S(2)}, u32[]{:S(2)}) collective-permute-start(bf16[4,32,128]{2,1,0:T(8,128)(2,1)S(1)} %get-tuple-element.25), channel_id=1, source_target_pairs={{0,1},{2,3},{4,5},{6,7},{1,0},{3,2},{5,4},{7,6},{8,9},{10,11},{12,... | collective-permute-start | bytes 98312 | tf_op jit(solution)/shard_map/ppermute | solution.py:410
  43.8 1.1 collective-permute-done.5.b_ref
  45.6 8.2 %collective-permute-start.8 = (bf16[8,32,128]{2,1,0:T(8,128)(2,1)S(1)}, bf16[8,32,128]{2,1,0:T(8,128)(2,1)S(1)}, u32[]{:S(2)}, u32[]{:S(2)}) collective-permute-start(bf16[8,32,128]{2,1,0:T(8,128)(2,1)S(1)} %get-tuple-element.28), channel_id=1, source_target_pairs={{8,16},{24,32},{40,48},{56,64},{72,80},{88,96},{104,112},{120,128}... | collective-permute-start | bytes 196616 | tf_op jit(solution)/shard_map/ppermute | solution.py:410
  54.0 1.9 %collective-permute-start.9 = (bf16[8,32,128]{2,1,0:T(8,128)(2,1)S(1)}, bf16[8,32,128]{2,1,0:T(8,128)(2,1)S(1)}, u32[]{:S(2)}, u32[]{:S(2)}) collective-permute-start(bf16[8,32,128]{2,1,0:T(8,128)(2,1)S(1)} %get-tuple-element.29), channel_id=1, source_target_pairs={{0,8},{16,24},{32,40},{48,56},{64,72},{80,88},{96,104},{112,120},{... | collective-permute-start | bytes 196616 | tf_op jit(solution)/shard_map/ppermute | solution.py:410
  55.9 4.8 %collective-permute-start.10 = (bf16[4,32,128]{2,1,0:T(8,128)(2,1)S(1)}, bf16[4,32,128]{2,1,0:T(8,128)(2,1)S(1)}, u32[]{:S(2)}, u32[]{:S(2)}) collective-permute-start(bf16[4,32,128]{2,1,0:T(8,128)(2,1)S(1)} %get-tuple-element.30), channel_id=1, source_target_pairs={{0,1},{2,3},{4,5},{6,7},{1,0},{3,2},{5,4},{7,6},{8,9},{10,11},{12,... | collective-permute-start | bytes 98312 | tf_op jit(solution)/shard_map/ppermute | solution.py:410
  61.4 1.3 %mail.1 = bf16[128,2,128]{2,1,0:T(2,128)(2,1)} custom-call(bf16[32,32,128]{2,1,0:T(8,128)(2,1)S(1)} %get-tuple-element.38.v_ref, bf16[32,32,128]{2,1,0:T(8,128)(2,1)S(1)} %get-tuple-element.27.refs_2_.w_ref, s32[1,128]{1,0:T(1,128)S(1)} %tile.13.ids_ref), custom_call_target="tpu_custom_call" | custom-call | flops 1073741824 | bytes 1048576 | tf_op jit(solution)/shard_map/mail/pallas_call | solution.py:357
  62.7 26.1 %all-to-all-start = ((bf16[128,2,128]{2,1,0:T(2,128)(2,1)}), bf16[128,2,128]{2,1,0:T(2,128)(2,1)S(1)}, u32[]{:S(2)}, u32[]{:S(2)}) async-start(bf16[128,2,128]{2,1,0:T(2,128)(2,1)} %mail.1), calls=%async_computation | async-start | bytes 131072 | tf_op jit(solution)/shard_map/all_to_all | solution.py:441
  88.8 6.9 %apply_tiles.1 = (f32[32,32,128]{2,1,0:T(8,128)S(1)}, bf16[8,32,128]{2,1,0:T(8,128)(2,1)S(1)}, bf16[8,32,128]{2,1,0:T(8,128)(2,1)S(1)}, bf16[4,32,128]{2,1,0:T(8,128)(2,1)S(1)}, bf16[4,32,128]{2,1,0:T(8,128)(2,1)S(1)}) custom-call(s32[2]{0:T(128)S(1)} %pad_add_fusion.refs_0_.side_ref, s32[204]{0:T(256)S(1)} %get-tuple-element.21.refs_1_, ...), custom_call_target="tpu_custom_call" | custom-call | flops 17179869184 | bytes 5286432 | tf_op jit(solution)/shard_map/apply_tiles/pallas_call | solution.py:325
  95.7 8.5 %collective-permute-start.12 = (bf16[8,32,128]{2,1,0:T(8,128)(2,1)S(1)}, bf16[8,32,128]{2,1,0:T(8,128)(2,1)S(1)}, u32[]{:S(2)}, u32[]{:S(2)}) collective-permute-start(bf16[8,32,128]{2,1,0:T(8,128)(2,1)S(1)} %get-tuple-element.33), channel_id=1, source_target_pairs={{8,16},{24,32},{40,48},{56,64},{72,80},{88,96},{104,112},{120,128}... | collective-permute-start | bytes 196616 | tf_op jit(solution)/shard_map/ppermute | solution.py:410
  104.2 1.9 %collective-permute-start.13 = (bf16[8,32,128]{2,1,0:T(8,128)(2,1)S(1)}, bf16[8,32,128]{2,1,0:T(8,128)(2,1)S(1)}, u32[]{:S(2)}, u32[]{:S(2)}) collective-permute-start(bf16[8,32,128]{2,1,0:T(8,128)(2,1)S(1)} %get-tuple-element.34), channel_id=1, source_target_pairs={{0,8},{16,24},{32,40},{48,56},{64,72},{80,88},{96,104},{112,120},{... | collective-permute-start | bytes 196616 | tf_op jit(solution)/shard_map/ppermute | solution.py:410
  106.1 1.9 %collective-permute-start.14 = (bf16[4,32,128]{2,1,0:T(8,128)(2,1)S(1)}, bf16[4,32,128]{2,1,0:T(8,128)(2,1)S(1)}, u32[]{:S(2)}, u32[]{:S(2)}) collective-permute-start(bf16[4,32,128]{2,1,0:T(8,128)(2,1)S(1)} %get-tuple-element.35), channel_id=1, source_target_pairs={{0,1},{2,3},{4,5},{6,7},{1,0},{3,2},{5,4},{7,6},{8,9},{10,11},{12,... | collective-permute-start | bytes 98312 | tf_op jit(solution)/shard_map/ppermute | solution.py:410
  108.7 2.7 %collective-permute-done.12.a_ref = bf16[8,32,128]{2,1,0:T(8,128)(2,1)S(1)} collective-permute-done((bf16[8,32,128]{2,1,0:T(8,128)(2,1)S(1)}, bf16[8,32,128]{2,1,0:T(8,128)(2,1)S(1)}, u32[]{:S(2)}, u32[]{:S(2)}) %collective-permute-start.12) | collective-permute-done | bytes 65568 | tf_op jit(solution)/shard_map/ppermute | solution.py:410
  111.4 1.5 %expand.1 = f32[8,4,512]{2,1,0:T(4,128)} custom-call(bf16[128,2,128]{2,1,0:T(2,128)(2,1)S(1)} %all-to-all-done.mail_ref), custom_call_target="tpu_custom_call" | custom-call | flops 1073741824 | bytes 262144 | tf_op jit(solution)/shard_map/expand/pallas_call | solution.py:370
  112.9 6.1 %all-to-all-start.1 = ((f32[8,4,512]{2,1,0:T(4,128)}), f32[8,4,512]{2,1,0:T(4,128)S(1)}, u32[]{:S(2)}, u32[]{:S(2)}) async-start(f32[8,4,512]{2,1,0:T(4,128)} %expand.1), calls=%async_computation.1 | async-start | bytes 131072 | tf_op jit(solution)/shard_map/all_to_all | solution.py:445
  119.0 1.4 %last.1 = bf16[4,8,4000]{2,1,0:T(8,128)(2,1)} custom-call(s32[2]{0:T(128)S(1)} %pad_add_fusion.refs_0_.side_ref, f32[32,32,128]{2,1,0:T(8,128)S(1)} %get-tuple-element.32.t_ref, bf16[8,32,128]{2,1,0:T(8,128)(2,1)S(1)} %collective-permute-done.12.a_ref, bf16[8,32,128]{2,1,0:T(8,128)(2,1)S(1)} %collective-permute-done.13.b_ref, ...), custom_call_target="tpu_custom_call" | custom-call | flops 17179869184 | bytes 1048576 | tf_op jit(solution)/shard_map/last/pallas_call | solution.py:391
  120.4 4.4 %all-to-all-done.1 = f32[8,4,512]{2,1,0:T(4,128)S(1)} async-done(((f32[8,4,512]{2,1,0:T(4,128)}), f32[8,4,512]{2,1,0:T(4,128)S(1)}, u32[]{:S(2)}, u32[]{:S(2)}) %all-to-all-start.1) | async-done | bytes 65568 | tf_op jit(solution)/shard_map/all_to_all | solution.py:445
  (36 shorter events, 6.2 us)
Async XLA Ops:
  1.9 19.3 %collective-permute-start.2 = (bf16[4,4000]{1,0:T(4,128)(2,1)S(1)}, bf16[4,4000]{1,0:T(4,128)(2,1)S(1)}, u32[]{:S(2)}, u32[]{:S(2)}) collective-permute-start(bf16[4,4000]{1,0:T(4,128)(2,1)S(1)} %get-tuple-element.45), channel_id=1, source_target_pairs={{0,1},{2,3},{4,5},{6,7},{1,0},{3,2},{5,4},{7,6},{8,9},{10,11},{12,... | collective-permute-start | bytes 96008 | tf_op jit(solution)/shard_map/ppermute | solution.py:410
  3.8 17.4 %collective-permute-start.3 = (bf16[4,4000]{1,0:T(4,128)(2,1)S(1)}, bf16[4,4000]{1,0:T(4,128)(2,1)S(1)}, u32[]{:S(2)}, u32[]{:S(2)}) collective-permute-start(bf16[4,4000]{1,0:T(4,128)(2,1)S(1)} %get-tuple-element.44), channel_id=1, source_target_pairs={{1,2},{3,4},{5,6},{2,1},{4,3},{6,5},{9,10},{11,12},{13,14},{10,9},... | collective-permute-start | bytes 96008 | tf_op jit(solution)/shard_map/ppermute | solution.py:410
  5.4 16.4 %copy-start.1 = (bf16[4,8,4000]{2,1,0:T(8,128)(2,1)S(1)}, bf16[4,8,4000]{2,1,0:T(8,128)(2,1)}, u32[]{:S(2)}) copy-start(bf16[4,8,4000]{2,1,0:T(8,128)(2,1)} %refs_4_.1) | copy-start | bytes 768004
  5.4 16.4 %copy-start.2 = (s32[20,6]{0,1:T(8,128)S(1)}, s32[20,6]{0,1:T(8,128)}, u32[]{:S(2)}) copy-start(s32[20,6]{0,1:T(8,128)} %param.8) | copy-start | bytes 1444
  5.4 16.4 %copy-start.3 = (s32[20]{0:T(128)S(1)}, s32[20]{0:T(128)}, u32[]{:S(2)}) copy-start(s32[20]{0:T(128)} %refs_2_.1) | copy-start | bytes 244
  5.4 15.8 %collective-permute-start = (bf16[8,4000]{1,0:T(8,128)(2,1)S(1)}, bf16[8,4000]{1,0:T(8,128)(2,1)S(1)}, u32[]{:S(2)}, u32[]{:S(2)}) collective-permute-start(bf16[8,4000]{1,0:T(8,128)(2,1)S(1)} %get-tuple-element.43), channel_id=1, source_target_pairs={{8,16},{24,32},{40,48},{56,64},{72,80},{88,96},{104,112},{120,128}... | collective-permute-start | bytes 192008 | tf_op jit(solution)/shard_map/ppermute | solution.py:410
  15.6 6.2 %collective-permute-start.1 = (bf16[8,4000]{1,0:T(8,128)(2,1)S(1)}, bf16[8,4000]{1,0:T(8,128)(2,1)S(1)}, u32[]{:S(2)}, u32[]{:S(2)}) collective-permute-start(bf16[8,4000]{1,0:T(8,128)(2,1)S(1)} %get-tuple-element.42), channel_id=1, source_target_pairs={{0,8},{16,24},{32,40},{48,56},{64,72},{80,88},{96,104},{112,120},{... | collective-permute-start | bytes 192008 | tf_op jit(solution)/shard_map/ppermute | solution.py:410
  20.5 8.4 %copy-start = (bf16[4,750,750]{2,1,0:T(8,128)(2,1)}, bf16[4,750,750]{2,1,0:T(8,128)(2,1)S(1)}, u32[]{:S(2)}) copy-start(bf16[4,750,750]{2,1,0:T(8,128)(2,1)S(1)} %copy.10.refs_9_.refs_7_) | copy-start | bytes 13500004
  21.7 32.1 %copy-start.4 = (s32[1,32]{1,0:T(1,128)S(1)}, s32[1,32]{1,0:T(1,128)}, u32[]{:S(2)}) copy-start(s32[1,32]{1,0:T(1,128)} %param.11) | copy-start | bytes 388
  28.9 14.9 %collective-permute-start.4 = (bf16[8,32,128]{2,1,0:T(8,128)(2,1)S(1)}, bf16[8,32,128]{2,1,0:T(8,128)(2,1)S(1)}, u32[]{:S(2)}, u32[]{:S(2)}) collective-permute-start(bf16[8,32,128]{2,1,0:T(8,128)(2,1)S(1)} %get-tuple-element.23), channel_id=1, source_target_pairs={{8,16},{24,32},{40,48},{56,64},{72,80},{88,96},{104,112},{120,128}... | collective-permute-start | bytes 196616 | tf_op jit(solution)/shard_map/ppermute | solution.py:410
  38.8 6.2 %collective-permute-start.5 = (bf16[8,32,128]{2,1,0:T(8,128)(2,1)S(1)}, bf16[8,32,128]{2,1,0:T(8,128)(2,1)S(1)}, u32[]{:S(2)}, u32[]{:S(2)}) collective-permute-start(bf16[8,32,128]{2,1,0:T(8,128)(2,1)S(1)} %get-tuple-element.24), channel_id=1, source_target_pairs={{0,8},{16,24},{32,40},{48,56},{64,72},{80,88},{96,104},{112,120},{... | collective-permute-start | bytes 196616 | tf_op jit(solution)/shard_map/ppermute | solution.py:410
  40.7 3.1 %collective-permute-start.6 = (bf16[4,32,128]{2,1,0:T(8,128)(2,1)S(1)}, bf16[4,32,128]{2,1,0:T(8,128)(2,1)S(1)}, u32[]{:S(2)}, u32[]{:S(2)}) collective-permute-start(bf16[4,32,128]{2,1,0:T(8,128)(2,1)S(1)} %get-tuple-element.25), channel_id=1, source_target_pairs={{0,1},{2,3},{4,5},{6,7},{1,0},{3,2},{5,4},{7,6},{8,9},{10,11},{12,... | collective-permute-start | bytes 98312 | tf_op jit(solution)/shard_map/ppermute | solution.py:410
  42.6 1.2 collective-permute-start.7
  45.6 15.8 %collective-permute-start.8 = (bf16[8,32,128]{2,1,0:T(8,128)(2,1)S(1)}, bf16[8,32,128]{2,1,0:T(8,128)(2,1)S(1)}, u32[]{:S(2)}, u32[]{:S(2)}) collective-permute-start(bf16[8,32,128]{2,1,0:T(8,128)(2,1)S(1)} %get-tuple-element.28), channel_id=1, source_target_pairs={{8,16},{24,32},{40,48},{56,64},{72,80},{88,96},{104,112},{120,128}... | collective-permute-start | bytes 196616 | tf_op jit(solution)/shard_map/ppermute | solution.py:410
  54.0 34.9 %collective-permute-start.9 = (bf16[8,32,128]{2,1,0:T(8,128)(2,1)S(1)}, bf16[8,32,128]{2,1,0:T(8,128)(2,1)S(1)}, u32[]{:S(2)}, u32[]{:S(2)}) collective-permute-start(bf16[8,32,128]{2,1,0:T(8,128)(2,1)S(1)} %get-tuple-element.29), channel_id=1, source_target_pairs={{0,8},{16,24},{32,40},{48,56},{64,72},{80,88},{96,104},{112,120},{... | collective-permute-start | bytes 196616 | tf_op jit(solution)/shard_map/ppermute | solution.py:410
  55.9 32.9 %collective-permute-start.10 = (bf16[4,32,128]{2,1,0:T(8,128)(2,1)S(1)}, bf16[4,32,128]{2,1,0:T(8,128)(2,1)S(1)}, u32[]{:S(2)}, u32[]{:S(2)}) collective-permute-start(bf16[4,32,128]{2,1,0:T(8,128)(2,1)S(1)} %get-tuple-element.30), channel_id=1, source_target_pairs={{0,1},{2,3},{4,5},{6,7},{1,0},{3,2},{5,4},{7,6},{8,9},{10,11},{12,... | collective-permute-start | bytes 98312 | tf_op jit(solution)/shard_map/ppermute | solution.py:410
  60.7 28.1 %collective-permute-start.11 = (bf16[4,32,128]{2,1,0:T(8,128)(2,1)S(1)}, bf16[4,32,128]{2,1,0:T(8,128)(2,1)S(1)}, u32[]{:S(2)}, u32[]{:S(2)}) collective-permute-start(bf16[4,32,128]{2,1,0:T(8,128)(2,1)S(1)} %get-tuple-element.31), channel_id=1, source_target_pairs={{1,2},{3,4},{5,6},{2,1},{4,3},{6,5},{9,10},{11,12},{13,14},{10,9},... | collective-permute-start | bytes 98312 | tf_op jit(solution)/shard_map/ppermute | solution.py:410
  62.7 48.7 %all-to-all-start = ((bf16[128,2,128]{2,1,0:T(2,128)(2,1)}), bf16[128,2,128]{2,1,0:T(2,128)(2,1)S(1)}, u32[]{:S(2)}, u32[]{:S(2)}) async-start(bf16[128,2,128]{2,1,0:T(2,128)(2,1)} %mail.1), calls=%async_computation | async-start | bytes 131072 | tf_op jit(solution)/shard_map/all_to_all | solution.py:441
  95.7 15.7 %collective-permute-start.12 = (bf16[8,32,128]{2,1,0:T(8,128)(2,1)S(1)}, bf16[8,32,128]{2,1,0:T(8,128)(2,1)S(1)}, u32[]{:S(2)}, u32[]{:S(2)}) collective-permute-start(bf16[8,32,128]{2,1,0:T(8,128)(2,1)S(1)} %get-tuple-element.33), channel_id=1, source_target_pairs={{8,16},{24,32},{40,48},{56,64},{72,80},{88,96},{104,112},{120,128}... | collective-permute-start | bytes 196616 | tf_op jit(solution)/shard_map/ppermute | solution.py:410
  104.2 14.8 %collective-permute-start.13 = (bf16[8,32,128]{2,1,0:T(8,128)(2,1)S(1)}, bf16[8,32,128]{2,1,0:T(8,128)(2,1)S(1)}, u32[]{:S(2)}, u32[]{:S(2)}) collective-permute-start(bf16[8,32,128]{2,1,0:T(8,128)(2,1)S(1)} %get-tuple-element.34), channel_id=1, source_target_pairs={{0,8},{16,24},{32,40},{48,56},{64,72},{80,88},{96,104},{112,120},{... | collective-permute-start | bytes 196616 | tf_op jit(solution)/shard_map/ppermute | solution.py:410
  106.1 12.9 %collective-permute-start.14 = (bf16[4,32,128]{2,1,0:T(8,128)(2,1)S(1)}, bf16[4,32,128]{2,1,0:T(8,128)(2,1)S(1)}, u32[]{:S(2)}, u32[]{:S(2)}) collective-permute-start(bf16[4,32,128]{2,1,0:T(8,128)(2,1)S(1)} %get-tuple-element.35), channel_id=1, source_target_pairs={{0,1},{2,3},{4,5},{6,7},{1,0},{3,2},{5,4},{7,6},{8,9},{10,11},{12,... | collective-permute-start | bytes 98312 | tf_op jit(solution)/shard_map/ppermute | solution.py:410
  108.0 10.9 %collective-permute-start.15 = (bf16[4,32,128]{2,1,0:T(8,128)(2,1)S(1)}, bf16[4,32,128]{2,1,0:T(8,128)(2,1)S(1)}, u32[]{:S(2)}, u32[]{:S(2)}) collective-permute-start(bf16[4,32,128]{2,1,0:T(8,128)(2,1)S(1)} %get-tuple-element.36), channel_id=1, source_target_pairs={{1,2},{3,4},{5,6},{2,1},{4,3},{6,5},{9,10},{11,12},{13,14},{10,9},... | collective-permute-start | bytes 98312 | tf_op jit(solution)/shard_map/ppermute | solution.py:410
  112.9 12.0 %all-to-all-start.1 = ((f32[8,4,512]{2,1,0:T(4,128)}), f32[8,4,512]{2,1,0:T(4,128)S(1)}, u32[]{:S(2)}, u32[]{:S(2)}) async-start(f32[8,4,512]{2,1,0:T(4,128)} %expand.1), calls=%async_computation.1 | async-start | bytes 131072 | tf_op jit(solution)/shard_map/all_to_all | solution.py:445
